TPU v7x, 32 devices: a whole 2x2x4 slice. The times are simulated.
32 devices in a mesh: ctx: 8 (over z, y), fsdp: 4 (over x, core).
Axes of the slice: x: 2, y: 2, z: 4, core: 2. Of those that a mesh axis runs over, the one named last changes fastest.
Arguments:
- layer_input: bfloat16 [16, 8, 2, 32, 1536], P('fsdp', 'ctx'), may hold values from -6 to 6
- gain_attn: bfloat16 [1536], P('fsdp'), may hold values from 0.5 to 1.5
- w_query: bfloat16 [1536, 1536], P('fsdp'), may hold values from -0.15625 to 0.15625
- key_projection_weight: bfloat16 [1536, 512], P('fsdp'), may hold values from -0.15625 to 0.15625
- value_projection_weight: bfloat16 [1536, 512], P('fsdp'), may hold values from -0.15625 to 0.15625
- w_out: bfloat16 [1536, 1536], P('fsdp'), may hold values from -0.4375 to 0.4375
- gain_ffn: bfloat16 [1536], P('fsdp'), may hold values from 0.5 to 1.5
- w_router: bfloat16 [1536, 40], P('fsdp'), may hold values from -0.3125 to 0.3125
- w_gate: bfloat16 [40, 1536, 512], P(None, None, 'fsdp'), may hold values from -0.15625 to 0.15625
- w_up: bfloat16 [40, 1536, 512], P(None, None, 'fsdp'), may hold values from -0.15625 to 0.15625
- w_down: bfloat16 [40, 1536, 512], P(None, None, 'fsdp'), may hold values from -1 to 1
- routes: int32 [16, 8, 2, 32, 8], P(None, 'ctx'), may hold values from 0 to 39, all different within a row; in each aligned block of 64 rows (0 to 63, 64 to 127, ..., all dimensions but the last counted through in order) at most 17 rows name the same one
- lengths: int32 [16], replicated, may hold values from 128 to 512, as said below
- cotangent: bfloat16 [16, 8, 2, 32, 1536], P('fsdp', 'ctx'), may hold values from -6 to 6
Outputs:
- layer_output: bfloat16 [16, 8, 2, 32, 1536], P('fsdp', 'ctx')
- grad_input: float32 [16, 8, 2, 32, 1536], P('fsdp', 'ctx')
- grad_gain_attn: float32 [1536], P(('ctx', 'fsdp'))
- grad_w_query: float32 [1536, 1536], P(('ctx', 'fsdp'))
- grad_w_key: float32 [1536, 512], P(('ctx', 'fsdp'))
- grad_w_value: float32 [1536, 512], P(('ctx', 'fsdp'))
- grad_w_out: float32 [1536, 1536], P(('ctx', 'fsdp'))
- grad_gain_ffn: float32 [1536], P(('ctx', 'fsdp'))
- grad_w_router: float32 [1536, 40], P(('ctx', 'fsdp'))
- grad_w_gate: float32 [40, 1536, 512], P(None, 'ctx', 'fsdp')
- grad_w_up: float32 [40, 1536, 512], P(None, 'ctx', 'fsdp')
- grad_w_down: float32 [40, 1536, 512], P(None, 'ctx', 'fsdp')
- aux_loss: float32 [], replicated
Inputs may be any that keep to these rules, and one draw needn't show every extreme that they name: `routes`: each slot names 8 different experts. Within one aligned block of 64 rows (the slots of one sequence on one device), no expert is named by more than 17 rows, and in every draw some expert is named by exactly 17 rows of some block. `lengths`: some sequence uses all 512 slots in every draw.
All inputs are finite; a program needn't handle non-finite values.
Results may differ from a plain program's by a relative error of at most 0.02.
Values may be sent and summed in bfloat16 or wider, within the bound.
No kernel may reach another device: no remote copies, remote signals or barrier semaphores. Data moves between devices by JAX's collectives and lax.ppermute only.
A program may use at most 448 MiB of HBM per device.

v0:
```python
import jax
import jax.numpy as jnp
from jax import lax
from jax.sharding import PartitionSpec as P

QUERY_HEADS = 24
KEY_VALUE_HEADS = 8
HEAD_DIM = 64
MOST = 17


epsilon = 1e-05
rope_base = 10000.0
loss_weight = 0.01
mask_value = -1e30


def rms_scale(values):
    return lax.rsqrt(jnp.mean(values * values, -1, keepdims=True) + epsilon)


def rope_tables(token_positions):
    frequency = rope_base ** (-jnp.arange(HEAD_DIM // 2, dtype=jnp.float32) * 2.0 / HEAD_DIM)
    angles = token_positions.astype(jnp.float32)[..., None] * frequency
    return (jnp.cos(angles)[..., None, :], jnp.sin(angles)[..., None, :])


def apply_rotation(values, token_positions):
    cosine, sine_part = rope_tables(token_positions)
    first_half = values[..., : HEAD_DIM // 2]
    second = values[..., HEAD_DIM // 2 :]
    return jnp.concatenate(
        [first_half * cosine - second * sine_part, second * cosine + first_half * sine_part], -1
    )


def unrotate(gradient, token_positions):
    cosine, sine_part = rope_tables(token_positions)
    first_half = gradient[..., : HEAD_DIM // 2]
    second = gradient[..., HEAD_DIM // 2 :]
    return jnp.concatenate(
        [first_half * cosine + second * sine_part, second * cosine - first_half * sine_part], -1
    )


def inner_rows(left_side, right_side):
    return lax.dot_general(
        left_side, right_side, (((0,), (0,)), ((), ())), preferred_element_type=jnp.float32
    )


def back_rows(gradient, weight):
    return lax.dot_general(
        gradient, weight, (((1,), (1,)), ((), ())), preferred_element_type=jnp.float32
    )


def gathered_positions(key_index, sequence_rows, half_rows, n_ctx):
    device = key_index // sequence_rows
    within = key_index % sequence_rows
    block_id = jnp.where(within < half_rows, device, 2 * n_ctx - 1 - device)
    return block_id * half_rows + within % half_rows


def block_scores(query_rotated_rows, key_portion, query_pos, key_pos, key_live):
    raw_scores = jnp.einsum(
        "sqhgd,kshd->shgqk", query_rotated_rows, key_portion, preferred_element_type=jnp.float32
    ) * HEAD_DIM ** (-0.5)
    causal = key_pos[None, :] <= query_pos[:, None]
    visible = (causal[None] & key_live.T[:, None, :])[:, None, None]
    return (jnp.where(visible, raw_scores, mask_value), visible)


def local(
    layer_input,
    gain_attn,
    w_query,
    key_projection_weight,
    value_projection_weight,
    w_out,
    gain_ffn,
    w_router,
    w_gate,
    w_up,
    w_down,
    routes,
    lengths,
    cotangent,
):
    n_ctx = lax.axis_size("ctx")
    n_shard = lax.axis_size("fsdp")
    ctx_pos = lax.axis_index("ctx")
    shard_pos = lax.axis_index("fsdp")
    local_sequences = layer_input.shape[0]
    half_rows = layer_input.shape[3]
    model_width = layer_input.shape[4]
    sequence_rows = 2 * half_rows
    tokens = local_sequences * sequence_rows
    seq_len = n_ctx * sequence_rows
    experts = w_gate.shape[0]
    hidden_part = w_gate.shape[2]
    top_k = routes.shape[4]
    query_group_width = QUERY_HEADS // KEY_VALUE_HEADS
    key_value_width = KEY_VALUE_HEADS * HEAD_DIM
    key_tile_rows = min(512, seq_len)
    key_blocks = seq_len // key_tile_rows
    gathered_rows = n_shard * tokens
    route_blocks = gathered_rows // sequence_rows
    capacity = route_blocks * MOST
    expert_groups = experts // 8
    local_positions = gathered_positions(
        ctx_pos * sequence_rows + jnp.arange(sequence_rows, dtype=jnp.int32),
        sequence_rows,
        half_rows,
        n_ctx,
    )
    seq_lengths = lax.dynamic_slice_in_dim(lengths, shard_pos * local_sequences, local_sequences)
    live_rows = (
        (local_positions[None, :] < seq_lengths[:, None]).astype(jnp.float32).reshape(tokens)
    )
    gain_one, query_matrix, key_matrix, value_matrix, output_matrix, gain_two, router_matrix = (
        lax.all_gather(gain_attn, "fsdp", axis=0, tiled=True),
        lax.all_gather(w_query, "fsdp", axis=0, tiled=True),
        lax.all_gather(key_projection_weight, "fsdp", axis=0, tiled=True),
        lax.all_gather(value_projection_weight, "fsdp", axis=0, tiled=True),
        lax.all_gather(w_out, "fsdp", axis=0, tiled=True),
        lax.all_gather(gain_ffn, "fsdp", axis=0, tiled=True),
        lax.all_gather(w_router, "fsdp", axis=0, tiled=True),
    )
    input_rows = layer_input.reshape(tokens, model_width).astype(jnp.float32)
    scale_one = rms_scale(input_rows)
    unit_one = input_rows * scale_one
    first_normed = (unit_one * gain_one.astype(jnp.float32)).astype(jnp.bfloat16)
    normed_seq = first_normed.reshape(local_sequences, sequence_rows, model_width)
    query_unrotated = jnp.dot(first_normed, query_matrix, preferred_element_type=jnp.float32)
    key_unrotated = jnp.einsum(
        "std,df->tsf", normed_seq, key_matrix, preferred_element_type=jnp.float32
    )
    value_pre = jnp.einsum(
        "std,df->tsf", normed_seq, value_matrix, preferred_element_type=jnp.float32
    )
    query_rotated_rows = apply_rotation(
        query_unrotated.reshape(local_sequences, sequence_rows, QUERY_HEADS, HEAD_DIM),
        local_positions,
    ).astype(jnp.bfloat16)
    query_rotated_rows = query_rotated_rows.reshape(
        local_sequences, sequence_rows, KEY_VALUE_HEADS, query_group_width, HEAD_DIM
    )
    key_rotated_rows = apply_rotation(
        key_unrotated.reshape(sequence_rows, local_sequences, KEY_VALUE_HEADS, HEAD_DIM),
        local_positions[:, None],
    ).astype(jnp.bfloat16)
    key_rotated_rows = key_rotated_rows.reshape(sequence_rows, local_sequences, key_value_width)
    value_low = value_pre.astype(jnp.bfloat16)
    key_all, value_all = (
        lax.all_gather(key_rotated_rows, "ctx", axis=0, tiled=True),
        lax.all_gather(value_low, "ctx", axis=0, tiled=True),
    )

    def key_info(block_id):
        key_index = block_id * key_tile_rows + jnp.arange(key_tile_rows, dtype=jnp.int32)
        key_pos = gathered_positions(key_index, sequence_rows, half_rows, n_ctx)
        return (key_pos, key_pos[:, None] < seq_lengths[None, :])

    def key_slices(key_src, value_src, block_id):
        key_portion = lax.dynamic_slice_in_dim(key_src, block_id * key_tile_rows, key_tile_rows, 0)
        value_portion = lax.dynamic_slice_in_dim(
            value_src, block_id * key_tile_rows, key_tile_rows, 0
        )
        return (
            key_portion.reshape(key_tile_rows, local_sequences, KEY_VALUE_HEADS, HEAD_DIM),
            value_portion.reshape(key_tile_rows, local_sequences, KEY_VALUE_HEADS, HEAD_DIM),
        )

    def running_max(state_pair, block_id):
        top_score, row_total = state_pair
        key_pos, key_live = key_info(block_id)
        key_portion, value_portion = key_slices(key_all, value_all, block_id)
        scores, visible = block_scores(
            query_rotated_rows, key_portion, local_positions, key_pos, key_live
        )
        new_top = jnp.maximum(top_score, jnp.max(scores, -1))
        row_total = row_total * jnp.exp(top_score - new_top) + jnp.sum(
            jnp.where(visible, jnp.exp(scores - new_top[..., None]), 0.0), -1
        )
        return ((new_top, row_total), None)

    statistic_shape = (local_sequences, KEY_VALUE_HEADS, query_group_width, sequence_rows)
    lse_pair, unused = lax.scan(
        running_max,
        (
            jnp.full(statistic_shape, mask_value, jnp.float32),
            jnp.zeros(statistic_shape, jnp.float32),
        ),
        jnp.arange(key_blocks),
    )
    log_norm = lse_pair[0] + jnp.log(lse_pair[1])

    def weigh_values(acc_out, block_id):
        key_pos, key_live = key_info(block_id)
        key_portion, value_portion = key_slices(key_all, value_all, block_id)
        scores, visible = block_scores(
            query_rotated_rows, key_portion, local_positions, key_pos, key_live
        )
        prob_low = jnp.where(visible, jnp.exp(scores - log_norm[..., None]), 0.0).astype(
            jnp.bfloat16
        )
        return (
            acc_out
            + jnp.einsum(
                "shgqk,kshd->sqhgd", prob_low, value_portion, preferred_element_type=jnp.float32
            ),
            None,
        )

    attended, unused = lax.scan(
        weigh_values,
        jnp.zeros(
            (local_sequences, sequence_rows, KEY_VALUE_HEADS, query_group_width, HEAD_DIM),
            jnp.float32,
        ),
        jnp.arange(key_blocks),
    )
    attended_low = attended.astype(jnp.bfloat16).reshape(tokens, QUERY_HEADS * HEAD_DIM)
    branch_output = jnp.dot(attended_low, output_matrix, preferred_element_type=jnp.float32)
    residual = input_rows + branch_output
    scale_two = rms_scale(residual)
    unit_two = residual * scale_two
    second_normed = (unit_two * gain_two.astype(jnp.float32)).astype(jnp.bfloat16)
    normed_all = lax.all_gather(second_normed, "fsdp", axis=0, tiled=True)
    router_logits = jnp.dot(normed_all, router_matrix, preferred_element_type=jnp.float32)
    router_probs = jax.nn.softmax(router_logits, axis=-1)
    route_rows = routes.reshape(gathered_rows, top_k)
    route_hot = route_rows[..., None] == jnp.arange(experts, dtype=jnp.int32)
    route_gates = jnp.sum(jnp.where(route_hot, router_probs[:, None, :], 0.0), -1)
    pair_hot = route_hot.reshape(route_blocks, sequence_rows * top_k, experts).astype(jnp.int32)
    rank_pair = jnp.sum((jnp.cumsum(pair_hot, axis=1) - 1) * pair_hot, -1)
    slot_ids = (
        route_rows.reshape(route_blocks, sequence_rows * top_k) * capacity
        + jnp.arange(route_blocks, dtype=jnp.int32)[:, None] * MOST
        + rank_pair
    )
    slot_table = (
        jnp.full((experts * capacity,), -1, jnp.int32)
        .at[slot_ids.reshape(-1)]
        .set(jnp.arange(gathered_rows * top_k, dtype=jnp.int32))
    )
    slot_groups = slot_table.reshape(expert_groups, 8, capacity)
    gate_groups = w_gate.reshape(expert_groups, 8, model_width, hidden_part)
    up_groups = w_up.reshape(expert_groups, 8, model_width, hidden_part)
    down_groups = w_down.reshape(expert_groups, 8, model_width, hidden_part)
    flat_gates = route_gates.reshape(-1)

    def slot_inputs(slot_group):
        live_slot = slot_group >= 0
        pair_id = jnp.maximum(slot_group, 0)
        token_id = pair_id // top_k
        slot_gate = jnp.where(live_slot, flat_gates[pair_id], 0.0)
        return (live_slot, pair_id, token_id, slot_gate)

    def expert_forward(moe_part, group_in):
        slot_group, gate_w, up_w, down_w = group_in
        live_slot, pair_id, token_id, slot_gate = slot_inputs(slot_group)
        picked = normed_all[token_id]
        gate_pre = jnp.einsum("ecd,edh->ech", picked, gate_w, preferred_element_type=jnp.float32)
        up_pre = jnp.einsum("ecd,edh->ech", picked, up_w, preferred_element_type=jnp.float32)
        scaled = (slot_gate[..., None] * jax.nn.silu(gate_pre) * up_pre).astype(jnp.bfloat16)
        produced = jnp.einsum("ech,edh->ecd", scaled, down_w, preferred_element_type=jnp.float32)
        moe_part = moe_part.at[token_id.reshape(-1)].add(produced.reshape(-1, model_width))
        return (moe_part, (gate_pre, up_pre))

    moe_part, kept_acts = lax.scan(
        expert_forward,
        jnp.zeros((gathered_rows, model_width), jnp.float32),
        (slot_groups, gate_groups, up_groups, down_groups),
    )
    moe_own = lax.psum_scatter(
        moe_part.astype(jnp.bfloat16), "fsdp", scatter_dimension=0, tiled=True
    ).astype(jnp.float32)
    block_out = residual + moe_own
    layer_output = block_out.astype(jnp.bfloat16).reshape(layer_input.shape)
    own_probs = lax.dynamic_slice_in_dim(router_probs, shard_pos * tokens, tokens, 0)
    own_hot = lax.dynamic_slice_in_dim(route_hot, shard_pos * tokens, tokens, 0).astype(jnp.float32)
    counts = jnp.sum(jnp.sum(own_hot, 1) * live_rows[:, None], 0)
    prob_mass = jnp.sum(own_probs * live_rows[:, None], 0)
    count_all, mass_all = lax.psum((counts, prob_mass), ("ctx", "fsdp"))
    live_all = jnp.sum(lengths).astype(jnp.float32)
    route_share = count_all / (top_k * live_all)
    aux_loss = experts * jnp.sum(route_share * mass_all / live_all)
    d_final = cotangent.reshape(tokens, model_width).astype(jnp.float32) * live_rows[:, None]
    d_moe_all = lax.all_gather(d_final.astype(jnp.bfloat16), "fsdp", axis=0, tiled=True)

    def expert_backward(state_pair, group_in):
        d_rows, d_gates = state_pair
        slot_group, gate_w, up_w, down_w, gate_pre, up_pre = group_in
        live_slot, pair_id, token_id, slot_gate = slot_inputs(slot_group)
        picked = normed_all[token_id]
        d_out_slot = d_moe_all[token_id]
        silu_gate = jax.nn.silu(gate_pre)
        scaled = (slot_gate[..., None] * silu_gate * up_pre).astype(jnp.bfloat16)
        d_down = jnp.einsum("ech,ecd->edh", scaled, d_out_slot, preferred_element_type=jnp.float32)
        d_scaled = jnp.einsum(
            "ecd,edh->ech", d_out_slot, down_w, preferred_element_type=jnp.float32
        )
        d_slot_gate = jnp.sum(d_scaled * silu_gate * up_pre, -1)
        d_act = d_scaled * slot_gate[..., None]
        sigmoid_gate = jax.nn.sigmoid(gate_pre)
        d_gate_pre = (
            d_act * up_pre * (sigmoid_gate + gate_pre * sigmoid_gate * (1.0 - sigmoid_gate))
        ).astype(jnp.bfloat16)
        d_up_pre = (d_act * silu_gate).astype(jnp.bfloat16)
        d_gate_w = jnp.einsum(
            "ecd,ech->edh", picked, d_gate_pre, preferred_element_type=jnp.float32
        )
        d_up_w = jnp.einsum("ecd,ech->edh", picked, d_up_pre, preferred_element_type=jnp.float32)
        d_picked = jnp.einsum(
            "ech,edh->ecd", d_gate_pre, gate_w, preferred_element_type=jnp.float32
        ) + jnp.einsum("ech,edh->ecd", d_up_pre, up_w, preferred_element_type=jnp.float32)
        d_rows = d_rows.at[token_id.reshape(-1)].add(d_picked.reshape(-1, model_width))
        d_gates = d_gates.at[pair_id.reshape(-1)].add(
            jnp.where(live_slot, d_slot_gate, 0.0).reshape(-1)
        )
        group_terms = (d_gate_w, d_up_w, d_down)
        return ((d_rows, d_gates), group_terms)

    grad_pair, expert_terms = lax.scan(
        expert_backward,
        (
            jnp.zeros((gathered_rows, model_width), jnp.float32),
            jnp.zeros((gathered_rows * top_k,), jnp.float32),
        ),
        (slot_groups, gate_groups, up_groups, down_groups, kept_acts[0], kept_acts[1]),
    )
    grad_gate, grad_up, grad_down = (
        lax.psum_scatter(
            expert_terms[0].reshape(experts, model_width, hidden_part).astype(jnp.bfloat16),
            "ctx",
            scatter_dimension=1,
            tiled=True,
        ).astype(jnp.float32),
        lax.psum_scatter(
            expert_terms[1].reshape(experts, model_width, hidden_part).astype(jnp.bfloat16),
            "ctx",
            scatter_dimension=1,
            tiled=True,
        ).astype(jnp.float32),
        lax.psum_scatter(
            expert_terms[2].reshape(experts, model_width, hidden_part).astype(jnp.bfloat16),
            "ctx",
            scatter_dimension=1,
            tiled=True,
        ).astype(jnp.float32),
    )
    d_own, d_gate_own = (
        lax.psum_scatter(
            grad_pair[0].astype(jnp.bfloat16), "fsdp", scatter_dimension=0, tiled=True
        ).astype(jnp.float32),
        lax.psum_scatter(
            grad_pair[1].reshape(gathered_rows, top_k).astype(jnp.bfloat16),
            "fsdp",
            scatter_dimension=0,
            tiled=True,
        ).astype(jnp.float32),
    )
    d_probs = (
        jnp.sum(d_gate_own[..., None] * own_hot, 1)
        + loss_weight * experts * route_share[None, :] * live_rows[:, None] / live_all
    )
    d_logits = (own_probs * (d_probs - jnp.sum(own_probs * d_probs, -1, keepdims=True))).astype(
        jnp.bfloat16
    )
    grad_router = inner_rows(second_normed, d_logits)
    d_normed_two = d_own + back_rows(d_logits, router_matrix)
    d_unit_two = d_normed_two * gain_two.astype(jnp.float32)
    grad_gain_two = jnp.sum(d_normed_two * unit_two, 0)
    d_resid = d_final + scale_two * (
        d_unit_two - unit_two * jnp.mean(d_unit_two * unit_two, -1, keepdims=True)
    )
    d_branch = d_resid.astype(jnp.bfloat16)
    grad_out = inner_rows(attended_low, d_branch)
    d_attended = (
        back_rows(d_branch, output_matrix)
        .astype(jnp.bfloat16)
        .reshape(local_sequences, sequence_rows, KEY_VALUE_HEADS, query_group_width, HEAD_DIM)
    )
    row_delta = jnp.sum(d_attended.astype(jnp.float32) * attended, -1).transpose(0, 2, 3, 1)
    key_again, value_again = (
        lax.all_gather(key_rotated_rows, "ctx", axis=0, tiled=True),
        lax.all_gather(value_low, "ctx", axis=0, tiled=True),
    )

    def attend_back(d_query, block_id):
        key_pos, key_live = key_info(block_id)
        key_portion, value_portion = key_slices(key_again, value_again, block_id)
        scores, visible = block_scores(
            query_rotated_rows, key_portion, local_positions, key_pos, key_live
        )
        soft_prob = jnp.where(visible, jnp.exp(scores - log_norm[..., None]), 0.0)
        d_value = jnp.einsum(
            "shgqk,sqhgd->kshd",
            soft_prob.astype(jnp.bfloat16),
            d_attended,
            preferred_element_type=jnp.float32,
        )
        d_prob = jnp.einsum(
            "sqhgd,kshd->shgqk", d_attended, value_portion, preferred_element_type=jnp.float32
        )
        d_score = (soft_prob * (d_prob - row_delta[..., None]) * HEAD_DIM ** (-0.5)).astype(
            jnp.bfloat16
        )
        d_query = d_query + jnp.einsum(
            "shgqk,kshd->sqhgd", d_score, key_portion, preferred_element_type=jnp.float32
        )
        d_key = jnp.einsum(
            "shgqk,sqhgd->kshd", d_score, query_rotated_rows, preferred_element_type=jnp.float32
        )
        return (
            d_query,
            (
                d_key.reshape(key_tile_rows, local_sequences, key_value_width),
                d_value.reshape(key_tile_rows, local_sequences, key_value_width),
            ),
        )

    d_query, kv_terms = lax.scan(
        attend_back,
        jnp.zeros(
            (local_sequences, sequence_rows, KEY_VALUE_HEADS, query_group_width, HEAD_DIM),
            jnp.float32,
        ),
        jnp.arange(key_blocks),
    )
    local_key_gradient, d_value_own = (
        lax.psum_scatter(
            kv_terms[0].reshape(seq_len, local_sequences, key_value_width).astype(jnp.bfloat16),
            "ctx",
            scatter_dimension=0,
            tiled=True,
        ).astype(jnp.float32),
        lax.psum_scatter(
            kv_terms[1].reshape(seq_len, local_sequences, key_value_width).astype(jnp.bfloat16),
            "ctx",
            scatter_dimension=0,
            tiled=True,
        ).astype(jnp.float32),
    )
    d_query_low = (
        unrotate(
            d_query.reshape(local_sequences, sequence_rows, QUERY_HEADS, HEAD_DIM), local_positions
        )
        .astype(jnp.bfloat16)
        .reshape(tokens, QUERY_HEADS * HEAD_DIM)
    )
    d_key_low = unrotate(
        local_key_gradient.reshape(sequence_rows, local_sequences, KEY_VALUE_HEADS, HEAD_DIM),
        local_positions[:, None],
    ).astype(jnp.bfloat16)
    d_key_low = d_key_low.reshape(sequence_rows, local_sequences, key_value_width)
    d_value_low = d_value_own.astype(jnp.bfloat16)
    grad_query = inner_rows(first_normed, d_query_low)
    grad_key = jnp.einsum("std,tsf->df", normed_seq, d_key_low, preferred_element_type=jnp.float32)
    grad_value = jnp.einsum(
        "std,tsf->df", normed_seq, d_value_low, preferred_element_type=jnp.float32
    )
    d_normed_one = (
        back_rows(d_query_low, query_matrix)
        + jnp.einsum(
            "tsf,df->std", d_key_low, key_matrix, preferred_element_type=jnp.float32
        ).reshape(tokens, model_width)
        + jnp.einsum(
            "tsf,df->std", d_value_low, value_matrix, preferred_element_type=jnp.float32
        ).reshape(tokens, model_width)
    )
    d_unit_one = d_normed_one * gain_one.astype(jnp.float32)
    grad_gain_one = jnp.sum(d_normed_one * unit_one, 0)
    grad_input = d_resid + scale_one * (
        d_unit_one - unit_one * jnp.mean(d_unit_one * unit_one, -1, keepdims=True)
    )
    summed = (
        lax.psum_scatter(grad_gain_one, ("ctx", "fsdp"), scatter_dimension=0, tiled=True),
        lax.psum_scatter(grad_query, ("ctx", "fsdp"), scatter_dimension=0, tiled=True),
        lax.psum_scatter(grad_key, ("ctx", "fsdp"), scatter_dimension=0, tiled=True),
        lax.psum_scatter(grad_value, ("ctx", "fsdp"), scatter_dimension=0, tiled=True),
        lax.psum_scatter(grad_out, ("ctx", "fsdp"), scatter_dimension=0, tiled=True),
        lax.psum_scatter(grad_gain_two, ("ctx", "fsdp"), scatter_dimension=0, tiled=True),
        lax.psum_scatter(grad_router, ("ctx", "fsdp"), scatter_dimension=0, tiled=True),
    )
    return (
        layer_output,
        grad_input.reshape(layer_input.shape),
        summed[0],
        summed[1],
        summed[2],
        summed[3],
        summed[4],
        summed[5],
        summed[6],
        grad_gate,
        grad_up,
        grad_down,
        aux_loss,
    )


def solution(mesh):
    placed = (
        P("fsdp", "ctx", None, None, None),
        P("fsdp"),
        P("fsdp", None),
        P("fsdp", None),
        P("fsdp", None),
        P("fsdp", None),
        P("fsdp"),
        P("fsdp", None),
        P(None, None, "fsdp"),
        P(None, None, "fsdp"),
        P(None, None, "fsdp"),
        P(None, "ctx", None, None, None),
        P(),
        P("fsdp", "ctx", None, None, None),
    )
    return jax.shard_map(
        local,
        mesh=mesh,
        in_specs=placed,
        out_specs=(
            P("fsdp", "ctx", None, None, None),
            P("fsdp", "ctx", None, None, None),
            P(("ctx", "fsdp")),
            P(("ctx", "fsdp"), None),
            P(("ctx", "fsdp"), None),
            P(("ctx", "fsdp"), None),
            P(("ctx", "fsdp"), None),
            P(("ctx", "fsdp")),
            P(("ctx", "fsdp"), None),
            P(None, "ctx", "fsdp"),
            P(None, "ctx", "fsdp"),
            P(None, "ctx", "fsdp"),
            P(),
        ),
        check_vma=False,
    )
```

profile of v0, /device:TPU:0, one launch (start us, length us, event | category | flops | bytes accessed | tf_op | source)
XLA Modules:
  0.0 3025.0 jit_solution(11447055263391223788)
XLA Ops:
  65.6 39.5 %all-gather.13.cloned.1.call-done = bf16[512,4,512]{2,0,1:T(8,128)(2,1)} async-done(((bf16[64,4,512]{2,0,1:T(8,128)(2,1)}), bf16[512,4,512]{2,0,1:T(8,128)(2,1)}) %all-gather.13.cloned.1.call-update) | async-done | bytes 2097168 | tf_op jit(solution)/shard_map/all_gather | solution.py:157
  109.2 46.1 %all-gather.17.cloned.1.call-done = bf16[512,4,512]{2,1,0:T(4,128)(2,1)} async-done(((bf16[64,4,512]{2,1,0:T(4,128)(2,1)}), bf16[512,4,512]{2,1,0:T(4,128)(2,1)}) %all-gather.17.cloned.1.call-update) | async-done | bytes 2097168 | tf_op jit(solution)/shard_map/all_gather | solution.py:156
  158.2 34.4 %all-gather.19.cloned.1.call-done = bf16[1536,1536]{1,0:T(8,128)(2,1)} async-done(((bf16[384,1536]{1,0:T(8,128)(2,1)}), bf16[1536,1536]{1,0:T(8,128)(2,1)}) %all-gather.19.cloned.1.call-update) | async-done | bytes 4718608 | tf_op jit(solution)/shard_map/all_gather | solution.py:123
  305.0 364.7 %while.8 = (s32[]{:T(128)}, f32[1024,1536]{1,0:T(8,128)}, f32[5,8,272,128]{3,2,1,0:T(8,128)}, f32[5,8,272,128]{3,2,1,0:T(8,128)}, s32[5,8,272]{2,1,0:T(8,128)S(1...) while((s32[]{:T(128)}, f32[1024,1536]{1,0:T(8,128)}, ...), condition=%wide.region_13.14_spmd, body=%wide.region_11.13_spmd.sunk | while | flops 2572255744 | bytes 123338400 | solution.py:272
  346.5 31.7 %scatter_fusion = f32[1024,1536]{1,0:T(8,128)} fusion(f32[1024,1536]{1,0:T(8,128)} %get-tuple-element.783, s32[2176]{0:T(1024)S(1)} %fusion.180, f32[2176,1536]{1,0:T(8,128)} %bitcast.393), kind=kCustom, calls=%fused_computation.5.clone.1 | custom fusion | flops 3342336 | bytes 40116736 | tf_op jit(solution)/shard_map/while/body/eval_jaxpr/scatter-add | solution.py:269
  673.2 671.7 %while.9 = (s32[]{:T(128)}, f32[1024,1536]{1,0:T(8,128)}, f32[8192]{0:T(1024)S(1)}, bf16[5,8,1536,128]{3,2,1,0:T(8,128)(2,1)}, bf16[5,8,1536,128]{3,2,1,0:T(8,12...) while((s32[]{:T(128)}, f32[1024,1536]{1,0:T(8,128)}, ...), condition=%wide.region_19.20_spmd, body=%wide.region_15.19_spmd.sunk | while | flops 5146970624 | bytes 176854800 | solution.py:326
  772.4 31.8 %scatter_fusion.1 = f32[1024,1536]{1,0:T(8,128)} fusion(f32[1024,1536]{1,0:T(8,128)} %get-tuple-element.821, s32[2176]{0:T(1024)S(1)} %fusion.193, f32[2176,1536]{1,0:T(8,128)} %bitcast.394), kind=kCustom, calls=%fused_computation.6.clone.1 | custom fusion | flops 3342336 | bytes 40116736 | tf_op jit(solution)/shard_map/while/body/eval_jaxpr/scatter-add | solution.py:319
  901.7 31.8 %scatter_fusion.1 = f32[1024,1536]{1,0:T(8,128)} fusion(f32[1024,1536]{1,0:T(8,128)} %get-tuple-element.821, s32[2176]{0:T(1024)S(1)} %fusion.193, f32[2176,1536]{1,0:T(8,128)} %bitcast.394), kind=kCustom, calls=%fused_computation.6.clone.1 | custom fusion | flops 3342336 | bytes 40116736 | tf_op jit(solution)/shard_map/while/body/eval_jaxpr/scatter-add | solution.py:319
  1030.9 31.8 %scatter_fusion.1 = f32[1024,1536]{1,0:T(8,128)} fusion(f32[1024,1536]{1,0:T(8,128)} %get-tuple-element.821, s32[2176]{0:T(1024)S(1)} %fusion.193, f32[2176,1536]{1,0:T(8,128)} %bitcast.394), kind=kCustom, calls=%fused_computation.6.clone.1 | custom fusion | flops 3342336 | bytes 40116736 | tf_op jit(solution)/shard_map/while/body/eval_jaxpr/scatter-add | solution.py:319
  1160.2 31.8 %scatter_fusion.1 = f32[1024,1536]{1,0:T(8,128)} fusion(f32[1024,1536]{1,0:T(8,128)} %get-tuple-element.821, s32[2176]{0:T(1024)S(1)} %fusion.193, f32[2176,1536]{1,0:T(8,128)} %bitcast.394), kind=kCustom, calls=%fused_computation.6.clone.1 | custom fusion | flops 3342336 | bytes 40116736 | tf_op jit(solution)/shard_map/while/body/eval_jaxpr/scatter-add | solution.py:319
  1289.6 31.8 %scatter_fusion.1 = f32[1024,1536]{1,0:T(8,128)} fusion(f32[1024,1536]{1,0:T(8,128)} %get-tuple-element.821, s32[2176]{0:T(1024)S(1)} %fusion.193, f32[2176,1536]{1,0:T(8,128)} %bitcast.394), kind=kCustom, calls=%fused_computation.6.clone.1 | custom fusion | flops 3342336 | bytes 40116736 | tf_op jit(solution)/shard_map/while/body/eval_jaxpr/scatter-add | solution.py:319
  1366.6 39.9 %psum.14 = f32[40]{0:T(128)S(1)} all-reduce(f32[40]{0:T(128)S(1)} %multiply_reduce_fusion.5), channel_id=1, replica_groups=mesh['ctx'=8,'fsdp'=4] {'ctx','fsdp'}, use_global_device_ids=true, to_apply=%region_25.26 | all-reduce | flops 40 | bytes 320 | tf_op jit(solution)/shard_map/psum | solution.py:286
  1411.2 37.1 %reduce-scatter.15.cloned.1.call-done = bf16[256,1536]{1,0:T(8,128)(2,1)} async-done(((bf16[1024,1536]{1,0:T(8,128)(2,1)}), bf16[256,1536]{1,0:T(8,128)(2,1)}) %reduce-scatter.15.cloned.1.call-update) | async-done | bytes 786448 | tf_op jit(solution)/shard_map/reduce_scatter | solution.py:277
  1497.4 86.1 %all-reduce.6.cloned.1.call-done = bf16[512,4,512]{2,1,0:T(4,128)(2,1)} async-done(((bf16[512,4,512]{2,1,0:T(4,128)(2,1)}), bf16[512,4,512]{2,1,0:T(4,128)(2,1)}) %all-reduce.6.cloned.1.call-update) | async-done | bytes 2097168
  1588.8 67.1 %reduce-scatter.21.cloned.1.call-done = bf16[64,4,512]{2,0,1:T(8,128)(2,1)} async-done(((bf16[512,4,512]{2,0,1:T(8,128)(2,1)}), bf16[64,4,512]{2,0,1:T(8,128)(2,1)}) %reduce-scatter.21.cloned.1.call-update) | async-done | bytes 262160 | tf_op jit(solution)/shard_map/reduce_scatter | solution.py:440
  1682.1 74.4 %reduce-scatter.37.cloned.1.call-done = f32[48,40]{1,0:T(8,128)} async-done(((f32[1536,40]{1,0:T(8,128)}), f32[48,40]{1,0:T(8,128)}) %reduce-scatter.37.cloned.1.call-update) | async-done | bytes 7696
  1766.3 45.7 %all-reduce.3 = (f32[1536]{0:T(1024)S(1)}, f32[1536]{0:T(1024)S(1)}, f32[40]{0:T(128)S(1)}) all-reduce(f32[1536]{0:T(1024)S(1)} %get-tuple-element.487, f32[1536]{0:T(1024)S(1)} %copy-done.55, f32[40]{0:T(128)S(1)} %copy-done.61), channel_id=7, replica_groups=mesh['ctx'=8,'fsdp'=4] {'ctx','fsdp'}, use_global_device_ids=true, to_apply=%region_34.35.clone | all-reduce | flops 3112 | bytes 24896
  1817.4 193.9 %reduce-scatter.33.cloned.1.call-done = bf16[40,192,128]{2,1,0:T(8,128)(2,1)} async-done(((bf16[40,1536,128]{2,1,0:T(8,128)(2,1)}), bf16[40,192,128]{2,1,0:T(8,128)(2,1)}) %reduce-scatter.33.cloned.1.call-update) | async-done | bytes 1966096 | tf_op jit(solution)/shard_map/reduce_scatter | solution.py:341
  2015.3 249.9 %reduce-scatter.31.cloned.1.call-done = bf16[40,192,128]{2,1,0:T(8,128)(2,1)} async-done(((bf16[40,1536,128]{2,1,0:T(8,128)(2,1)}), bf16[40,192,128]{2,1,0:T(8,128)(2,1)}) %reduce-scatter.31.cloned.1.call-update) | async-done | bytes 1966096 | tf_op jit(solution)/shard_map/reduce_scatter | solution.py:335
  2269.1 250.0 %reduce-scatter.35.cloned.1.call-done = bf16[40,192,128]{2,1,0:T(8,128)(2,1)} async-done(((bf16[40,1536,128]{2,1,0:T(8,128)(2,1)}), bf16[40,192,128]{2,1,0:T(8,128)(2,1)}) %reduce-scatter.35.cloned.1.call-update) | async-done | bytes 1966096 | tf_op jit(solution)/shard_map/reduce_scatter | solution.py:347
  2523.0 103.3 %reduce-scatter.25.cloned.1.call-done = f32[48,512]{1,0:T(8,128)} async-done(((f32[1536,512]{1,0:T(8,128)}), f32[48,512]{1,0:T(8,128)}) %reduce-scatter.25.cloned.1.call-update) | async-done | bytes 98320 | tf_op jit(solution)/shard_map/reduce_scatter | solution.py:482
  2626.3 107.2 %reduce-scatter.27.cloned.1.call-done = f32[48,512]{1,0:T(8,128)} async-done(((f32[1536,512]{1,0:T(8,128)}), f32[48,512]{1,0:T(8,128)}) %reduce-scatter.27.cloned.1.call-update) | async-done | bytes 98320 | tf_op jit(solution)/shard_map/reduce_scatter | solution.py:483
  2733.5 141.6 %reduce-scatter.29.cloned.1.call-done = f32[48,1536]{1,0:T(8,128)} async-done(((f32[1536,1536]{1,0:T(8,128)}), f32[48,1536]{1,0:T(8,128)}) %reduce-scatter.29.cloned.1.call-update) | async-done | bytes 294928 | tf_op jit(solution)/shard_map/reduce_scatter | solution.py:484
  2875.1 141.7 %reduce-scatter.23.cloned.1.call-done = f32[48,1536]{1,0:T(8,128)} async-done(((f32[1536,1536]{1,0:T(8,128)}), f32[48,1536]{1,0:T(8,128)}) %reduce-scatter.23.cloned.1.call-update) | async-done | bytes 294928 | tf_op jit(solution)/shard_map/reduce_scatter | solution.py:481
  (562 shorter events, 1130.9 us)
Async XLA Ops:
  7.2 24.8 all-gather.11.cloned.1.call-start
  7.9 45.2 %all-gather.15.cloned.1.call-start = ((), (), s32[]{:S(2)}) async-start(), calls=%async_computation.14 | async-start | bytes 1966080 | tf_op jit(solution)/shard_map/all_gather | solution.py:124
  8.7 96.4 %all-gather.13.cloned.1.call-start = ((), (), s32[]{:S(2)}) async-start(), calls=%async_computation.13 | async-start | bytes 2359296 | tf_op jit(solution)/shard_map/all_gather | solution.py:157
  34.6 120.6 %all-gather.17.cloned.1.call-start = ((), (), s32[]{:S(2)}) async-start(), calls=%async_computation.15 | async-start | bytes 2359296 | tf_op jit(solution)/shard_map/all_gather | solution.py:156
  34.9 169.4 %copy-start.43 = (f32[64,32]{0,1:T(8,128)}, f32[64,32]{0,1:T(8,128)S(1)}, u32[]{:S(2)}) copy-start(f32[64,32]{0,1:T(8,128)S(1)} %get-tuple-element.575) | copy-start | bytes 24580
  57.4 135.2 %all-gather.19.cloned.1.call-start = ((), (), s32[]{:S(2)}) async-start(), calls=%async_computation.16 | async-start | bytes 5898240 | tf_op jit(solution)/shard_map/all_gather | solution.py:123
  58.0 173.5 %all-gather.21.cloned.1.call-start = ((), (), s32[]{:S(2)}) async-start(), calls=%async_computation.17 | async-start | bytes 5898240 | tf_op jit(solution)/shard_map/all_gather | solution.py:126
  58.6 238.6 %all-gather.23.cloned.1.call-start = ((), (), s32[]{:S(2)}) async-start(), calls=%async_computation.18 | async-start | bytes 3932160 | tf_op jit(solution)/shard_map/all_gather | solution.py:230
  64.0 171.4 %copy-start.47 = (f32[1536]{0:T(1024)}, f32[1536]{0:T(1024)S(1)}, u32[]{:S(2)}) copy-start(f32[1536]{0:T(1024)S(1)} %reshape.1130) | copy-start | bytes 18436
  237.7 432.0 %all-gather.25.cloned.1.call-start = ((), (), s32[]{:S(2)}) async-start(), calls=%async_computation.20 | async-start | bytes 3932160 | tf_op jit(solution)/shard_map/all_gather | solution.py:291
  239.0 1126.8 %reduce-scatter.19.cloned.1.call-start = ((), (), s32[]{:S(2)}) async-start(), calls=%async_computation.22 | async-start | bytes 20480 | tf_op jit(solution)/shard_map/reduce_scatter | solution.py:358
  1346.0 61.6 %reduce-scatter.17.cloned.1.call-start = ((), (), s32[]{:S(2)}) async-start(), calls=%async_computation.21 | async-start | bytes 3932160 | tf_op jit(solution)/shard_map/reduce_scatter | solution.py:355
  1350.9 97.4 %reduce-scatter.15.cloned.1.call-start = ((), (), s32[]{:S(2)}) async-start(), calls=%async_computation.19 | async-start | bytes 3932160 | tf_op jit(solution)/shard_map/reduce_scatter | solution.py:277
  1355.9 227.6 %all-reduce.6.cloned.1.call-start = ((), (), s32[]{:S(2)}) async-start(), calls=%async_computation.32 | async-start | bytes 4194304
  1451.5 207.6 %copy-start.13 = (f32[256,1536]{1,0:T(8,128)}, f32[256,1536]{1,0:T(8,128)S(1)}, u32[]{:S(2)}) copy-start(f32[256,1536]{1,0:T(8,128)S(1)} %get-tuple-element.569) | copy-start | bytes 4718596
  1481.1 174.8 %reduce-scatter.21.cloned.1.call-start = ((), (), s32[]{:S(2)}) async-start(), calls=%async_computation.23 | async-start | bytes 2359296 | tf_op jit(solution)/shard_map/reduce_scatter | solution.py:440
  1492.7 263.9 %reduce-scatter.37.cloned.1.call-start = ((), (), s32[]{:S(2)}) async-start(), calls=%async_computation.31 | async-start | bytes 811008
  1494.3 517.0 %reduce-scatter.33.cloned.1.call-start = ((), (), s32[]{:S(2)}) async-start(), calls=%async_computation.29 | async-start | bytes 17694720 | tf_op jit(solution)/shard_map/reduce_scatter | solution.py:341
  1494.9 770.3 %reduce-scatter.31.cloned.1.call-start = ((), (), s32[]{:S(2)}) async-start(), calls=%async_computation.28 | async-start | bytes 17694720 | tf_op jit(solution)/shard_map/reduce_scatter | solution.py:335
  1495.5 1023.6 %reduce-scatter.35.cloned.1.call-start = ((), (), s32[]{:S(2)}) async-start(), calls=%async_computation.30 | async-start | bytes 17694720 | tf_op jit(solution)/shard_map/reduce_scatter | solution.py:347
  1496.1 1130.2 %reduce-scatter.25.cloned.1.call-start = ((), (), s32[]{:S(2)}) async-start(), calls=%async_computation.25 | async-start | bytes 3244032 | tf_op jit(solution)/shard_map/reduce_scatter | solution.py:482
  1588.7 1144.8 %reduce-scatter.27.cloned.1.call-start = ((), (), s32[]{:S(2)}) async-start(), calls=%async_computation.26 | async-start | bytes 3244032 | tf_op jit(solution)/shard_map/reduce_scatter | solution.py:483
  1659.1 1216.0 %reduce-scatter.29.cloned.1.call-start = ((), (), s32[]{:S(2)}) async-start(), calls=%async_computation.27 | async-start | bytes 9732096 | tf_op jit(solution)/shard_map/reduce_scatter | solution.py:484
  1664.2 1352.6 %reduce-scatter.23.cloned.1.call-start = ((), (), s32[]{:S(2)}) async-start(), calls=%async_computation.24 | async-start | bytes 9732096 | tf_op jit(solution)/shard_map/reduce_scatter | solution.py:481
  (80 other events, 1676.4 us)
Sparse Core Ops, SparseCore 0:
  9.5 22.3 all-gather.10
  33.5 19.6 all-gather.14
  55.9 49.0 all-gather.12
  107.6 47.6 all-gather.16
  156.6 35.9 all-gather.18
  194.1 37.4 all-gather.20
  237.8 28.4 all-gather.22
  268.4 28.4 all-gather.24
  1346.1 19.5 reduce-scatter.18
  1368.7 38.4 reduce-scatter.16
  1410.3 38.0 reduce-scatter.14
  1481.2 102.2 all-reduce.5
  1587.6 68.1 reduce-scatter.20
  1661.4 95.1 reduce-scatter.36
  1760.0 251.3 reduce-scatter.32
  2014.8 250.3 reduce-scatter.30
  2268.6 250.4 reduce-scatter.34
  2525.0 101.2 reduce-scatter.24
  2632.3 101.1 reduce-scatter.26
  2739.8 135.2 reduce-scatter.28
  2881.6 135.1 reduce-scatter.22
where the time goes:
time: 3030 us
  waiting for transfers between devices  1620 us (53%)
  other arithmetic  466 us (15%)
  matrix products  401 us (13%)
  local copies, waits for them, and re-layouts  392 us (13%)
  blocking collectives  103 us (3%)
    reduce_scatter x1, waiting for transfers between devices, local(): lax.psum_scatter(expert_terms[2].reshape(experts, model_width, hidden_par...  250 us
    reduce_scatter x1, waiting for transfers between devices, local(): lax.psum_scatter(expert_terms[0].reshape(experts, model_width, hidden_par...  250 us
    reduce_scatter x1, waiting for transfers between devices, local(): lax.psum_scatter(expert_terms[1].reshape(experts, model_width, hidden_par...  194 us
    unnamed x23, waiting for transfers between devices  165 us
    scatter-add x5, other arithmetic, expert_backward(): d_rows.at[token_id.reshape(-1)].add(d_picked.reshape(-1, model_width))  159 us
    scatter-add x5, other arithmetic, expert_forward(): moe_part.at[token_id.reshape(-1)].add(produced.reshape(-1, model_width))  158 us
    reduce_scatter x1, waiting for transfers between devices, local(): lax.psum_scatter(grad_query, ('ctx', 'fsdp'), scatter_dimension=0, tiled=...  142 us
    reduce_scatter x1, waiting for transfers between devices, local(): lax.psum_scatter(grad_out, ('ctx', 'fsdp'), scatter_dimension=0, tiled=True)  142 us
  transfers between devices with their start and end apart: 21, of which 18 were waited for; matrix products, arithmetic and copies ran while one was open for 19% of the time, Pallas kernels for 0%

commit v1 on v0

--- a/solution.py
+++ b/solution.py
@@ -1,12 +1,16 @@
 import jax
 import jax.numpy as jnp
 from jax import lax
+from jax.experimental import pallas as pl
+from jax.experimental.pallas import tpu as pltpu
 from jax.sharding import PartitionSpec as P
 
 QUERY_HEADS = 24
 KEY_VALUE_HEADS = 8
 HEAD_DIM = 64
-MOST = 17
+LANES = 128
+EXPERT_CALLS = 4
+ROW_BLOCK = 256
 
 
 epsilon = 1e-05
@@ -69,6 +73,168 @@
     causal = key_pos[None, :] <= query_pos[:, None]
     visible = (causal[None] & key_live.T[:, None, :])[:, None, None]
     return (jnp.where(visible, raw_scores, mask_value), visible)
+
+
+def expert_call(
+    first_expert,
+    expert_total,
+    normed_rows,
+    normed_turned,
+    cotangent_rows,
+    cotangent_turned,
+    gate_table,
+    w_gate,
+    w_up,
+    w_down,
+):
+    rows, width = normed_rows.shape
+    hidden = w_gate.shape[2]
+    pair_width = 2 * hidden
+    width_block = width // 3
+
+    def kernel(
+        normed,
+        normed_t,
+        cotan,
+        cotan_t,
+        gates,
+        gate_w,
+        up_w,
+        down_w,
+        gate_grad,
+        up_grad,
+        down_grad,
+        moe,
+        d_rows,
+        d_gates,
+        scaled_keep,
+        d_gate_keep,
+        d_up_keep,
+    ):
+        pair = pl.program_id(0)
+        first = first_expert + 2 * pair
+
+        @pl.when(pair == 0)
+        def _():
+            moe[...] = jnp.zeros_like(moe)
+            d_rows[...] = jnp.zeros_like(d_rows)
+            d_gates[...] = jnp.zeros_like(d_gates)
+
+        def joined(pair_ref):
+            return jnp.concatenate([pair_ref[0], pair_ref[1]], axis=1)
+
+        def plain(left_side, right_side):
+            return jnp.dot(left_side, right_side, preferred_element_type=jnp.float32)
+
+        def turned(left_side, right_side):
+            return lax.dot_general(
+                left_side, right_side, (((1,), (1,)), ((), ())), preferred_element_type=jnp.float32
+            )
+
+        gate_pair, up_pair, down_pair = joined(gate_w), joined(up_w), joined(down_w)
+        lane = lax.broadcasted_iota(jnp.int32, (ROW_BLOCK, LANES), 1)
+
+        def row_step(block, carry):
+            span = pl.ds(pl.multiple_of(block * ROW_BLOCK, ROW_BLOCK), ROW_BLOCK)
+            normed_part, cotan_part = normed[span, :], cotan[span, :]
+            gate_part = gates[span, :]
+            slot_gate = jnp.concatenate(
+                [
+                    jnp.broadcast_to(
+                        jnp.sum(
+                            jnp.where(lane == first + j, gate_part, 0.0), axis=1, keepdims=True
+                        ),
+                        (ROW_BLOCK, hidden),
+                    )
+                    for j in range(2)
+                ],
+                axis=1,
+            )
+            gate_pre = plain(normed_part, gate_pair)
+            up_pre = plain(normed_part, up_pair)
+            d_scaled = plain(cotan_part, down_pair)
+            sigmoid_gate = jax.nn.sigmoid(gate_pre)
+            silu_gate = gate_pre * sigmoid_gate
+            scaled = (slot_gate * silu_gate * up_pre).astype(jnp.bfloat16)
+            gate_term = d_scaled * silu_gate * up_pre
+            d_gate_part = d_gates[span, :]
+            for j in range(2):
+                d_gate_part = d_gate_part + jnp.where(
+                    lane == first + j,
+                    jnp.sum(gate_term[:, j * hidden : (j + 1) * hidden], axis=1, keepdims=True),
+                    0.0,
+                )
+            d_gates[span, :] = d_gate_part
+            d_act = d_scaled * slot_gate
+            d_gate_pre = (
+                d_act * up_pre * (sigmoid_gate + silu_gate * (1.0 - sigmoid_gate))
+            ).astype(jnp.bfloat16)
+            d_up_pre = (d_act * silu_gate).astype(jnp.bfloat16)
+            scaled_keep[span, :] = scaled
+            d_gate_keep[span, :] = d_gate_pre
+            d_up_keep[span, :] = d_up_pre
+            moe[span, :] += turned(scaled, down_pair)
+            d_rows[span, :] += turned(d_gate_pre, gate_pair) + turned(d_up_pre, up_pair)
+            return carry
+
+        lax.fori_loop(0, rows // ROW_BLOCK, row_step, 0)
+
+        def width_step(block, carry):
+            span = pl.ds(pl.multiple_of(block * width_block, width_block), width_block)
+            for source, kept, grad in (
+                (normed_t, d_gate_keep, gate_grad),
+                (normed_t, d_up_keep, up_grad),
+                (cotan_t, scaled_keep, down_grad),
+            ):
+                term = plain(source[span, :], kept[...]).astype(jnp.bfloat16)
+                for j in range(2):
+                    grad[j, span, :] = term[:, j * hidden : (j + 1) * hidden]
+            return carry
+
+        lax.fori_loop(0, 3, width_step, 0)
+
+    def whole(shape):
+        return pl.BlockSpec(shape, lambda pair: (0, 0), pipeline_mode=pl.Buffered(1))
+
+    def pair_block(offset):
+        return pl.BlockSpec((2, width, hidden), lambda pair: (pair + offset, 0, 0))
+
+    start = first_expert // 2
+    grad_shape = jax.ShapeDtypeStruct((expert_total, width, hidden), jnp.bfloat16)
+    row_shape = jax.ShapeDtypeStruct((rows, width), jnp.float32)
+    outs = pl.pallas_call(
+        kernel,
+        grid=(expert_total // 2,),
+        in_specs=[
+            whole((rows, width)),
+            whole((width, rows)),
+            whole((rows, width)),
+            whole((width, rows)),
+            whole((rows, LANES)),
+            pair_block(start),
+            pair_block(start),
+            pair_block(start),
+        ],
+        out_specs=[pair_block(0)] * 3
+        + [whole((rows, width)), whole((rows, width)), whole((rows, LANES))],
+        out_shape=[grad_shape] * 3
+        + [row_shape, row_shape, jax.ShapeDtypeStruct((rows, LANES), jnp.float32)],
+        scratch_shapes=[pltpu.VMEM((rows, pair_width), jnp.bfloat16)] * 3,
+        name="expert_step",
+        compiler_params=pltpu.CompilerParams(
+            dimension_semantics=("arbitrary",), vmem_limit_bytes=60 * 1024 * 1024
+        ),
+    )(
+        normed_rows,
+        normed_turned,
+        cotangent_rows,
+        cotangent_turned,
+        gate_table,
+        w_gate,
+        w_up,
+        w_down,
+    )
+    return outs[:3], outs[3], outs[4], outs[5]
 
 
 def local(
@@ -98,16 +264,12 @@
     tokens = local_sequences * sequence_rows
     seq_len = n_ctx * sequence_rows
     experts = w_gate.shape[0]
-    hidden_part = w_gate.shape[2]
     top_k = routes.shape[4]
     query_group_width = QUERY_HEADS // KEY_VALUE_HEADS
     key_value_width = KEY_VALUE_HEADS * HEAD_DIM
     key_tile_rows = min(512, seq_len)
     key_blocks = seq_len // key_tile_rows
     gathered_rows = n_shard * tokens
-    route_blocks = gathered_rows // sequence_rows
-    capacity = route_blocks * MOST
-    expert_groups = experts // 8
     local_positions = gathered_positions(
         ctx_pos * sequence_rows + jnp.arange(sequence_rows, dtype=jnp.int32),
         sequence_rows,
@@ -127,6 +289,8 @@
         lax.all_gather(gain_ffn, "fsdp", axis=0, tiled=True),
         lax.all_gather(w_router, "fsdp", axis=0, tiled=True),
     )
+    d_final = cotangent.reshape(tokens, model_width).astype(jnp.float32) * live_rows[:, None]
+    d_moe_all = lax.all_gather(d_final.astype(jnp.bfloat16), "fsdp", axis=0, tiled=True)
     input_rows = layer_input.reshape(tokens, model_width).astype(jnp.float32)
     scale_one = rms_scale(input_rows)
     unit_one = input_rows * scale_one
@@ -231,139 +395,74 @@
     router_logits = jnp.dot(normed_all, router_matrix, preferred_element_type=jnp.float32)
     router_probs = jax.nn.softmax(router_logits, axis=-1)
     route_rows = routes.reshape(gathered_rows, top_k)
-    route_hot = route_rows[..., None] == jnp.arange(experts, dtype=jnp.int32)
-    route_gates = jnp.sum(jnp.where(route_hot, router_probs[:, None, :], 0.0), -1)
-    pair_hot = route_hot.reshape(route_blocks, sequence_rows * top_k, experts).astype(jnp.int32)
-    rank_pair = jnp.sum((jnp.cumsum(pair_hot, axis=1) - 1) * pair_hot, -1)
-    slot_ids = (
-        route_rows.reshape(route_blocks, sequence_rows * top_k) * capacity
-        + jnp.arange(route_blocks, dtype=jnp.int32)[:, None] * MOST
-        + rank_pair
-    )
-    slot_table = (
-        jnp.full((experts * capacity,), -1, jnp.int32)
-        .at[slot_ids.reshape(-1)]
-        .set(jnp.arange(gathered_rows * top_k, dtype=jnp.int32))
-    )
-    slot_groups = slot_table.reshape(expert_groups, 8, capacity)
-    gate_groups = w_gate.reshape(expert_groups, 8, model_width, hidden_part)
-    up_groups = w_up.reshape(expert_groups, 8, model_width, hidden_part)
-    down_groups = w_down.reshape(expert_groups, 8, model_width, hidden_part)
-    flat_gates = route_gates.reshape(-1)
-
-    def slot_inputs(slot_group):
-        live_slot = slot_group >= 0
-        pair_id = jnp.maximum(slot_group, 0)
-        token_id = pair_id // top_k
-        slot_gate = jnp.where(live_slot, flat_gates[pair_id], 0.0)
-        return (live_slot, pair_id, token_id, slot_gate)
-
-    def expert_forward(moe_part, group_in):
-        slot_group, gate_w, up_w, down_w = group_in
-        live_slot, pair_id, token_id, slot_gate = slot_inputs(slot_group)
-        picked = normed_all[token_id]
-        gate_pre = jnp.einsum("ecd,edh->ech", picked, gate_w, preferred_element_type=jnp.float32)
-        up_pre = jnp.einsum("ecd,edh->ech", picked, up_w, preferred_element_type=jnp.float32)
-        scaled = (slot_gate[..., None] * jax.nn.silu(gate_pre) * up_pre).astype(jnp.bfloat16)
-        produced = jnp.einsum("ech,edh->ecd", scaled, down_w, preferred_element_type=jnp.float32)
-        moe_part = moe_part.at[token_id.reshape(-1)].add(produced.reshape(-1, model_width))
-        return (moe_part, (gate_pre, up_pre))
-
-    moe_part, kept_acts = lax.scan(
-        expert_forward,
-        jnp.zeros((gathered_rows, model_width), jnp.float32),
-        (slot_groups, gate_groups, up_groups, down_groups),
-    )
+    route_hot = jnp.any(
+        route_rows[..., None] == jnp.arange(experts, dtype=jnp.int32), axis=1
+    ).astype(jnp.float32)
+    live_everywhere = (
+        (local_positions[None, :] < lengths[:, None]).astype(jnp.float32).reshape(gathered_rows)
+    )
+    expert_gates = router_probs * route_hot
+    gate_table = jnp.pad(expert_gates, ((0, 0), (0, LANES - experts)))
+    pieces = EXPERT_CALLS
+    per_call = experts // pieces
+    grad_pieces, moe_pieces, row_pieces, gate_pieces = [], [], [], []
+    normed_turned = normed_all.T
+    d_moe_turned = d_moe_all.T
+    for piece in range(pieces):
+        piece_grads, moe_piece, row_piece, gate_piece = expert_call(
+            piece * per_call,
+            per_call,
+            normed_all,
+            normed_turned,
+            d_moe_all,
+            d_moe_turned,
+            gate_table,
+            w_gate,
+            w_up,
+            w_down,
+        )
+        grad_pieces.append(
+            [
+                lax.psum_scatter(piece_grad, "ctx", scatter_dimension=1, tiled=True).astype(
+                    jnp.float32
+                )
+                for piece_grad in piece_grads
+            ]
+        )
+        moe_pieces.append(moe_piece)
+        row_pieces.append(row_piece)
+        gate_pieces.append(gate_piece)
+    grad_gate, grad_up, grad_down = (
+        jnp.concatenate([grads[kind] for grads in grad_pieces], 0) for kind in range(3)
+    )
+    d_own = lax.psum_scatter(
+        sum(row_pieces).astype(jnp.bfloat16), "fsdp", scatter_dimension=0, tiled=True
+    ).astype(jnp.float32)
+    d_gate_own = lax.psum_scatter(
+        (sum(gate_pieces)[:, :experts] * route_hot).astype(jnp.bfloat16),
+        "fsdp",
+        scatter_dimension=0,
+        tiled=True,
+    ).astype(jnp.float32)
     moe_own = lax.psum_scatter(
-        moe_part.astype(jnp.bfloat16), "fsdp", scatter_dimension=0, tiled=True
+        sum(moe_pieces).astype(jnp.bfloat16), "fsdp", scatter_dimension=0, tiled=True
     ).astype(jnp.float32)
     block_out = residual + moe_own
     layer_output = block_out.astype(jnp.bfloat16).reshape(layer_input.shape)
     own_probs = lax.dynamic_slice_in_dim(router_probs, shard_pos * tokens, tokens, 0)
-    own_hot = lax.dynamic_slice_in_dim(route_hot, shard_pos * tokens, tokens, 0).astype(jnp.float32)
-    counts = jnp.sum(jnp.sum(own_hot, 1) * live_rows[:, None], 0)
-    prob_mass = jnp.sum(own_probs * live_rows[:, None], 0)
-    count_all, mass_all = lax.psum((counts, prob_mass), ("ctx", "fsdp"))
+    group_sums = jnp.concatenate(
+        [
+            jnp.sum(route_hot * live_everywhere[:, None], 0),
+            jnp.sum(router_probs * live_everywhere[:, None], 0),
+        ]
+    )
+    all_sums = jnp.sum(lax.all_gather(group_sums, "ctx", axis=0, tiled=False), 0)
+    count_all, mass_all = all_sums[:experts], all_sums[experts:]
     live_all = jnp.sum(lengths).astype(jnp.float32)
     route_share = count_all / (top_k * live_all)
     aux_loss = experts * jnp.sum(route_share * mass_all / live_all)
-    d_final = cotangent.reshape(tokens, model_width).astype(jnp.float32) * live_rows[:, None]
-    d_moe_all = lax.all_gather(d_final.astype(jnp.bfloat16), "fsdp", axis=0, tiled=True)
-
-    def expert_backward(state_pair, group_in):
-        d_rows, d_gates = state_pair
-        slot_group, gate_w, up_w, down_w, gate_pre, up_pre = group_in
-        live_slot, pair_id, token_id, slot_gate = slot_inputs(slot_group)
-        picked = normed_all[token_id]
-        d_out_slot = d_moe_all[token_id]
-        silu_gate = jax.nn.silu(gate_pre)
-        scaled = (slot_gate[..., None] * silu_gate * up_pre).astype(jnp.bfloat16)
-        d_down = jnp.einsum("ech,ecd->edh", scaled, d_out_slot, preferred_element_type=jnp.float32)
-        d_scaled = jnp.einsum(
-            "ecd,edh->ech", d_out_slot, down_w, preferred_element_type=jnp.float32
-        )
-        d_slot_gate = jnp.sum(d_scaled * silu_gate * up_pre, -1)
-        d_act = d_scaled * slot_gate[..., None]
-        sigmoid_gate = jax.nn.sigmoid(gate_pre)
-        d_gate_pre = (
-            d_act * up_pre * (sigmoid_gate + gate_pre * sigmoid_gate * (1.0 - sigmoid_gate))
-        ).astype(jnp.bfloat16)
-        d_up_pre = (d_act * silu_gate).astype(jnp.bfloat16)
-        d_gate_w = jnp.einsum(
-            "ecd,ech->edh", picked, d_gate_pre, preferred_element_type=jnp.float32
-        )
-        d_up_w = jnp.einsum("ecd,ech->edh", picked, d_up_pre, preferred_element_type=jnp.float32)
-        d_picked = jnp.einsum(
-            "ech,edh->ecd", d_gate_pre, gate_w, preferred_element_type=jnp.float32
-        ) + jnp.einsum("ech,edh->ecd", d_up_pre, up_w, preferred_element_type=jnp.float32)
-        d_rows = d_rows.at[token_id.reshape(-1)].add(d_picked.reshape(-1, model_width))
-        d_gates = d_gates.at[pair_id.reshape(-1)].add(
-            jnp.where(live_slot, d_slot_gate, 0.0).reshape(-1)
-        )
-        group_terms = (d_gate_w, d_up_w, d_down)
-        return ((d_rows, d_gates), group_terms)
-
-    grad_pair, expert_terms = lax.scan(
-        expert_backward,
-        (
-            jnp.zeros((gathered_rows, model_width), jnp.float32),
-            jnp.zeros((gathered_rows * top_k,), jnp.float32),
-        ),
-        (slot_groups, gate_groups, up_groups, down_groups, kept_acts[0], kept_acts[1]),
-    )
-    grad_gate, grad_up, grad_down = (
-        lax.psum_scatter(
-            expert_terms[0].reshape(experts, model_width, hidden_part).astype(jnp.bfloat16),
-            "ctx",
-            scatter_dimension=1,
-            tiled=True,
-        ).astype(jnp.float32),
-        lax.psum_scatter(
-            expert_terms[1].reshape(experts, model_width, hidden_part).astype(jnp.bfloat16),
-            "ctx",
-            scatter_dimension=1,
-            tiled=True,
-        ).astype(jnp.float32),
-        lax.psum_scatter(
-            expert_terms[2].reshape(experts, model_width, hidden_part).astype(jnp.bfloat16),
-            "ctx",
-            scatter_dimension=1,
-            tiled=True,
-        ).astype(jnp.float32),
-    )
-    d_own, d_gate_own = (
-        lax.psum_scatter(
-            grad_pair[0].astype(jnp.bfloat16), "fsdp", scatter_dimension=0, tiled=True
-        ).astype(jnp.float32),
-        lax.psum_scatter(
-            grad_pair[1].reshape(gathered_rows, top_k).astype(jnp.bfloat16),
-            "fsdp",
-            scatter_dimension=0,
-            tiled=True,
-        ).astype(jnp.float32),
-    )
     d_probs = (
-        jnp.sum(d_gate_own[..., None] * own_hot, 1)
+        d_gate_own
         + loss_weight * experts * route_share[None, :] * live_rows[:, None] / live_all
     )
     d_logits = (own_probs * (d_probs - jnp.sum(own_probs * d_probs, -1, keepdims=True))).astype(
@@ -378,16 +477,23 @@
     )
     d_branch = d_resid.astype(jnp.bfloat16)
     grad_out = inner_rows(attended_low, d_branch)
+    early_terms = jnp.concatenate(
+        [
+            grad_out,
+            jnp.pad(
+                jnp.concatenate([grad_router, grad_gain_two[:, None]], 1),
+                ((0, 0), (0, LANES - experts - 1)),
+            ),
+        ],
+        1,
+    ).astype(jnp.bfloat16)
     d_attended = (
         back_rows(d_branch, output_matrix)
         .astype(jnp.bfloat16)
         .reshape(local_sequences, sequence_rows, KEY_VALUE_HEADS, query_group_width, HEAD_DIM)
     )
     row_delta = jnp.sum(d_attended.astype(jnp.float32) * attended, -1).transpose(0, 2, 3, 1)
-    key_again, value_again = (
-        lax.all_gather(key_rotated_rows, "ctx", axis=0, tiled=True),
-        lax.all_gather(value_low, "ctx", axis=0, tiled=True),
-    )
+    key_again, value_again = (key_all, value_all)
 
     def attend_back(d_query, block_id):
         key_pos, key_live = key_info(block_id)
@@ -430,20 +536,20 @@
         ),
         jnp.arange(key_blocks),
     )
-    local_key_gradient, d_value_own = (
-        lax.psum_scatter(
-            kv_terms[0].reshape(seq_len, local_sequences, key_value_width).astype(jnp.bfloat16),
-            "ctx",
-            scatter_dimension=0,
-            tiled=True,
-        ).astype(jnp.float32),
-        lax.psum_scatter(
-            kv_terms[1].reshape(seq_len, local_sequences, key_value_width).astype(jnp.bfloat16),
-            "ctx",
-            scatter_dimension=0,
-            tiled=True,
-        ).astype(jnp.float32),
-    )
+    key_value_gradient = lax.psum_scatter(
+        jnp.concatenate(
+            [
+                term.reshape(seq_len, local_sequences, key_value_width).astype(jnp.bfloat16)
+                for term in kv_terms
+            ],
+            -1,
+        ),
+        "ctx",
+        scatter_dimension=0,
+        tiled=True,
+    ).astype(jnp.float32)
+    local_key_gradient = key_value_gradient[..., :key_value_width]
+    d_value_own = key_value_gradient[..., key_value_width:]
     d_query_low = (
         unrotate(
             d_query.reshape(local_sequences, sequence_rows, QUERY_HEADS, HEAD_DIM), local_positions
@@ -476,14 +582,28 @@
     grad_input = d_resid + scale_one * (
         d_unit_one - unit_one * jnp.mean(d_unit_one * unit_one, -1, keepdims=True)
     )
+    late_rows = lax.psum_scatter(
+        jnp.concatenate(
+            [grad_query, grad_key, grad_value, jnp.pad(grad_gain_one[:, None], ((0, 0), (0, 127)))],
+            1,
+        ).astype(jnp.bfloat16),
+        ("ctx", "fsdp"),
+        scatter_dimension=0,
+        tiled=True,
+    ).astype(jnp.float32)
+    early_rows = lax.psum_scatter(early_terms, ("ctx", "fsdp"), scatter_dimension=0, tiled=True)
+    early_rows = early_rows.astype(jnp.float32)
+    query_width = QUERY_HEADS * HEAD_DIM
+    key_end = query_width + key_value_width
+    value_end = key_end + key_value_width
     summed = (
-        lax.psum_scatter(grad_gain_one, ("ctx", "fsdp"), scatter_dimension=0, tiled=True),
-        lax.psum_scatter(grad_query, ("ctx", "fsdp"), scatter_dimension=0, tiled=True),
-        lax.psum_scatter(grad_key, ("ctx", "fsdp"), scatter_dimension=0, tiled=True),
-        lax.psum_scatter(grad_value, ("ctx", "fsdp"), scatter_dimension=0, tiled=True),
-        lax.psum_scatter(grad_out, ("ctx", "fsdp"), scatter_dimension=0, tiled=True),
-        lax.psum_scatter(grad_gain_two, ("ctx", "fsdp"), scatter_dimension=0, tiled=True),
-        lax.psum_scatter(grad_router, ("ctx", "fsdp"), scatter_dimension=0, tiled=True),
+        late_rows[:, value_end],
+        late_rows[:, :query_width],
+        late_rows[:, query_width:key_end],
+        late_rows[:, key_end:value_end],
+        early_rows[:, :model_width],
+        early_rows[:, model_width + experts],
+        early_rows[:, model_width : model_width + experts],
     )
     return (
         layer_output,

time: 3030 us -> 2120 us (0.70)
  other arithmetic: 466 us -> 80.4 us
  matrix products: 401 us -> 76.2 us
  local copies, waits for them, and re-layouts: 392 us -> 159 us
  Pallas kernels: 0 us -> 231 us
  waiting for transfers between devices: 1620 us -> 1510 us
  blocking collectives: 103 us -> 38.9 us
    scatter-add x15 -> x0, other arithmetic: 396 us -> none  [the longest x5 159 us: expert_backward(): d_rows.at[token_id.reshape(-1)].add(d_picked.reshape(-1, model_width))]
    dot_general x45 -> x0, matrix products: 319 us -> none  [the longest x5 43.3 us: expert_backward(): jnp.einsum('ech,edh->ecd', d_up_pre, up_w, preferred_element_type=jnp.flo...]
    gather x35 -> x0, local copies, waits for them, and re-layouts: 290 us -> none  [the longest x20 118 us: slot_inputs(): slot_gate = jnp.where(live_slot, flat_gates[pair_id], 0.0)]
    pallas_call x0 -> x4, Pallas kernels: none -> 231 us  [expert_call(): pl.pallas_call(kernel, grid=(expert_total // 2,), in_specs=[whole((rows,...]
    reduce_scatter x11 -> x16, waiting for transfers between devices: 1300 us -> 1070 us  [the longest x12 1010 us: local(): lax.psum_scatter(piece_grad, 'ctx', scatter_dimension=1, tiled=True)]
    unnamed x23 -> x28, waiting for transfers between devices: 165 us -> 245 us
    pallas_call x0 -> x8, local copies, waits for them, and re-layouts: none -> 53.6 us  [expert_call(): pl.pallas_call(kernel, grid=(expert_total // 2,), in_specs=[whole((rows,...]
    psum x1 -> x0, blocking collectives: 39.9 us -> none  [local(): count_all, mass_all = lax.psum((counts, prob_mass), ('ctx', 'fsdp'))]
  transfers between devices with their start and end apart: 21 -> 26, of which waited for: 18 -> 24; matrix products, arithmetic and copies ran while one was open for 19% -> 11% of each run, Pallas kernels for 0% -> 0%
where the time goes in v1:
time: 2120 us; the launch traced here: 2110 us
  waiting for transfers between devices  1510 us (71%)
  Pallas kernels  231 us (11%)
  local copies, waits for them, and re-layouts  159 us (8%)
  other arithmetic  80.4 us (4%)
  matrix products  76.2 us (4%)
  blocking collectives  38.9 us (2%)
    reduce_scatter x12, waiting for transfers between devices, local(): lax.psum_scatter(piece_grad, 'ctx', scatter_dimension=1, tiled=True)  1010 us
    unnamed x28, waiting for transfers between devices  245 us
    pallas_call x4, Pallas kernels, expert_call(): pl.pallas_call(kernel, grid=(expert_total // 2,), in_specs=[whole((rows,...  231 us
    pallas_call x8, local copies, waits for them, and re-layouts, expert_call(): pl.pallas_call(kernel, grid=(expert_total // 2,), in_specs=[whole((rows,...  53.6 us
    reduce_scatter x1, waiting for transfers between devices, local(): lax.psum_scatter(jnp.concatenate([term.reshape(seq_len, local_sequences,...  51 us
    all_gather x1, waiting for transfers between devices, local(): lax.all_gather(key_rotated_rows, 'ctx', axis=0, tiled=True)  46.1 us
  transfers between devices with their start and end apart: 26, of which 24 were waited for; matrix products, arithmetic and copies ran while one was open for 11% of the time, Pallas kernels for 0%

profile of v1, /device:TPU:0, one launch (start us, length us, event | category | flops | bytes accessed | tf_op | source)
XLA Modules:
  0.0 2114.3 jit_solution(15246583263881476564)
XLA Ops:
  74.8 30.2 %all-gather.14.cloned.1.call-done = bf16[512,4,512]{2,0,1:T(8,128)(2,1)} async-done(((bf16[64,4,512]{2,0,1:T(8,128)(2,1)}), bf16[512,4,512]{2,0,1:T(8,128)(2,1)}) %all-gather.14.cloned.1.call-update) | async-done | bytes 2097168 | tf_op jit(solution)/shard_map/all_gather | solution.py:321
  109.2 46.1 %all-gather.18.cloned.1.call-done = bf16[512,4,512]{2,1,0:T(4,128)(2,1)} async-done(((bf16[64,4,512]{2,1,0:T(4,128)(2,1)}), bf16[512,4,512]{2,1,0:T(4,128)(2,1)}) %all-gather.18.cloned.1.call-update) | async-done | bytes 2097168 | tf_op jit(solution)/shard_map/all_gather | solution.py:320
  158.2 34.4 %all-gather.20.cloned.1.call-done = bf16[1536,1536]{1,0:T(8,128)(2,1)} async-done(((bf16[384,1536]{1,0:T(8,128)(2,1)}), bf16[1536,1536]{1,0:T(8,128)(2,1)}) %all-gather.20.cloned.1.call-update) | async-done | bytes 4718608 | tf_op jit(solution)/shard_map/all_gather | solution.py:285
  267.6 25.8 %all-gather.24.cloned.1.call-done = bf16[1024,1536]{0,1:T(8,128)(2,1)} async-done(((bf16[256,1536]{0,1:T(8,128)(2,1)}), bf16[1024,1536]{0,1:T(8,128)(2,1)}) %all-gather.24.cloned.1.call-update) | async-done | bytes 3145744 | tf_op jit(solution)/shard_map/all_gather | solution.py:394
  305.2 57.8 %expert_step.7 = (bf16[10,1536,128]{2,1,0:T(8,128)(2,1)}, bf16[10,1536,128]{2,1,0:T(8,128)(2,1)}, bf16[10,1536,128]{2,1,0:T(8,128)(2,1)}, f32[1024,1536]{1,0:T(8...) custom-call(bf16[1024,1536]{1,0:T(8,128)(2,1)} %copy.193.normed, bf16[1536,1024]{1,0:T(8,128)(2,1)} %bitcast.173, ...), custom_call_target="tpu_custom_call" | custom-call | tf_op jit(solution)/shard_map/expert_step/pallas_call | solution.py:205
  363.0 57.6 %expert_step.6 = (bf16[10,1536,128]{2,1,0:T(8,128)(2,1)}, bf16[10,1536,128]{2,1,0:T(8,128)(2,1)}, bf16[10,1536,128]{2,1,0:T(8,128)(2,1)}, f32[1024,1536]{1,0:T(8...) custom-call(bf16[1024,1536]{1,0:T(8,128)(2,1)} %copy.193.normed, bf16[1536,1024]{1,0:T(8,128)(2,1)} %bitcast.174, ...), custom_call_target="tpu_custom_call" | custom-call | tf_op jit(solution)/shard_map/expert_step/pallas_call | solution.py:205
  420.7 57.8 %expert_step.5 = (bf16[10,1536,128]{2,1,0:T(8,128)(2,1)}, bf16[10,1536,128]{2,1,0:T(8,128)(2,1)}, bf16[10,1536,128]{2,1,0:T(8,128)(2,1)}, f32[1024,1536]{1,0:T(8...) custom-call(bf16[1024,1536]{1,0:T(8,128)(2,1)} %copy.193.normed, bf16[1536,1024]{1,0:T(8,128)(2,1)} %bitcast.175, ...), custom_call_target="tpu_custom_call" | custom-call | tf_op jit(solution)/shard_map/expert_step/pallas_call | solution.py:205
  478.5 58.2 %expert_step.4 = (bf16[10,1536,128]{2,1,0:T(8,128)(2,1)}, bf16[10,1536,128]{2,1,0:T(8,128)(2,1)}, bf16[10,1536,128]{2,1,0:T(8,128)(2,1)}, f32[1024,1536]{1,0:T(8...) custom-call(bf16[1024,1536]{1,0:T(8,128)(2,1)} %copy.193.normed, bf16[1536,1024]{1,0:T(8,128)(2,1)} %bitcast.176, ...), custom_call_target="tpu_custom_call" | custom-call | tf_op jit(solution)/shard_map/expert_step/pallas_call | solution.py:205
  619.7 21.3 %all-reduce.3 = f32[640]{0:T(1024)S(1)} all-reduce(f32[640]{0:T(1024)S(1)} %maximum_dynamic-update-slice_fusion), channel_id=2, replica_groups=mesh['ctx'=8,'fsdp'=4] {'ctx'}, use_global_device_ids=true, to_apply=%add.3 | all-reduce | flops 640 | bytes 5120
  743.9 51.0 %reduce-scatter.29.cloned.1.call-done = bf16[64,4,1024]{2,0,1:T(8,128)(2,1)} async-done(((bf16[512,4,1024]{2,0,1:T(8,128)(2,1)}), bf16[64,4,1024]{2,0,1:T(8,128)(2,1)}) %reduce-scatter.29.cloned.1.call-update) | async-done | bytes 524304 | tf_op jit(solution)/shard_map/reduce_scatter | solution.py:539
  832.3 51.1 %reduce-scatter.53.cloned.1.call-done = bf16[10,192,128]{2,1,0:T(8,128)(2,1)} async-done(((bf16[10,1536,128]{2,1,0:T(8,128)(2,1)}), bf16[10,192,128]{2,1,0:T(8,128)(2,1)}) %reduce-scatter.53.cloned.1.call-update) | async-done | bytes 491536 | tf_op jit(solution)/shard_map/reduce_scatter | solution.py:426
  883.5 87.8 %reduce-scatter.51.cloned.1.call-done = bf16[10,192,128]{2,1,0:T(8,128)(2,1)} async-done(((bf16[10,1536,128]{2,1,0:T(8,128)(2,1)}), bf16[10,192,128]{2,1,0:T(8,128)(2,1)}) %reduce-scatter.51.cloned.1.call-update) | async-done | bytes 491536 | tf_op jit(solution)/shard_map/reduce_scatter | solution.py:426
  971.2 87.8 %reduce-scatter.49.cloned.1.call-done = bf16[10,192,128]{2,1,0:T(8,128)(2,1)} async-done(((bf16[10,1536,128]{2,1,0:T(8,128)(2,1)}), bf16[10,192,128]{2,1,0:T(8,128)(2,1)}) %reduce-scatter.49.cloned.1.call-update) | async-done | bytes 491536 | tf_op jit(solution)/shard_map/reduce_scatter | solution.py:426
  1059.1 87.8 %reduce-scatter.47.cloned.1.call-done = bf16[10,192,128]{2,1,0:T(8,128)(2,1)} async-done(((bf16[10,1536,128]{2,1,0:T(8,128)(2,1)}), bf16[10,192,128]{2,1,0:T(8,128)(2,1)}) %reduce-scatter.47.cloned.1.call-update) | async-done | bytes 491536 | tf_op jit(solution)/shard_map/reduce_scatter | solution.py:426
  1150.6 84.7 %reduce-scatter.45.cloned.1.call-done = bf16[10,192,128]{2,1,0:T(8,128)(2,1)} async-done(((bf16[10,1536,128]{2,1,0:T(8,128)(2,1)}), bf16[10,192,128]{2,1,0:T(8,128)(2,1)}) %reduce-scatter.45.cloned.1.call-update) | async-done | bytes 491536 | tf_op jit(solution)/shard_map/reduce_scatter | solution.py:426
  1235.3 87.8 %reduce-scatter.43.cloned.1.call-done = bf16[10,192,128]{2,1,0:T(8,128)(2,1)} async-done(((bf16[10,1536,128]{2,1,0:T(8,128)(2,1)}), bf16[10,192,128]{2,1,0:T(8,128)(2,1)}) %reduce-scatter.43.cloned.1.call-update) | async-done | bytes 491536 | tf_op jit(solution)/shard_map/reduce_scatter | solution.py:426
  1323.1 88.0 %reduce-scatter.41.cloned.1.call-done = bf16[10,192,128]{2,1,0:T(8,128)(2,1)} async-done(((bf16[10,1536,128]{2,1,0:T(8,128)(2,1)}), bf16[10,192,128]{2,1,0:T(8,128)(2,1)}) %reduce-scatter.41.cloned.1.call-update) | async-done | bytes 491536 | tf_op jit(solution)/shard_map/reduce_scatter | solution.py:426
  1411.1 87.8 %reduce-scatter.39.cloned.1.call-done = bf16[10,192,128]{2,1,0:T(8,128)(2,1)} async-done(((bf16[10,1536,128]{2,1,0:T(8,128)(2,1)}), bf16[10,192,128]{2,1,0:T(8,128)(2,1)}) %reduce-scatter.39.cloned.1.call-update) | async-done | bytes 491536 | tf_op jit(solution)/shard_map/reduce_scatter | solution.py:426
  1502.6 84.8 %reduce-scatter.37.cloned.1.call-done = bf16[10,192,128]{2,1,0:T(8,128)(2,1)} async-done(((bf16[10,1536,128]{2,1,0:T(8,128)(2,1)}), bf16[10,192,128]{2,1,0:T(8,128)(2,1)}) %reduce-scatter.37.cloned.1.call-update) | async-done | bytes 491536 | tf_op jit(solution)/shard_map/reduce_scatter | solution.py:426
  1587.4 88.0 %reduce-scatter.35.cloned.1.call-done = bf16[10,192,128]{2,1,0:T(8,128)(2,1)} async-done(((bf16[10,1536,128]{2,1,0:T(8,128)(2,1)}), bf16[10,192,128]{2,1,0:T(8,128)(2,1)}) %reduce-scatter.35.cloned.1.call-update) | async-done | bytes 491536 | tf_op jit(solution)/shard_map/reduce_scatter | solution.py:426
  1675.4 88.0 %reduce-scatter.33.cloned.1.call-done = bf16[10,192,128]{2,1,0:T(8,128)(2,1)} async-done(((bf16[10,1536,128]{2,1,0:T(8,128)(2,1)}), bf16[10,192,128]{2,1,0:T(8,128)(2,1)}) %reduce-scatter.33.cloned.1.call-update) | async-done | bytes 491536 | tf_op jit(solution)/shard_map/reduce_scatter | solution.py:426
  1763.4 87.9 %reduce-scatter.31.cloned.1.call-done = bf16[10,192,128]{2,1,0:T(8,128)(2,1)} async-done(((bf16[10,1536,128]{2,1,0:T(8,128)(2,1)}), bf16[10,192,128]{2,1,0:T(8,128)(2,1)}) %reduce-scatter.31.cloned.1.call-update) | async-done | bytes 491536 | tf_op jit(solution)/shard_map/reduce_scatter | solution.py:426
  1855.0 111.0 %reduce-scatter.57.cloned.1.call-done = bf16[48,1664]{1,0:T(8,128)(2,1)} async-done(((bf16[1536,1664]{1,0:T(8,128)(2,1)}), bf16[48,1664]{1,0:T(8,128)(2,1)}) %reduce-scatter.57.cloned.1.call-update) | async-done | bytes 159760
  1977.5 124.4 %reduce-scatter.55.cloned.1.call-done = bf16[48,2688]{1,0:T(8,128)(2,1)} async-done(((bf16[1536,2688]{1,0:T(8,128)(2,1)}), bf16[48,2688]{1,0:T(8,128)(2,1)}) %reduce-scatter.55.cloned.1.call-update) | async-done | bytes 258064
  (335 shorter events, 408.6 us)
Async XLA Ops:
  8.7 96.4 %all-gather.14.cloned.1.call-start = ((), (), s32[]{:S(2)}) async-start(), calls=%async_computation.19 | async-start | bytes 2359296 | tf_op jit(solution)/shard_map/all_gather | solution.py:321
  34.7 120.6 %all-gather.18.cloned.1.call-start = ((), (), s32[]{:S(2)}) async-start(), calls=%async_computation.21 | async-start | bytes 2359296 | tf_op jit(solution)/shard_map/all_gather | solution.py:320
  59.2 133.4 %all-gather.20.cloned.1.call-start = ((), (), s32[]{:S(2)}) async-start(), calls=%async_computation.22 | async-start | bytes 5898240 | tf_op jit(solution)/shard_map/all_gather | solution.py:285
  59.8 171.7 %all-gather.22.cloned.1.call-start = ((), (), s32[]{:S(2)}) async-start(), calls=%async_computation.23 | async-start | bytes 5898240 | tf_op jit(solution)/shard_map/all_gather | solution.py:288
  60.4 202.6 %all-gather.26.cloned.1.call-start = ((), (), s32[]{:S(2)}) async-start(), calls=%async_computation.25 | async-start | bytes 3932160 | tf_op jit(solution)/shard_map/all_gather | solution.py:293
  65.2 228.2 %all-gather.24.cloned.1.call-start = ((), (), s32[]{:S(2)}) async-start(), calls=%async_computation.24 | async-start | bytes 3932160 | tf_op jit(solution)/shard_map/all_gather | solution.py:394
  238.4 403.3 %reduce-scatter.27.cloned.1.call-start = ((), (), s32[]{:S(2)}) async-start(), calls=%async_computation.28 | async-start | bytes 327680 | tf_op jit(solution)/shard_map/reduce_scatter | solution.py:441
  557.5 85.4 %reduce-scatter.25.cloned.1.call-start = ((), (), s32[]{:S(2)}) async-start(), calls=%async_computation.27 | async-start | bytes 3932160 | tf_op jit(solution)/shard_map/reduce_scatter | solution.py:438
  576.6 81.5 %reduce-scatter.23.cloned.1.call-start = ((), (), s32[]{:S(2)}) async-start(), calls=%async_computation.26 | async-start | bytes 3932160 | tf_op jit(solution)/shard_map/reduce_scatter | solution.py:447
  616.4 178.5 %reduce-scatter.29.cloned.1.call-start = ((), (), s32[]{:S(2)}) async-start(), calls=%async_computation.29 | async-start | bytes 4718592 | tf_op jit(solution)/shard_map/reduce_scatter | solution.py:539
  706.0 177.4 %reduce-scatter.53.cloned.1.call-start = ((), (), s32[]{:S(2)}) async-start(), calls=%async_computation.41 | async-start | bytes 4423680 | tf_op jit(solution)/shard_map/reduce_scatter | solution.py:426
  706.8 264.5 %reduce-scatter.51.cloned.1.call-start = ((), (), s32[]{:S(2)}) async-start(), calls=%async_computation.40 | async-start | bytes 4423680 | tf_op jit(solution)/shard_map/reduce_scatter | solution.py:426
  707.4 351.7 %reduce-scatter.49.cloned.1.call-start = ((), (), s32[]{:S(2)}) async-start(), calls=%async_computation.39 | async-start | bytes 4423680 | tf_op jit(solution)/shard_map/reduce_scatter | solution.py:426
  708.0 438.9 %reduce-scatter.47.cloned.1.call-start = ((), (), s32[]{:S(2)}) async-start(), calls=%async_computation.38 | async-start | bytes 4423680 | tf_op jit(solution)/shard_map/reduce_scatter | solution.py:426
  708.5 526.7 %reduce-scatter.45.cloned.1.call-start = ((), (), s32[]{:S(2)}) async-start(), calls=%async_computation.37 | async-start | bytes 4423680 | tf_op jit(solution)/shard_map/reduce_scatter | solution.py:426
  709.1 614.0 %reduce-scatter.43.cloned.1.call-start = ((), (), s32[]{:S(2)}) async-start(), calls=%async_computation.36 | async-start | bytes 4423680 | tf_op jit(solution)/shard_map/reduce_scatter | solution.py:426
  709.7 701.4 %reduce-scatter.41.cloned.1.call-start = ((), (), s32[]{:S(2)}) async-start(), calls=%async_computation.35 | async-start | bytes 4423680 | tf_op jit(solution)/shard_map/reduce_scatter | solution.py:426
  710.4 788.5 %reduce-scatter.39.cloned.1.call-start = ((), (), s32[]{:S(2)}) async-start(), calls=%async_computation.34 | async-start | bytes 4423680 | tf_op jit(solution)/shard_map/reduce_scatter | solution.py:426
  711.0 876.4 %reduce-scatter.37.cloned.1.call-start = ((), (), s32[]{:S(2)}) async-start(), calls=%async_computation.33 | async-start | bytes 4423680 | tf_op jit(solution)/shard_map/reduce_scatter | solution.py:426
  711.8 963.6 %reduce-scatter.35.cloned.1.call-start = ((), (), s32[]{:S(2)}) async-start(), calls=%async_computation.32 | async-start | bytes 4423680 | tf_op jit(solution)/shard_map/reduce_scatter | solution.py:426
  712.5 1050.9 %reduce-scatter.33.cloned.1.call-start = ((), (), s32[]{:S(2)}) async-start(), calls=%async_computation.31 | async-start | bytes 4423680 | tf_op jit(solution)/shard_map/reduce_scatter | solution.py:426
  713.3 1138.0 %reduce-scatter.31.cloned.1.call-start = ((), (), s32[]{:S(2)}) async-start(), calls=%async_computation.30 | async-start | bytes 4423680 | tf_op jit(solution)/shard_map/reduce_scatter | solution.py:426
  713.9 1252.1 %reduce-scatter.57.cloned.1.call-start = ((), (), s32[]{:S(2)}) async-start(), calls=%async_computation.43 | async-start | bytes 5271552
  727.7 1374.2 %reduce-scatter.55.cloned.1.call-start = ((), (), s32[]{:S(2)}) async-start(), calls=%async_computation.42 | async-start | bytes 8515584
  (64 other events, 968.8 us)
Sparse Core Ops, SparseCore 0:
  9.6 22.3 all-gather.11
  55.9 49.0 all-gather.13
  107.6 47.6 all-gather.17
  156.7 35.9 all-gather.19
  194.1 37.4 all-gather.21
  233.7 29.2 all-gather.25
  264.5 28.8 all-gather.23
  580.1 37.7 reduce-scatter.24
  620.4 37.7 reduce-scatter.22
  706.2 88.7 reduce-scatter.28
  799.2 84.2 reduce-scatter.52
  887.0 84.2 reduce-scatter.50
  974.8 84.2 reduce-scatter.48
  1062.6 84.2 reduce-scatter.46
  1151.0 84.2 reduce-scatter.44
  1238.8 84.2 reduce-scatter.42
  1326.8 84.2 reduce-scatter.40
  1414.6 84.2 reduce-scatter.38
  1503.1 84.2 reduce-scatter.36
  1591.1 84.2 reduce-scatter.34
  1679.1 84.2 reduce-scatter.32
  1766.9 84.3 reduce-scatter.30
  1856.9 109.0 reduce-scatter.56
  1971.7 130.0 reduce-scatter.54
  (2 shorter events, 39.5 us)

commit v2 on v1

v2 whole, which is shorter than its diff:
```python
import jax
import jax.numpy as jnp
from jax import lax
from jax.experimental import pallas as pl
from jax.experimental.pallas import tpu as pltpu
from jax.sharding import Mesh
from jax.sharding import PartitionSpec as P

QUERY_HEADS = 24
KEY_VALUE_HEADS = 8
HEAD_DIM = 64
GROUP = QUERY_HEADS // KEY_VALUE_HEADS
QUERY_GROUP = GROUP * HEAD_DIM
FUSED_GROUP = QUERY_GROUP + 2 * HEAD_DIM
FUSED_WIDTH = KEY_VALUE_HEADS * FUSED_GROUP
LANES = 128
ROW_BLOCK = 512
CHUNKS = (8, 8, 8, 8, 8)
CTX = ("z", "y")
SHARD = ("x", "k")
EVERY = ("z", "y", "x", "k")

epsilon = 1e-05
rope_base = 10000.0
loss_weight = 0.01
mask_value = -1e30


def plain(left_side, right_side):
    return jnp.dot(left_side, right_side, preferred_element_type=jnp.float32)


def turned(left_side, right_side):
    return lax.dot_general(
        left_side, right_side, (((1,), (1,)), ((), ())), preferred_element_type=jnp.float32
    )


def over_rows(left_side, right_side):
    return lax.dot_general(
        left_side, right_side, (((0,), (0,)), ((), ())), preferred_element_type=jnp.float32
    )


def rms_scale(values):
    return lax.rsqrt(jnp.mean(values * values, -1, keepdims=True) + epsilon)


def params(count):
    return pltpu.CompilerParams(
        dimension_semantics=("arbitrary",) * count, vmem_limit_bytes=60 * 1024 * 1024
    )


def whole(shape, single=True):
    zeros = (0,) * len(shape)
    if single:
        return pl.BlockSpec(shape, lambda *ids: zeros, pipeline_mode=pl.Buffered(1))
    return pl.BlockSpec(shape, lambda *ids: zeros)


def rope_tables(token_positions):
    frequency = rope_base ** (-jnp.arange(HEAD_DIM // 2, dtype=jnp.float32) * 2.0 / HEAD_DIM)
    angles = token_positions.astype(jnp.float32)[..., None] * frequency
    cosine, sine_part = jnp.cos(angles), jnp.sin(angles)
    return (
        jnp.concatenate([cosine, cosine], -1),
        jnp.concatenate([-sine_part, sine_part], -1),
    )


def swapped_halves(values):
    width = values.shape[1]
    lane = lax.broadcasted_iota(jnp.int32, values.shape, 1)
    ahead = pltpu.roll(values, width - HEAD_DIM // 2, 1)
    behind = pltpu.roll(values, HEAD_DIM // 2, 1)
    return jnp.where(lane % HEAD_DIM < HEAD_DIM // 2, ahead, behind)


def project_in(rows_in, gain_row, fused_weight, cosine, sine_part):
    tokens, width = rows_in.shape
    step_width = 2 * FUSED_GROUP

    def kernel(rows, gain, weight, cos_ref, sin_ref, fused, normed):
        @pl.when(pl.program_id(0) == 0)
        def _():
            values = rows[...].astype(jnp.float32)
            normed[...] = (values * rms_scale(values) * gain[...]).astype(jnp.bfloat16)

        product = plain(normed[...], weight[...])
        rotated = (product * cos_ref[...] + swapped_halves(product) * sin_ref[...]).astype(
            jnp.bfloat16
        )
        fused[0] = rotated[:, :FUSED_GROUP]
        fused[1] = rotated[:, FUSED_GROUP:]

    return pl.pallas_call(
        kernel,
        grid=(KEY_VALUE_HEADS // 2,),
        in_specs=[
            whole((tokens, width)),
            whole((1, width)),
            pl.BlockSpec((width, step_width), lambda i: (0, i)),
            whole((tokens, step_width)),
            whole((tokens, step_width)),
        ],
        out_specs=[
            pl.BlockSpec((2, tokens, FUSED_GROUP), lambda i: (i, 0, 0)),
            whole((tokens, width)),
        ],
        out_shape=[
            jax.ShapeDtypeStruct((KEY_VALUE_HEADS, tokens, FUSED_GROUP), jnp.bfloat16),
            jax.ShapeDtypeStruct((tokens, width), jnp.bfloat16),
        ],
        name="project_in",
        compiler_params=params(1),
    )(rows_in, gain_row, fused_weight, cosine, sine_part)


def head_probs(query_head, key_rows, visible):
    scores = jnp.where(visible, turned(query_head, key_rows) * HEAD_DIM ** (-0.5), mask_value)
    weights = jnp.exp(scores - jnp.max(scores, -1, keepdims=True))
    return weights * (1.0 / jnp.sum(weights, -1, keepdims=True))


def attend(fused_rows, row_positions, column_positions, lengths_here):
    n_ctx, sequences, span, unused = fused_rows.shape
    seq_len = n_ctx * span
    blocks = max(1, min(n_ctx, 512 * 512 // seq_len // span))
    tile = blocks * span

    def kernel(lengths_ref, query_ref, key_ref, row_ref, column_ref, out_ref):
        length = lengths_ref[pl.program_id(0)]
        fused_keys = key_ref[...].reshape(seq_len, FUSED_GROUP)
        key_rows = fused_keys[:, QUERY_GROUP : QUERY_GROUP + HEAD_DIM]
        value_rows = fused_keys[:, QUERY_GROUP + HEAD_DIM :]
        queries = query_ref[...].reshape(tile, FUSED_GROUP)
        key_pos = column_ref[:1, :]
        visible = (key_pos <= row_ref[:, :1]) & (key_pos < length)
        outs = []
        for head in range(GROUP):
            prob = head_probs(queries[:, head * HEAD_DIM : (head + 1) * HEAD_DIM], key_rows, visible)
            outs.append(plain(prob.astype(jnp.bfloat16), value_rows).astype(jnp.bfloat16))
        out_ref[...] = jnp.concatenate(outs, 1).reshape(blocks, 1, span, QUERY_GROUP)

    return pl.pallas_call(
        kernel,
        grid_spec=pltpu.PrefetchScalarGridSpec(
            num_scalar_prefetch=1,
            grid=(sequences, n_ctx // blocks),
            in_specs=[
                pl.BlockSpec((blocks, 1, span, FUSED_GROUP), lambda s, i, n: (i, s, 0, 0)),
                pl.BlockSpec((n_ctx, 1, span, FUSED_GROUP), lambda s, i, n: (0, s, 0, 0)),
                pl.BlockSpec((tile, LANES), lambda s, i, n: (i, 0)),
                pl.BlockSpec((8, seq_len), lambda s, i, n: (0, 0)),
            ],
            out_specs=pl.BlockSpec((blocks, 1, span, QUERY_GROUP), lambda s, i, n: (i, s, 0, 0)),
        ),
        out_shape=jax.ShapeDtypeStruct((n_ctx, sequences, span, QUERY_GROUP), jnp.bfloat16),
        name="attend",
        compiler_params=params(2),
    )(lengths_here, fused_rows, fused_rows, row_positions, column_positions)


def attend_back(
    fused_rows, d_attended, row_positions, column_positions, cosine, sine_part, lengths_here
):
    n_ctx, sequences, span, unused = fused_rows.shape
    seq_len = n_ctx * span
    blocks = max(1, min(n_ctx, 512 * 512 // seq_len // span))
    tile = blocks * span
    padded = FUSED_GROUP + HEAD_DIM

    def kernel(
        lengths_ref,
        query_ref,
        key_ref,
        d_ref,
        row_ref,
        column_ref,
        cos_ref,
        sin_ref,
        out_ref,
        d_query_keep,
        d_key_keep,
        d_value_keep,
    ):
        part = pl.program_id(1)
        length = lengths_ref[pl.program_id(0)]
        fused_keys = key_ref[...].reshape(seq_len, FUSED_GROUP)
        key_rows = fused_keys[:, QUERY_GROUP : QUERY_GROUP + HEAD_DIM]
        value_rows = fused_keys[:, QUERY_GROUP + HEAD_DIM :]
        queries = query_ref[...].reshape(tile, FUSED_GROUP)
        d_rows = d_ref[...].reshape(tile, QUERY_GROUP)
        key_pos = column_ref[:1, :]
        visible = (key_pos <= row_ref[:, :1]) & (key_pos < length)

        @pl.when(part == 0)
        def _():
            d_key_keep[...] = jnp.zeros_like(d_key_keep)
            d_value_keep[...] = jnp.zeros_like(d_value_keep)

        d_queries = []
        for head in range(GROUP):
            lanes = slice(head * HEAD_DIM, (head + 1) * HEAD_DIM)
            query_head, d_head = queries[:, lanes], d_rows[:, lanes]
            prob = head_probs(query_head, key_rows, visible)
            d_prob = turned(d_head, value_rows)
            delta = jnp.sum(prob * d_prob, -1, keepdims=True)
            d_score = (prob * (d_prob - delta) * HEAD_DIM ** (-0.5)).astype(jnp.bfloat16)
            d_queries.append(plain(d_score, key_rows))
            d_key_keep[...] += over_rows(d_score, query_head)
            d_value_keep[...] += over_rows(prob.astype(jnp.bfloat16), d_head)
        d_query_keep[pl.ds(pl.multiple_of(part * tile, tile), tile), :] = jnp.concatenate(
            d_queries, 1
        )

        @pl.when(part == pl.num_programs(1) - 1)
        def _():
            turned_part = jnp.concatenate([d_query_keep[...], d_key_keep[...]], 1)
            table_cos = jnp.concatenate([cos_ref[...], cos_ref[...]], 1)
            table_sin = jnp.concatenate([sin_ref[...], sin_ref[...]], 1)
            back = turned_part * table_cos - swapped_halves(turned_part) * table_sin
            out_ref[...] = (
                jnp.concatenate([back, d_value_keep[...]], 1)
                .astype(jnp.bfloat16)
                .reshape(n_ctx, 1, span, FUSED_GROUP)
            )

    return pl.pallas_call(
        kernel,
        grid_spec=pltpu.PrefetchScalarGridSpec(
            num_scalar_prefetch=1,
            grid=(sequences, n_ctx // blocks),
            in_specs=[
                pl.BlockSpec((blocks, 1, span, FUSED_GROUP), lambda s, i, n: (i, s, 0, 0)),
                pl.BlockSpec((n_ctx, 1, span, FUSED_GROUP), lambda s, i, n: (0, s, 0, 0)),
                pl.BlockSpec((blocks, 1, span, QUERY_GROUP), lambda s, i, n: (i, s, 0, 0)),
                pl.BlockSpec((tile, LANES), lambda s, i, n: (i, 0)),
                pl.BlockSpec((8, seq_len), lambda s, i, n: (0, 0)),
                pl.BlockSpec((seq_len, LANES), lambda s, i, n: (0, 0)),
                pl.BlockSpec((seq_len, LANES), lambda s, i, n: (0, 0)),
            ],
            out_specs=pl.BlockSpec((n_ctx, 1, span, FUSED_GROUP), lambda s, i, n: (0, s, 0, 0)),
            scratch_shapes=[
                pltpu.VMEM((seq_len, QUERY_GROUP), jnp.float32),
                pltpu.VMEM((seq_len, HEAD_DIM), jnp.float32),
                pltpu.VMEM((seq_len, HEAD_DIM), jnp.float32),
            ],
        ),
        out_shape=jax.ShapeDtypeStruct((n_ctx, sequences, span, FUSED_GROUP), jnp.bfloat16),
        name="attend_back",
        compiler_params=params(2),
    )(
        lengths_here,
        fused_rows,
        fused_rows,
        d_attended,
        row_positions,
        column_positions,
        cosine,
        sine_part,
    )


def project_out(attended_groups, rows_in, out_weight, gain_row):
    tokens, width = rows_in.shape

    def kernel(groups, rows, weight, gain, residual, normed, joined):
        attended = jnp.concatenate([groups[j] for j in range(KEY_VALUE_HEADS)], 1)
        joined[...] = attended
        total = rows[...].astype(jnp.float32) + plain(attended, weight[...])
        residual[...] = total
        normed[...] = (total * rms_scale(total) * gain[...]).astype(jnp.bfloat16)

    return pl.pallas_call(
        kernel,
        grid=(1,),
        in_specs=[
            whole(attended_groups.shape),
            whole((tokens, width)),
            whole((QUERY_HEADS * HEAD_DIM, width)),
            whole((1, width)),
        ],
        out_specs=[
            whole((tokens, width)),
            whole((tokens, width)),
            whole((tokens, QUERY_HEADS * HEAD_DIM)),
        ],
        out_shape=[
            jax.ShapeDtypeStruct((tokens, width), jnp.float32),
            jax.ShapeDtypeStruct((tokens, width), jnp.bfloat16),
            jax.ShapeDtypeStruct((tokens, QUERY_HEADS * HEAD_DIM), jnp.bfloat16),
        ],
        name="project_out",
        compiler_params=params(1),
    )(attended_groups, rows_in, out_weight, gain_row)


def expert_chunk(
    first_expert,
    expert_total,
    side,
    ctx_parts,
    normed_rows,
    normed_turned,
    cotangent_rows,
    cotangent_turned,
    gate_table,
    w_gate,
    w_up,
    w_down,
    kept,
):
    rows, width = normed_rows.shape
    experts, unused, hidden = w_gate.shape
    pair_width = 2 * hidden
    slab = width // (2 * ctx_parts)
    row_block = min(ROW_BLOCK, rows)

    def kernel(
        side_ref,
        normed,
        normed_t,
        cotan,
        cotan_t,
        gates,
        gate_w,
        up_w,
        down_w,
        *rest,
    ):
        stay, leave, acts, d_gates = rest[-4:]
        first = first_expert + 2 * pl.program_id(0)

        @pl.when(pl.program_id(0) == 0)
        def _():
            d_gates[...] = jnp.zeros_like(d_gates)

        def joined(pair_ref):
            return jnp.concatenate([pair_ref[0], pair_ref[1]], axis=1)

        gate_pair, up_pair, down_pair = joined(gate_w), joined(up_w), joined(down_w)
        lane = lax.broadcasted_iota(jnp.int32, (row_block, LANES), 1)

        def row_step(block, carry):
            span = pl.ds(pl.multiple_of(block * row_block, row_block), row_block)
            normed_part, cotan_part = normed[span, :], cotan[span, :]
            gate_part = gates[span, :]
            slot_gate = jnp.concatenate(
                [
                    jnp.broadcast_to(
                        jnp.sum(
                            jnp.where(lane == first + j, gate_part, 0.0), axis=1, keepdims=True
                        ),
                        (row_block, hidden),
                    )
                    for j in range(2)
                ],
                axis=1,
            )
            gate_pre = plain(normed_part, gate_pair)
            up_pre = plain(normed_part, up_pair)
            d_scaled = plain(cotan_part, down_pair)
            sigmoid_gate = jax.nn.sigmoid(gate_pre)
            silu_gate = gate_pre * sigmoid_gate
            scaled = (slot_gate * silu_gate * up_pre).astype(jnp.bfloat16)
            gate_term = d_scaled * silu_gate * up_pre
            d_gate_part = d_gates[span, :]
            for j in range(2):
                d_gate_part = d_gate_part + jnp.where(
                    lane == first + j,
                    jnp.sum(gate_term[:, j * hidden : (j + 1) * hidden], axis=1, keepdims=True),
                    0.0,
                )
            d_gates[span, :] = d_gate_part
            d_act = d_scaled * slot_gate
            acts[0, 0, span, :] = scaled
            acts[1, 0, span, :] = (
                d_act * up_pre * (sigmoid_gate + silu_gate * (1.0 - sigmoid_gate))
            ).astype(jnp.bfloat16)
            acts[2, 0, span, :] = (d_act * silu_gate).astype(jnp.bfloat16)
            return carry

        lax.fori_loop(0, rows // row_block, row_step, 0)
        for target, choice in ((leave, 1 - side_ref[0]), (stay, side_ref[0])):
            for kind, source in ((0, normed_t), (1, normed_t), (2, cotan_t)):
                left_side = jnp.concatenate(
                    [
                        source[pl.ds(pl.multiple_of((2 * part + choice) * slab, 16), slab), :]
                        for part in range(ctx_parts)
                    ],
                    0,
                )
                term = plain(left_side, acts[(1, 2, 0)[kind], 0]).astype(jnp.bfloat16)
                for j in range(2):
                    target[kind, j] = term[:, j * hidden : (j + 1) * hidden]

    start = first_expert // 2

    def weight_block():
        return pl.BlockSpec((2, width, hidden), lambda pair, side: (pair + start, 0, 0))

    half_block = pl.BlockSpec((3, 2, width // 2, hidden), lambda pair, side: (0, pair, 0, 0))
    half_shape = jax.ShapeDtypeStruct((3, expert_total, width // 2, hidden), jnp.bfloat16)
    extra = [] if kept is None else [kept]
    return pl.pallas_call(
        kernel,
        grid_spec=pltpu.PrefetchScalarGridSpec(
            num_scalar_prefetch=1,
            grid=(expert_total // 2,),
            in_specs=[
                whole((rows, width)),
                whole((width, rows)),
                whole((rows, width)),
                whole((width, rows)),
                whole((rows, LANES)),
                weight_block(),
                weight_block(),
                weight_block(),
            ]
            + [pl.BlockSpec(memory_space=pl.ANY)] * len(extra),
            out_specs=[
                half_block,
                half_block,
                pl.BlockSpec(
                    (3, 1, rows, pair_width), lambda pair, side: (0, pair + start, 0, 0)
                ),
                whole((rows, LANES)),
            ],
        ),
        out_shape=[
            half_shape,
            half_shape,
            jax.ShapeDtypeStruct((3, experts // 2, rows, pair_width), jnp.bfloat16),
            jax.ShapeDtypeStruct((rows, LANES), jnp.float32),
        ],
        input_output_aliases={9: 2} if extra else {},
        name="expert_chunk",
        compiler_params=params(1),
    )(
        side,
        normed_rows,
        normed_turned,
        cotangent_rows,
        cotangent_turned,
        gate_table,
        w_gate,
        w_up,
        w_down,
        *extra,
    )


def expert_rows(kinds, weights, acts, d_gates, route_hot):
    unused, pairs, rows, pair_width = acts.shape
    experts, width, hidden = weights[0].shape
    step_pairs = 4
    total = len(kinds)
    gate_lanes = 0 if d_gates is None else LANES
    row_block = min(256, rows)

    def kernel(*refs):
        act_refs, weight_refs = refs[:total], refs[total : 2 * total]
        keep = refs[-1]
        out_ref = refs[-2]
        step = pl.program_id(0)
        right_side = jnp.concatenate(
            [ref[j] for ref in weight_refs for j in range(2 * step_pairs)], 1
        )

        def row_step(block, carry):
            span = pl.ds(pl.multiple_of(block * row_block, row_block), row_block)
            left_side = jnp.concatenate(
                [ref[0, j, span, :] for ref in act_refs for j in range(step_pairs)], 1
            )
            term = turned(left_side, right_side)

            @pl.when(step == 0)
            def _():
                keep[span, :] = term

            @pl.when((step > 0) & (step < pl.num_programs(0) - 1))
            def _():
                keep[span, :] += term

            @pl.when(step == pl.num_programs(0) - 1)
            def _():
                out_ref[span, :width] = (keep[span, :] + term).astype(jnp.bfloat16)
                if gate_lanes:
                    out_ref[span, width:] = (
                        refs[2 * total][span, :] * refs[2 * total + 1][span, :]
                    ).astype(jnp.bfloat16)

            return carry

        lax.fori_loop(0, rows // row_block, row_step, 0)

    def act_block(kind):
        return pl.BlockSpec((1, step_pairs, rows, pair_width), lambda i: (kind, i, 0, 0))

    extra = [] if d_gates is None else [d_gates, route_hot]
    return pl.pallas_call(
        kernel,
        grid=(pairs // step_pairs,),
        in_specs=[act_block(kind) for kind in kinds]
        + [pl.BlockSpec((2 * step_pairs, width, hidden), lambda i: (i, 0, 0))] * total
        + [whole((rows, LANES))] * len(extra),
        out_specs=whole((rows, width + gate_lanes)),
        out_shape=jax.ShapeDtypeStruct((rows, width + gate_lanes), jnp.bfloat16),
        scratch_shapes=[pltpu.VMEM((rows, width), jnp.float32)],
        name="expert_rows",
        compiler_params=params(1),
    )(*([acts] * total), *weights, *extra)


def middle_back(d_packed, probs, share_row, live_lanes, residual, cotangent_rows, gain_row, weight):
    tokens, width = residual.shape

    def kernel(
        packed,
        prob_ref,
        share_ref,
        live_ref,
        residual_ref,
        cotan_ref,
        gain_ref,
        weight_ref,
        d_residual,
        d_branch,
        d_logits,
        d_gain,
        d_groups,
    ):
        prob = prob_ref[...]
        live = live_ref[...]
        d_prob = packed[:, width:].astype(jnp.float32) + share_ref[...] * live
        logits = (prob * (d_prob - jnp.sum(prob * d_prob, -1, keepdims=True))).astype(jnp.bfloat16)
        d_logits[...] = logits
        d_normed = packed[:, :width].astype(jnp.float32) + turned(logits, weight_ref[:, width:])
        total = residual_ref[...]
        scale = rms_scale(total)
        unit = total * scale
        d_gain[...] = jnp.broadcast_to(jnp.sum(d_normed * unit, 0, keepdims=True), (8, width))
        d_unit = d_normed * gain_ref[...]
        d_total = cotan_ref[...].astype(jnp.float32) * live[:, :1] + scale * (
            d_unit - unit * jnp.mean(d_unit * unit, -1, keepdims=True)
        )
        d_residual[...] = d_total
        low = d_total.astype(jnp.bfloat16)
        d_branch[...] = low
        for j in range(KEY_VALUE_HEADS):
            d_groups[j] = turned(
                low, weight_ref[j * QUERY_GROUP : (j + 1) * QUERY_GROUP, :width]
            ).astype(jnp.bfloat16)

    inputs = (d_packed, probs, share_row, live_lanes, residual, cotangent_rows, gain_row, weight)
    out_shape = [
        jax.ShapeDtypeStruct((tokens, width), jnp.float32),
        jax.ShapeDtypeStruct((tokens, width), jnp.bfloat16),
        jax.ShapeDtypeStruct((tokens, LANES), jnp.bfloat16),
        jax.ShapeDtypeStruct((8, width), jnp.float32),
        jax.ShapeDtypeStruct((KEY_VALUE_HEADS, tokens, QUERY_GROUP), jnp.bfloat16),
    ]
    return pl.pallas_call(
        kernel,
        grid=(1,),
        in_specs=[whole(value.shape) for value in inputs],
        out_specs=[whole(value.shape) for value in out_shape],
        out_shape=out_shape,
        name="middle_back",
        compiler_params=params(1),
    )(*inputs)


def early_grads(attended, d_branch, normed, d_logits, d_gain, gain_lane):
    tokens, width = normed.shape
    block = width // 3

    def kernel(attended_ref, branch_ref, normed_ref, logits_ref, gain_ref, out_ref):
        out_ref[:, :width] = over_rows(attended_ref[...], branch_ref[...]).astype(jnp.bfloat16)
        side_term = over_rows(normed_ref[...], logits_ref[...])
        column = jnp.broadcast_to(gain_ref[:1, :], (LANES, block)).T
        lane = lax.broadcasted_iota(jnp.int32, (block, LANES), 1)
        out_ref[:, width:] = jnp.where(lane == gain_lane, column, side_term).astype(jnp.bfloat16)

    return pl.pallas_call(
        kernel,
        grid=(3,),
        in_specs=[
            pl.BlockSpec((tokens, block), lambda i: (0, i)),
            whole((tokens, width)),
            pl.BlockSpec((tokens, block), lambda i: (0, i)),
            whole((tokens, LANES)),
            pl.BlockSpec((8, block), lambda i: (0, i)),
        ],
        out_specs=pl.BlockSpec((block, width + LANES), lambda i: (i, 0)),
        out_shape=jax.ShapeDtypeStruct((width, width + LANES), jnp.bfloat16),
        name="early_grads",
        compiler_params=params(1),
    )(attended, d_branch, normed, d_logits, d_gain)


def project_back(d_fused, fused_weight, normed, rows_in, gain_row, d_residual):
    tokens, width = rows_in.shape
    step_width = 2 * FUSED_GROUP
    steps = KEY_VALUE_HEADS // 2

    def kernel(d_ref, weight, normed_ref, rows, gain, d_residual_ref, late, d_input, keep):
        step = pl.program_id(0)
        d_pair = jnp.concatenate([d_ref[0], d_ref[1]], 1)
        late[:, pl.ds(pl.multiple_of(step * step_width, LANES), step_width)] = over_rows(
            normed_ref[...], d_pair
        ).astype(jnp.bfloat16)
        term = turned(d_pair, weight[...])

        @pl.when(step == 0)
        def _():
            keep[...] = term

        @pl.when(step > 0)
        def _():
            keep[...] += term

        @pl.when(step == steps - 1)
        def _():
            values = rows[...].astype(jnp.float32)
            scale = rms_scale(values)
            unit = values * scale
            d_normed = keep[...]
            d_unit = d_normed * gain[...]
            d_input[...] = d_residual_ref[...] + scale * (
                d_unit - unit * jnp.mean(d_unit * unit, -1, keepdims=True)
            )
            d_gain = jnp.sum(d_normed * unit, 0, keepdims=True)
            late[:, FUSED_WIDTH:] = jnp.broadcast_to(d_gain, (LANES, width)).T.astype(jnp.bfloat16)

    return pl.pallas_call(
        kernel,
        grid=(steps,),
        in_specs=[
            pl.BlockSpec((2, tokens, FUSED_GROUP), lambda i: (i, 0, 0)),
            pl.BlockSpec((width, step_width), lambda i: (0, i)),
            whole((tokens, width)),
            whole((tokens, width)),
            whole((1, width)),
            whole((tokens, width)),
        ],
        out_specs=[whole((width, FUSED_WIDTH + LANES)), whole((tokens, width))],
        out_shape=[
            jax.ShapeDtypeStruct((width, FUSED_WIDTH + LANES), jnp.bfloat16),
            jax.ShapeDtypeStruct((tokens, width), jnp.float32),
        ],
        scratch_shapes=[pltpu.VMEM((tokens, width), jnp.float32)],
        name="project_back",
        compiler_params=params(1),
    )(d_fused, fused_weight, normed, rows_in, gain_row, d_residual)


def local(
    layer_input,
    gain_attn,
    w_query,
    key_projection_weight,
    value_projection_weight,
    w_out,
    gain_ffn,
    w_router,
    w_gate,
    w_up,
    w_down,
    routes,
    lengths,
    cotangent,
):
    ctx_parts = lax.axis_size("z")
    n_ctx = 2 * ctx_parts
    n_shard = 2 * lax.axis_size("x")
    ctx_side = lax.axis_index("y")
    ctx_pos = 2 * lax.axis_index("z") + ctx_side
    shard_pos = 2 * lax.axis_index("x") + lax.axis_index("k")
    local_sequences = layer_input.shape[0]
    half_rows = layer_input.shape[3]
    model_width = layer_input.shape[4]
    sequence_rows = 2 * half_rows
    tokens = local_sequences * sequence_rows
    seq_len = n_ctx * sequence_rows
    experts = w_gate.shape[0]
    top_k = routes.shape[4]
    gathered_rows = n_shard * tokens
    head_shares = n_ctx // KEY_VALUE_HEADS
    here_sequences = local_sequences // head_shares
    width_rows = gain_attn.shape[0]

    def fused_columns(query_part, key_part, value_part):
        rows = query_part.shape[0]
        return jnp.concatenate(
            [
                query_part.reshape(rows, KEY_VALUE_HEADS, QUERY_GROUP),
                key_part.reshape(rows, KEY_VALUE_HEADS, HEAD_DIM),
                value_part.reshape(rows, KEY_VALUE_HEADS, HEAD_DIM),
            ],
            -1,
        ).reshape(rows, FUSED_WIDTH)

    fused_weight = lax.all_gather(
        jnp.concatenate(
            [
                fused_columns(w_query, key_projection_weight, value_projection_weight),
                jnp.pad(gain_attn[:, None], ((0, 0), (0, LANES - 1))),
            ],
            1,
        ),
        SHARD,
        axis=0,
        tiled=True,
    )
    out_weight = lax.all_gather(
        jnp.concatenate(
            [
                w_out,
                w_router,
                gain_ffn[:, None],
                jnp.zeros((width_rows, LANES - experts - 1), jnp.bfloat16),
            ],
            1,
        ),
        SHARD,
        axis=0,
        tiled=True,
    )
    gain_one = fused_weight[:, FUSED_WIDTH].astype(jnp.float32)[None, :]
    gain_two = out_weight[:, model_width + experts].astype(jnp.float32)[None, :]
    router_matrix = out_weight[:, model_width : model_width + experts]

    slots = jnp.arange(seq_len, dtype=jnp.int32)
    slot_ctx, slot_row = slots // sequence_rows, slots % sequence_rows
    all_positions = (
        jnp.where(slot_row < half_rows, slot_ctx, 2 * n_ctx - 1 - slot_ctx) * half_rows
        + slot_row % half_rows
    )
    local_positions = lax.dynamic_slice_in_dim(all_positions, ctx_pos * sequence_rows, sequence_rows)
    seq_lengths = lax.dynamic_slice_in_dim(lengths, shard_pos * local_sequences, local_sequences)
    lengths_here = lax.dynamic_slice_in_dim(
        seq_lengths, (ctx_pos % head_shares) * here_sequences, here_sequences
    )
    live_rows = (local_positions[None, :] < seq_lengths[:, None]).reshape(tokens)
    live_lanes = jnp.broadcast_to(live_rows.astype(jnp.float32)[:, None], (tokens, LANES))
    live_group = (
        (local_positions[None, :] < lengths[:, None]).astype(jnp.float32).reshape(gathered_rows)
    )
    row_positions = jnp.broadcast_to(all_positions[:, None], (seq_len, LANES))
    column_positions = jnp.broadcast_to(all_positions[None, :], (8, seq_len))
    every_cos, every_sin = rope_tables(all_positions)
    own_cos, own_sin = rope_tables(local_positions)
    still = jnp.ones_like(own_cos)
    step_cos = jnp.tile(
        jnp.concatenate([own_cos] * (GROUP + 1) + [still], 1), (local_sequences, 2)
    )
    step_sin = jnp.tile(
        jnp.concatenate([own_sin] * (GROUP + 1) + [0.0 * still], 1), (local_sequences, 2)
    )
    pair_cos, pair_sin = jnp.tile(every_cos, (1, 2)), jnp.tile(every_sin, (1, 2))

    rows_in = layer_input.reshape(tokens, model_width)
    cotangent_rows = cotangent.reshape(tokens, model_width)
    d_moe = jnp.where(live_rows[:, None], cotangent_rows, jnp.bfloat16(0.0))
    d_moe_all = lax.all_gather(d_moe, SHARD, axis=0, tiled=True)
    d_moe_turned = d_moe_all.T

    def exchange(groups):
        return lax.all_to_all(groups, CTX, 0, 0, tiled=True)

    fused_own, first_normed = project_in(rows_in, gain_one, fused_weight, step_cos, step_sin)
    fused_rows = exchange(
        fused_own.reshape(n_ctx, here_sequences, sequence_rows, FUSED_GROUP)
    )
    attended_rows = attend(fused_rows, row_positions, column_positions, lengths_here)
    attended_groups = exchange(attended_rows).reshape(KEY_VALUE_HEADS, tokens, QUERY_GROUP)
    residual, second_normed, attended_low = project_out(
        attended_groups, rows_in, out_weight, gain_two
    )

    normed_all = lax.all_gather(second_normed, SHARD, axis=0, tiled=True)
    normed_turned = normed_all.T
    router_probs = jax.nn.softmax(plain(normed_all, router_matrix), axis=-1)
    route_hot = jnp.any(
        routes.reshape(gathered_rows, top_k, 1) == jnp.arange(experts, dtype=jnp.int32), axis=1
    ).astype(jnp.float32)
    lane_pad = ((0, 0), (0, LANES - experts))
    prob_table = jnp.pad(router_probs, lane_pad)
    hot_table = jnp.pad(route_hot, lane_pad)
    gate_table = prob_table * hot_table

    side = ctx_side.astype(jnp.int32).reshape(1)
    swap = [(0, 1), (1, 0)]
    acts, d_gates, reduced = None, None, []
    first_expert = 0
    for chunk in CHUNKS:
        stay, leave, acts, gate_piece = expert_chunk(
            first_expert,
            chunk,
            side,
            ctx_parts,
            normed_all,
            normed_turned,
            d_moe_all,
            d_moe_turned,
            gate_table,
            w_gate,
            w_up,
            w_down,
            acts,
        )
        first_expert += chunk
        d_gates = gate_piece if d_gates is None else d_gates + gate_piece
        arrived = lax.ppermute(leave, "y", swap)
        halved = (stay.astype(jnp.float32) + arrived.astype(jnp.float32)).astype(jnp.bfloat16)
        reduced.append(lax.psum_scatter(halved, "z", scatter_dimension=2, tiled=True))

    d_packed = expert_rows((1, 2), (w_gate, w_up), acts, d_gates, hot_table)
    d_packed_own = lax.psum_scatter(d_packed, SHARD, scatter_dimension=0, tiled=True)
    moe_rows = expert_rows((0,), (w_down,), acts, None, None)
    moe_own = lax.psum_scatter(moe_rows, SHARD, scatter_dimension=0, tiled=True)
    layer_output = (
        (residual + moe_own.astype(jnp.float32)).astype(jnp.bfloat16).reshape(layer_input.shape)
    )

    group_sums = jnp.stack(
        [jnp.sum(route_hot * live_group[:, None], 0), jnp.sum(router_probs * live_group[:, None], 0)]
    )
    all_sums = lax.psum(group_sums, CTX)
    live_all = jnp.sum(lengths).astype(jnp.float32)
    route_share = all_sums[0] / (top_k * live_all)
    aux_loss = experts * jnp.sum(route_share * all_sums[1] / live_all)
    share_row = jnp.pad((loss_weight * experts / live_all) * route_share[None, :], lane_pad)

    own_probs = lax.dynamic_slice_in_dim(prob_table, shard_pos * tokens, tokens, 0)
    d_residual, d_branch, d_logits, d_gain_two, d_groups = middle_back(
        d_packed_own,
        own_probs,
        share_row,
        live_lanes,
        residual,
        cotangent_rows,
        gain_two,
        out_weight,
    )
    d_attended = exchange(d_groups.reshape(n_ctx, here_sequences, sequence_rows, QUERY_GROUP))
    early_terms = early_grads(attended_low, d_branch, second_normed, d_logits, d_gain_two, experts)
    d_fused_rows = attend_back(
        fused_rows,
        d_attended,
        row_positions,
        column_positions,
        pair_cos,
        pair_sin,
        lengths_here,
    )
    d_fused = exchange(d_fused_rows).reshape(KEY_VALUE_HEADS, tokens, FUSED_GROUP)
    late_terms, grad_input = project_back(
        d_fused, fused_weight, first_normed, rows_in, gain_one, d_residual
    )
    early_rows = lax.psum_scatter(early_terms, EVERY, scatter_dimension=0, tiled=True)
    late_rows = lax.psum_scatter(late_terms, EVERY, scatter_dimension=0, tiled=True)
    early_rows, late_rows = early_rows.astype(jnp.float32), late_rows.astype(jnp.float32)
    late_groups = late_rows[:, :FUSED_WIDTH].reshape(-1, KEY_VALUE_HEADS, FUSED_GROUP)
    own_rows = late_rows.shape[0]
    grads = [
        jnp.concatenate([piece[kind] for piece in reduced], 0).astype(jnp.float32)
        for kind in range(3)
    ]
    return (
        layer_output,
        grad_input.reshape(layer_input.shape),
        late_rows[:, FUSED_WIDTH],
        late_groups[:, :, :QUERY_GROUP].reshape(own_rows, -1),
        late_groups[:, :, QUERY_GROUP : QUERY_GROUP + HEAD_DIM].reshape(own_rows, -1),
        late_groups[:, :, QUERY_GROUP + HEAD_DIM :].reshape(own_rows, -1),
        early_rows[:, :model_width],
        early_rows[:, model_width + experts],
        early_rows[:, model_width : model_width + experts],
        grads[0],
        grads[1],
        grads[2],
        aux_loss,
    )


def solution(mesh):
    n_ctx, n_shard = mesh.shape["ctx"], mesh.shape["fsdp"]
    fine = Mesh(mesh.devices.reshape(n_ctx // 2, 2, n_shard // 2, 2), EVERY)
    placed = (
        P(SHARD, CTX, None, None, None),
        P(SHARD),
        P(SHARD, None),
        P(SHARD, None),
        P(SHARD, None),
        P(SHARD, None),
        P(SHARD),
        P(SHARD, None),
        P(None, None, SHARD),
        P(None, None, SHARD),
        P(None, None, SHARD),
        P(None, CTX, None, None, None),
        P(),
        P(SHARD, CTX, None, None, None),
    )
    return jax.shard_map(
        local,
        mesh=fine,
        in_specs=placed,
        out_specs=(
            P(SHARD, CTX, None, None, None),
            P(SHARD, CTX, None, None, None),
            P(EVERY),
            P(EVERY, None),
            P(EVERY, None),
            P(EVERY, None),
            P(EVERY, None),
            P(EVERY),
            P(EVERY, None),
            P(None, CTX, SHARD),
            P(None, CTX, SHARD),
            P(None, CTX, SHARD),
            P(),
        ),
        check_vma=False,
    )
```

time: 2120 us -> 1330 us (0.63)
  waiting for transfers between devices: 1510 us -> 742 us
  local copies, waits for them, and re-layouts: 159 us -> 55.7 us
  blocking collectives: 38.9 us -> 127 us
  matrix products: 76.2 us -> 2.77 us
  Pallas kernels: 231 us -> 304 us
  other arithmetic: 80.4 us -> 57.5 us
    reduce_scatter x16 -> x9, waiting for transfers between devices: 1070 us -> 108 us  [the longest x1 108 us: local(): lax.psum_scatter(late_terms, EVERY, scatter_dimension=0, tiled=True)]
    ppermute x0 -> x5, waiting for transfers between devices: none -> 493 us  [local(): arrived = lax.ppermute(leave, 'y', swap)]
    unnamed x28 -> x13, waiting for transfers between devices: 245 us -> 0.21 us
    all_gather x8 -> x4, waiting for transfers between devices: 190 us -> 73.1 us  [the longest x1 52.8 us: local(): lax.all_gather(jnp.concatenate([fused_columns(w_query, key_projection_wei...]
    all_to_all x0 -> x2, blocking collectives: none -> 106 us  [exchange(): return lax.all_to_all(groups, CTX, 0, 0, tiled=True)]
    dot_general x21 -> x1, matrix products: 76.2 us -> 2.77 us  [plain(): return jnp.dot(left_side, right_side, preferred_element_type=jnp.float32)]
    pallas_call x4 -> x14, Pallas kernels: 231 us -> 304 us  [the longest x5 156 us: expert_chunk(): pl.pallas_call(kernel, grid_spec=pltpu.PrefetchScalarGridSpec(num_scalar_...]
    all_to_all x0 -> x2, waiting for transfers between devices: none -> 67.3 us  [exchange(): return lax.all_to_all(groups, CTX, 0, 0, tiled=True)]
  transfers between devices with their start and end apart: 26 -> 20, of which waited for: 24 -> 10; matrix products, arithmetic and copies ran while one was open for 11% -> 6% of each run, Pallas kernels for 0% -> 8%
where the time goes in v2:
time: 1330 us
  waiting for transfers between devices  742 us (56%)
  Pallas kernels  304 us (23%)
  blocking collectives  127 us (10%)
  other arithmetic  57.5 us (4%)
  local copies, waits for them, and re-layouts  55.7 us (4%)
  starting transfers between devices  19.6 us (1%)
  between operations  17.5 us (1%)
    ppermute x5, waiting for transfers between devices, local(): arrived = lax.ppermute(leave, 'y', swap)  493 us
    pallas_call x5, Pallas kernels, expert_chunk(): pl.pallas_call(kernel, grid_spec=pltpu.PrefetchScalarGridSpec(num_scalar_...  156 us
    reduce_scatter x1, waiting for transfers between devices, local(): lax.psum_scatter(late_terms, EVERY, scatter_dimension=0, tiled=True)  108 us
    all_to_all x2, blocking collectives, exchange(): return lax.all_to_all(groups, CTX, 0, 0, tiled=True)  106 us
    pallas_call x2, Pallas kernels, expert_rows(): pl.pallas_call(kernel, grid=(pairs // step_pairs,), in_specs=[act_block(k...  76.3 us
    all_to_all x2, waiting for transfers between devices, exchange(): return lax.all_to_all(groups, CTX, 0, 0, tiled=True)  67.3 us
    all_gather x1, waiting for transfers between devices, local(): lax.all_gather(jnp.concatenate([fused_columns(w_query, key_projection_wei...  52.8 us
    convert_element_type x5, other arithmetic, local(): (stay.astype(jnp.float32) + arrived.astype(jnp.float32)).astype(jnp.bfloa...  30.1 us
  transfers between devices with their start and end apart: 20, of which 10 were waited for; matrix products, arithmetic and copies ran while one was open for 6% of the time, Pallas kernels for 8%

profile of v2, /device:TPU:0, one launch (start us, length us, event | category | flops | bytes accessed | tf_op | source)
XLA Modules:
  0.0 1325.7 jit_solution(4015124823111136991)
XLA Ops:
  27.9 52.8 %all-gather.5.cloned.1.call-done.weight = bf16[1536,2688]{1,0:T(8,128)(2,1)} async-done(((bf16[384,2688]{1,0:T(8,128)(2,1)}), bf16[1536,2688]{1,0:T(8,128)(2,1)}) %all-gather.5.cloned.1.call-update) | async-done | bytes 8257552 | tf_op jit(solution)/shard_map/all_gather | solution.py:706
  90.7 42.9 %all_to_all.20.query_ref.key_ref = bf16[8,4,64,320]{3,2,1,0:T(8,128)(2,1)} all-to-all(bf16[8,4,64,320]{3,2,1,0:T(8,128)(2,1)} %bitcast.101), channel_id=1, replica_groups=mesh['z'=4,'y'=2,'x'=2,'k'=2] {'z','y'}, dimensions={0} | all-to-all | bytes 2621440 | tf_op jit(solution)/shard_map/all_to_all | solution.py:772
  135.1 11.7 attend.1
  152.4 23.8 %all-to-all-done.1 = bf16[8,4,64,192]{3,2,1,0:T(8,128)(2,1)S(1)} async-done(((bf16[8,4,64,192]{3,2,1,0:T(8,128)(2,1)}), bf16[8,4,64,192]{3,2,1,0:T(8,128)(2,1)S(1)}, u32[]{:S(2)}, u32[]{:S(2)}) %all-to-all-start.1) | async-done | bytes 786464 | tf_op jit(solution)/shard_map/all_to_all | solution.py:772
  192.5 20.3 %all-gather.9.cloned.1.call-done = bf16[1024,1536]{0,1:T(8,128)(2,1)} async-done(((bf16[256,1536]{0,1:T(8,128)(2,1)}), bf16[1024,1536]{0,1:T(8,128)(2,1)}) %all-gather.9.cloned.1.call-update) | async-done | bytes 3145744 | tf_op jit(solution)/shard_map/all_gather | solution.py:784
  224.6 31.1 %expert_chunk.5 = (bf16[3,8,768,128]{3,2,1,0:T(8,128)(2,1)}, bf16[3,8,768,128]{3,2,1,0:T(8,128)(2,1)}, bf16[3,20,1024,256]{3,2,1,0:T(8,128)(2,1)}, f32[1024,128]{1,0:T(8,128)}) custom-call(s32[1]{0:T(128)} %bitcast.7.side_ref, bf16[1024,1536]{1,0:T(8,128)(2,1)} %copy.120.normed, bf16[1536,1024]{1,0:T(8,128)(2,1)} %bitcast.87, ...), custom_call_target="tpu_custom_call" | custom-call | tf_op jit(solution)/shard_map/expert_chunk/pallas_call | solution.py:407
  255.7 31.3 %expert_chunk.6 = (bf16[3,8,768,128]{3,2,1,0:T(8,128)(2,1)}, bf16[3,8,768,128]{3,2,1,0:T(8,128)(2,1)}, bf16[3,20,1024,256]{3,2,1,0:T(8,128)(2,1)}, f32[1024,128]{1,0:T(8,128)}) custom-call(s32[1]{0:T(128)} %bitcast.7.side_ref, bf16[1024,1536]{1,0:T(8,128)(2,1)} %copy.120.normed, bf16[1536,1024]{1,0:T(8,128)(2,1)} %bitcast.88, ...), custom_call_target="tpu_custom_call", output_to_operand_aliasing={{2}: (9, {})} | custom-call | tf_op jit(solution)/shard_map/expert_chunk/pallas_call | solution.py:407
  287.0 31.4 %expert_chunk.7 = (bf16[3,8,768,128]{3,2,1,0:T(8,128)(2,1)}, bf16[3,8,768,128]{3,2,1,0:T(8,128)(2,1)}, bf16[3,20,1024,256]{3,2,1,0:T(8,128)(2,1)}, f32[1024,128]{1,0:T(8,128)}) custom-call(s32[1]{0:T(128)} %bitcast.7.side_ref, bf16[1024,1536]{1,0:T(8,128)(2,1)} %copy.120.normed, bf16[1536,1024]{1,0:T(8,128)(2,1)} %bitcast.89, ...), custom_call_target="tpu_custom_call", output_to_operand_aliasing={{2}: (9, {})} | custom-call | tf_op jit(solution)/shard_map/expert_chunk/pallas_call | solution.py:407
  318.4 31.1 %expert_chunk.8 = (bf16[3,8,768,128]{3,2,1,0:T(8,128)(2,1)}, bf16[3,8,768,128]{3,2,1,0:T(8,128)(2,1)}, bf16[3,20,1024,256]{3,2,1,0:T(8,128)(2,1)}, f32[1024,128]{1,0:T(8,128)}) custom-call(s32[1]{0:T(128)} %bitcast.7.side_ref, bf16[1024,1536]{1,0:T(8,128)(2,1)} %copy.120.normed, bf16[1536,1024]{1,0:T(8,128)(2,1)} %bitcast.90, ...), custom_call_target="tpu_custom_call", output_to_operand_aliasing={{2}: (9, {})} | custom-call | tf_op jit(solution)/shard_map/expert_chunk/pallas_call | solution.py:407
  349.6 31.3 %expert_chunk.9 = (bf16[3,8,768,128]{3,2,1,0:T(8,128)(2,1)}, bf16[3,8,768,128]{3,2,1,0:T(8,128)(2,1)}, bf16[3,20,1024,256]{3,2,1,0:T(8,128)(2,1)}, f32[1024,128]{1,0:T(8,128)}) custom-call(s32[1]{0:T(128)} %bitcast.7.side_ref, bf16[1024,1536]{1,0:T(8,128)(2,1)} %copy.120.normed, bf16[1536,1024]{1,0:T(8,128)(2,1)} %bitcast.91, ...), custom_call_target="tpu_custom_call", output_to_operand_aliasing={{2}: (9, {})} | custom-call | tf_op jit(solution)/shard_map/expert_chunk/pallas_call | solution.py:407
  382.9 48.1 %expert_rows.3 = bf16[1024,1664]{1,0:T(8,128)(2,1)} custom-call(bf16[3,20,1024,256]{3,2,1,0:T(8,128)(2,1)} %get-tuple-element.52.refs_0_.refs_1_, bf16[3,20,1024,256]{3,2,1,0:T(8,128)(2,1)} %get-tuple-element.52.refs_0_.refs_1_, bf16[40,1536,128]{2,1,0:T(8,128)(2,1)} %refs_2_.1, bf16[40,1536,128]{2,1,0:T(8,128)(2,1)} %refs_3_.1, ...), custom_call_target="tpu_custom_call" | custom-call | tf_op jit(solution)/shard_map/expert_rows/pallas_call | solution.py:503
  431.0 28.2 %expert_rows.2 = bf16[1024,1536]{1,0:T(8,128)(2,1)} custom-call(bf16[3,20,1024,256]{3,2,1,0:T(8,128)(2,1)} %get-tuple-element.52.refs_0_.refs_1_, bf16[40,1536,128]{2,1,0:T(8,128)(2,1)} %refs_1_.1), custom_call_target="tpu_custom_call" | custom-call | tf_op jit(solution)/shard_map/expert_rows/pallas_call | solution.py:503
  461.2 21.4 %psum.7 = f32[2,40]{1,0:T(2,128)S(1)} all-reduce(f32[2,40]{1,0:T(2,128)S(1)} %pad_maximum_fusion.3), channel_id=1, replica_groups=mesh['z'=4,'y'=2,'x'=2,'k'=2] {'z','y'}, use_global_device_ids=true, to_apply=%region_8.9 | all-reduce | flops 80 | bytes 640 | tf_op jit(solution)/shard_map/psum | solution.py:832
  498.0 114.7 %collective-permute-done = bf16[3,8,768,128]{3,2,1,0:T(8,128)(2,1)S(1)} collective-permute-done((bf16[3,8,768,128]{3,2,1,0:T(8,128)(2,1)}, bf16[3,8,768,128]{3,2,1,0:T(8,128)(2,1)S(1)}, u32[]{:S(2)}, u32[]{:S(2)}) %collective-permute-start) | collective-permute-done | bytes 4718624 | tf_op jit(solution)/shard_map/ppermute | solution.py:817
  619.2 96.8 %collective-permute-done.1 = bf16[3,8,768,128]{3,2,1,0:T(8,128)(2,1)S(1)} collective-permute-done((bf16[3,8,768,128]{3,2,1,0:T(8,128)(2,1)}, bf16[3,8,768,128]{3,2,1,0:T(8,128)(2,1)S(1)}, u32[]{:S(2)}, u32[]{:S(2)}) %collective-permute-start.1) | collective-permute-done | bytes 4718624 | tf_op jit(solution)/shard_map/ppermute | solution.py:817
  723.0 94.4 %collective-permute-done.2 = bf16[3,8,768,128]{3,2,1,0:T(8,128)(2,1)S(1)} collective-permute-done((bf16[3,8,768,128]{3,2,1,0:T(8,128)(2,1)}, bf16[3,8,768,128]{3,2,1,0:T(8,128)(2,1)S(1)}, u32[]{:S(2)}, u32[]{:S(2)}) %collective-permute-start.2) | collective-permute-done | bytes 4718624 | tf_op jit(solution)/shard_map/ppermute | solution.py:817
  825.0 94.5 %collective-permute-done.3 = bf16[3,8,768,128]{3,2,1,0:T(8,128)(2,1)S(1)} collective-permute-done((bf16[3,8,768,128]{3,2,1,0:T(8,128)(2,1)}, bf16[3,8,768,128]{3,2,1,0:T(8,128)(2,1)S(1)}, u32[]{:S(2)}, u32[]{:S(2)}) %collective-permute-start.3) | collective-permute-done | bytes 4718624 | tf_op jit(solution)/shard_map/ppermute | solution.py:817
  927.0 92.5 %collective-permute-done.4 = bf16[3,8,768,128]{3,2,1,0:T(8,128)(2,1)S(1)} collective-permute-done((bf16[3,8,768,128]{3,2,1,0:T(8,128)(2,1)}, bf16[3,8,768,128]{3,2,1,0:T(8,128)(2,1)S(1)}, u32[]{:S(2)}, u32[]{:S(2)}) %collective-permute-start.4) | collective-permute-done | bytes 4718624 | tf_op jit(solution)/shard_map/ppermute | solution.py:817
  1025.4 10.6 all-to-all-start.2
  1038.2 43.5 %all-to-all-done.2.d_ref = bf16[8,4,64,192]{3,2,1,0:T(8,128)(2,1)S(1)} async-done(((bf16[8,4,64,192]{3,2,1,0:T(8,128)(2,1)}), bf16[8,4,64,192]{3,2,1,0:T(8,128)(2,1)S(1)}, u32[]{:S(2)}, u32[]{:S(2)}) %all-to-all-start.2) | async-done | bytes 786464 | tf_op jit(solution)/shard_map/all_to_all | solution.py:772
  1082.7 18.7 %attend_back.1 = bf16[8,4,64,320]{3,2,1,0:T(8,128)(2,1)} custom-call(s32[4]{0:T(128)} %copy-done.22, bf16[8,4,64,320]{3,2,1,0:T(8,128)(2,1)} %all_to_all.20.query_ref.key_ref, bf16[8,4,64,320]{3,2,1,0:T(8,128)(2,1)} %all_to_all.20.query_ref.key_ref, bf16[8,4,64,192]{3,2,1,0:T(8,128)(2,1)} %copy-done.4, s32[512,128]{1,0:T(8,128)} %broadcast_in_dim.28.row_ref, ...), custom_call_target="tpu_custom_call" | custom-call | tf_op jit(solution)/shard_map/attend_back/pallas_call | solution.py:230
  1101.4 62.9 %all_to_all.21 = bf16[8,4,64,320]{3,2,1,0:T(8,128)(2,1)} all-to-all(bf16[8,4,64,320]{3,2,1,0:T(8,128)(2,1)} %attend_back.1), channel_id=1, replica_groups=mesh['z'=4,'y'=2,'x'=2,'k'=2] {'z','y'}, dimensions={0} | all-to-all | bytes 2621440 | tf_op jit(solution)/shard_map/all_to_all | solution.py:772
  1164.3 13.9 %project_back.1 = (bf16[1536,2688]{1,0:T(8,128)(2,1)}, f32[256,1536]{1,0:T(8,128)}) custom-call(bf16[8,256,320]{2,1,0:T(8,128)(2,1)} %bitcast.97, bf16[1536,2688]{1,0:T(8,128)(2,1)} %all-gather.5.cloned.1.call-done.weight, bf16[256,1536]{1,0:T(8,128)(2,1)} %get-tuple-element.59.normed_ref, bf16[256,1536]{1,0:T(8,128)(2,1)} %bitcast.96, ...), custom_call_target="tpu_custom_call" | custom-call | tf_op jit(solution)/shard_map/project_back/pallas_call | solution.py:638
  1205.0 108.2 %reduce-scatter.14.cloned.1.call-done = bf16[48,2688]{1,0:T(8,128)(2,1)} async-done(((bf16[1536,2688]{1,0:T(8,128)(2,1)}), bf16[48,2688]{1,0:T(8,128)(2,1)}) %reduce-scatter.14.cloned.1.call-update) | async-done | bytes 258064 | tf_op jit(solution)/shard_map/reduce_scatter | solution.py:865
  (194 shorter events, 152.2 us)
Async XLA Ops:
  7.2 73.5 %all-gather.5.cloned.1.call-start = ((), (), s32[]{:S(2)}) async-start(), calls=%async_computation.13 | async-start | bytes 10321920 | tf_op jit(solution)/shard_map/all_gather | solution.py:706
  20.2 130.2 %all-gather.7.cloned.1.call-start = ((), (), s32[]{:S(2)}) async-start(), calls=%async_computation.14 | async-start | bytes 6389760 | tf_op jit(solution)/shard_map/all_gather | solution.py:718
  22.4 165.3 %all-gather.11.cloned.1.call-start = ((), (), s32[]{:S(2)}) async-start(), calls=%async_computation.16 | async-start | bytes 3932160 | tf_op jit(solution)/shard_map/all_gather | solution.py:768
  146.8 29.4 %all-to-all-start.1 = ((bf16[8,4,64,192]{3,2,1,0:T(8,128)(2,1)}), bf16[8,4,64,192]{3,2,1,0:T(8,128)(2,1)S(1)}, u32[]{:S(2)}, u32[]{:S(2)}) async-start(bf16[8,4,64,192]{3,2,1,0:T(8,128)(2,1)} %attend.1), calls=%async_computation.1 | async-start | bytes 2097152 | tf_op jit(solution)/shard_map/all_to_all | solution.py:772
  150.4 62.4 %all-gather.9.cloned.1.call-start = ((), (), s32[]{:S(2)}) async-start(), calls=%async_computation.15 | async-start | bytes 3932160 | tf_op jit(solution)/shard_map/all_gather | solution.py:784
  185.5 298.9 %reduce-scatter.12.cloned.1.call-start = ((), (), s32[]{:S(2)}) async-start(), calls=%async_computation.18 | async-start | bytes 4259840 | tf_op jit(solution)/shard_map/reduce_scatter | solution.py:822
  349.6 31.3 %copy-start.11 = (f32[1024,128]{1,0:T(8,128)S(1)}, f32[1024,128]{1,0:T(8,128)}, u32[]{:S(2)}) copy-start(f32[1024,128]{1,0:T(8,128)} %get-tuple-element.53) | copy-start | bytes 1572868
  349.6 31.3 %copy-start.12 = (f32[1024,128]{1,0:T(8,128)S(1)}, f32[1024,128]{1,0:T(8,128)}, u32[]{:S(2)}) copy-start(f32[1024,128]{1,0:T(8,128)} %get-tuple-element.54) | copy-start | bytes 1572868
  349.6 31.3 %copy-start.13 = (f32[1024,128]{1,0:T(8,128)S(1)}, f32[1024,128]{1,0:T(8,128)}, u32[]{:S(2)}) copy-start(f32[1024,128]{1,0:T(8,128)} %get-tuple-element.55) | copy-start | bytes 1572868
  349.6 31.3 %copy-start.14 = (f32[1024,128]{1,0:T(8,128)S(1)}, f32[1024,128]{1,0:T(8,128)}, u32[]{:S(2)}) copy-start(f32[1024,128]{1,0:T(8,128)} %get-tuple-element.56) | copy-start | bytes 1572868
  431.0 748.1 %reduce-scatter.10.cloned.1.call-start = ((), (), s32[]{:S(2)}) async-start(), calls=%async_computation.17 | async-start | bytes 3932160 | tf_op jit(solution)/shard_map/reduce_scatter | solution.py:824
  459.3 722.6 %reduce-scatter.16.cloned.1.call-start = ((), (), s32[]{:S(2)}) async-start(), calls=%async_computation.20 | async-start | bytes 5271552 | tf_op jit(solution)/shard_map/reduce_scatter | solution.py:864
  497.9 688.6 %reduce-scatter.18.cloned.1.call-start = ((), (), s32[]{:S(2)}) async-start(), calls=%async_computation.21 | async-start | bytes 5898240 | tf_op jit(solution)/shard_map/reduce_scatter | solution.py:819
  497.9 114.8 %collective-permute-start = (bf16[3,8,768,128]{3,2,1,0:T(8,128)(2,1)}, bf16[3,8,768,128]{3,2,1,0:T(8,128)(2,1)S(1)}, u32[]{:S(2)}, u32[]{:S(2)}) collective-permute-start(bf16[3,8,768,128]{3,2,1,0:T(8,128)(2,1)} %get-tuple-element.68), channel_id=1, source_target_pairs={{0,4},{4,0},{1,5},{5,1},{2,6},{6,2},{3,7},{7,3},{8,12},{12,8},{9,1... | collective-permute-start | bytes 14155784 | tf_op jit(solution)/shard_map/ppermute | solution.py:817
  618.8 570.1 %reduce-scatter.20.cloned.1.call-start = ((), (), s32[]{:S(2)}) async-start(), calls=%async_computation.22 | async-start | bytes 5898240 | tf_op jit(solution)/shard_map/reduce_scatter | solution.py:819
  618.8 97.1 %collective-permute-start.1 = (bf16[3,8,768,128]{3,2,1,0:T(8,128)(2,1)}, bf16[3,8,768,128]{3,2,1,0:T(8,128)(2,1)S(1)}, u32[]{:S(2)}, u32[]{:S(2)}) collective-permute-start(bf16[3,8,768,128]{3,2,1,0:T(8,128)(2,1)} %get-tuple-element.70), channel_id=1, source_target_pairs={{0,4},{4,0},{1,5},{5,1},{2,6},{6,2},{3,7},{7,3},{8,12},{12,8},{9,1... | collective-permute-start | bytes 14155784 | tf_op jit(solution)/shard_map/ppermute | solution.py:817
  722.1 469.0 %reduce-scatter.22.cloned.1.call-start = ((), (), s32[]{:S(2)}) async-start(), calls=%async_computation.23 | async-start | bytes 5898240 | tf_op jit(solution)/shard_map/reduce_scatter | solution.py:819
  722.1 95.3 %collective-permute-start.2 = (bf16[3,8,768,128]{3,2,1,0:T(8,128)(2,1)}, bf16[3,8,768,128]{3,2,1,0:T(8,128)(2,1)S(1)}, u32[]{:S(2)}, u32[]{:S(2)}) collective-permute-start(bf16[3,8,768,128]{3,2,1,0:T(8,128)(2,1)} %get-tuple-element.72), channel_id=1, source_target_pairs={{0,4},{4,0},{1,5},{5,1},{2,6},{6,2},{3,7},{7,3},{8,12},{12,8},{9,1... | collective-permute-start | bytes 14155784 | tf_op jit(solution)/shard_map/ppermute | solution.py:817
  823.5 369.9 %reduce-scatter.24.cloned.1.call-start = ((), (), s32[]{:S(2)}) async-start(), calls=%async_computation.24 | async-start | bytes 5898240 | tf_op jit(solution)/shard_map/reduce_scatter | solution.py:819
  823.8 95.7 %collective-permute-start.3 = (bf16[3,8,768,128]{3,2,1,0:T(8,128)(2,1)}, bf16[3,8,768,128]{3,2,1,0:T(8,128)(2,1)S(1)}, u32[]{:S(2)}, u32[]{:S(2)}) collective-permute-start(bf16[3,8,768,128]{3,2,1,0:T(8,128)(2,1)} %get-tuple-element.74), channel_id=1, source_target_pairs={{0,4},{4,0},{1,5},{5,1},{2,6},{6,2},{3,7},{7,3},{8,12},{12,8},{9,1... | collective-permute-start | bytes 14155784 | tf_op jit(solution)/shard_map/ppermute | solution.py:817
  925.5 270.1 %reduce-scatter.26.cloned.1.call-start = ((), (), s32[]{:S(2)}) async-start(), calls=%async_computation.25 | async-start | bytes 5898240 | tf_op jit(solution)/shard_map/reduce_scatter | solution.py:819
  925.5 93.9 %collective-permute-start.4 = (bf16[3,8,768,128]{3,2,1,0:T(8,128)(2,1)}, bf16[3,8,768,128]{3,2,1,0:T(8,128)(2,1)S(1)}, u32[]{:S(2)}, u32[]{:S(2)}) collective-permute-start(bf16[3,8,768,128]{3,2,1,0:T(8,128)(2,1)} %get-tuple-element.76), channel_id=1, source_target_pairs={{0,4},{4,0},{1,5},{5,1},{2,6},{6,2},{3,7},{7,3},{8,12},{12,8},{9,1... | collective-permute-start | bytes 14155784 | tf_op jit(solution)/shard_map/ppermute | solution.py:817
  1025.4 56.2 %all-to-all-start.2 = ((bf16[8,4,64,192]{3,2,1,0:T(8,128)(2,1)}), bf16[8,4,64,192]{3,2,1,0:T(8,128)(2,1)S(1)}, u32[]{:S(2)}, u32[]{:S(2)}) async-start(bf16[8,4,64,192]{3,2,1,0:T(8,128)(2,1)} %bitcast.15), calls=%async_computation.4 | async-start | bytes 2097152 | tf_op jit(solution)/shard_map/all_to_all | solution.py:772
  1036.0 277.1 %reduce-scatter.14.cloned.1.call-start = ((), (), s32[]{:S(2)}) async-start(), calls=%async_computation.19 | async-start | bytes 8515584 | tf_op jit(solution)/shard_map/reduce_scatter | solution.py:865
  (24 other events, 92.2 us)
Sparse Core Ops, SparseCore 0:
  20.4 60.2 all-gather.4
  82.8 39.6 all-gather.6
  124.0 28.4 all-gather.10
  185.6 27.0 all-gather.8
  431.1 39.5 reduce-scatter.11
  473.6 37.8 reduce-scatter.9
  517.1 119.4 reduce-scatter.15
  638.9 84.3 reduce-scatter.17
  725.6 85.7 reduce-scatter.19
  823.6 84.7 reduce-scatter.21
  925.6 88.9 reduce-scatter.23
  1025.6 123.1 reduce-scatter.25
  1178.4 134.7 reduce-scatter.13

commit v3 on v2

--- a/solution.py
+++ b/solution.py
@@ -5,6 +5,7 @@
 from jax.experimental.pallas import tpu as pltpu
 from jax.sharding import Mesh
 from jax.sharding import PartitionSpec as P
+
 
 QUERY_HEADS = 24
 KEY_VALUE_HEADS = 8
@@ -79,30 +80,47 @@
 
 def project_in(rows_in, gain_row, fused_weight, cosine, sine_part):
     tokens, width = rows_in.shape
-    step_width = 2 * FUSED_GROUP
-
-    def kernel(rows, gain, weight, cos_ref, sin_ref, fused, normed):
+    query_step, head_step = 2 * QUERY_GROUP, 2 * HEAD_DIM
+    rotated_width = query_step + head_step
+
+    def kernel(rows, gain, query_w, key_w, value_w, cos_ref, sin_ref, fused, normed):
         @pl.when(pl.program_id(0) == 0)
         def _():
             values = rows[...].astype(jnp.float32)
             normed[...] = (values * rms_scale(values) * gain[...]).astype(jnp.bfloat16)
 
-        product = plain(normed[...], weight[...])
-        rotated = (product * cos_ref[...] + swapped_halves(product) * sin_ref[...]).astype(
+        product = plain(
+            normed[...], jnp.concatenate([query_w[...], key_w[...], value_w[...]], 1)
+        )
+        turning = product[:, :rotated_width]
+        rotated = (turning * cos_ref[...] + swapped_halves(turning) * sin_ref[...]).astype(
             jnp.bfloat16
         )
-        fused[0] = rotated[:, :FUSED_GROUP]
-        fused[1] = rotated[:, FUSED_GROUP:]
-
+        values_low = product[:, rotated_width:].astype(jnp.bfloat16)
+        for j in range(2):
+            lanes = slice(j * HEAD_DIM, (j + 1) * HEAD_DIM)
+            fused[j] = jnp.concatenate(
+                [
+                    rotated[:, j * QUERY_GROUP : (j + 1) * QUERY_GROUP],
+                    rotated[:, query_step:][:, lanes],
+                    values_low[:, lanes],
+                ],
+                1,
+            )
+
+    key_start = KEY_VALUE_HEADS * QUERY_GROUP // head_step
+    value_start = key_start + KEY_VALUE_HEADS // 2
     return pl.pallas_call(
         kernel,
         grid=(KEY_VALUE_HEADS // 2,),
         in_specs=[
             whole((tokens, width)),
             whole((1, width)),
-            pl.BlockSpec((width, step_width), lambda i: (0, i)),
-            whole((tokens, step_width)),
-            whole((tokens, step_width)),
+            pl.BlockSpec((width, query_step), lambda i: (0, i)),
+            pl.BlockSpec((width, head_step), lambda i: (0, key_start + i)),
+            pl.BlockSpec((width, head_step), lambda i: (0, value_start + i)),
+            whole((tokens, rotated_width)),
+            whole((tokens, rotated_width)),
         ],
         out_specs=[
             pl.BlockSpec((2, tokens, FUSED_GROUP), lambda i: (i, 0, 0)),
@@ -114,7 +132,7 @@
         ],
         name="project_in",
         compiler_params=params(1),
-    )(rows_in, gain_row, fused_weight, cosine, sine_part)
+    )(rows_in, gain_row, fused_weight, fused_weight, fused_weight, cosine, sine_part)
 
 
 def head_probs(query_head, key_rows, visible):
@@ -124,7 +142,7 @@
 
 
 def attend(fused_rows, row_positions, column_positions, lengths_here):
-    n_ctx, sequences, span, unused = fused_rows.shape
+    n_ctx, sequences, span, _ = fused_rows.shape
     seq_len = n_ctx * span
     blocks = max(1, min(n_ctx, 512 * 512 // seq_len // span))
     tile = blocks * span
@@ -165,11 +183,10 @@
 def attend_back(
     fused_rows, d_attended, row_positions, column_positions, cosine, sine_part, lengths_here
 ):
-    n_ctx, sequences, span, unused = fused_rows.shape
+    n_ctx, sequences, span, _ = fused_rows.shape
     seq_len = n_ctx * span
     blocks = max(1, min(n_ctx, 512 * 512 // seq_len // span))
     tile = blocks * span
-    padded = FUSED_GROUP + HEAD_DIM
 
     def kernel(
         lengths_ref,
@@ -311,9 +328,10 @@
     w_up,
     w_down,
     kept,
+    halves,
 ):
     rows, width = normed_rows.shape
-    experts, unused, hidden = w_gate.shape
+    experts, _, hidden = w_gate.shape
     pair_width = 2 * hidden
     slab = width // (2 * ctx_parts)
     row_block = min(ROW_BLOCK, rows)
@@ -330,7 +348,7 @@
         down_w,
         *rest,
     ):
-        stay, leave, acts, d_gates = rest[-4:]
+        grads, acts, d_gates = rest[-4 + (not halves) : -2], rest[-2], rest[-1]
         first = first_expert + 2 * pl.program_id(0)
 
         @pl.when(pl.program_id(0) == 0)
@@ -383,26 +401,37 @@
             return carry
 
         lax.fori_loop(0, rows // row_block, row_step, 0)
-        for target, choice in ((leave, 1 - side_ref[0]), (stay, side_ref[0])):
+        for turn in range(2):
+            choice = side_ref[0] if turn else 1 - side_ref[0]
             for kind, source in ((0, normed_t), (1, normed_t), (2, cotan_t)):
-                left_side = jnp.concatenate(
-                    [
-                        source[pl.ds(pl.multiple_of((2 * part + choice) * slab, 16), slab), :]
-                        for part in range(ctx_parts)
-                    ],
-                    0,
-                )
+                if halves:
+                    left_side = jnp.concatenate(
+                        [
+                            source[pl.ds(pl.multiple_of((2 * part + choice) * slab, 16), slab), :]
+                            for part in range(ctx_parts)
+                        ],
+                        0,
+                    )
+                    target, base = grads[1 - turn], 0
+                else:
+                    base = turn * (width // 2)
+                    left_side = source[base : base + width // 2, :]
+                    target = grads[0]
                 term = plain(left_side, acts[(1, 2, 0)[kind], 0]).astype(jnp.bfloat16)
                 for j in range(2):
-                    target[kind, j] = term[:, j * hidden : (j + 1) * hidden]
+                    target[kind, j, base : base + width // 2, :] = term[
+                        :, j * hidden : (j + 1) * hidden
+                    ]
 
     start = first_expert // 2
 
     def weight_block():
         return pl.BlockSpec((2, width, hidden), lambda pair, side: (pair + start, 0, 0))
 
-    half_block = pl.BlockSpec((3, 2, width // 2, hidden), lambda pair, side: (0, pair, 0, 0))
-    half_shape = jax.ShapeDtypeStruct((3, expert_total, width // 2, hidden), jnp.bfloat16)
+    grad_count = 2 if halves else 1
+    grad_width = width // grad_count
+    grad_block = pl.BlockSpec((3, 2, grad_width, hidden), lambda pair, side: (0, pair, 0, 0))
+    grad_shape = jax.ShapeDtypeStruct((3, expert_total, grad_width, hidden), jnp.bfloat16)
     extra = [] if kept is None else [kept]
     return pl.pallas_call(
         kernel,
@@ -420,22 +449,20 @@
                 weight_block(),
             ]
             + [pl.BlockSpec(memory_space=pl.ANY)] * len(extra),
-            out_specs=[
-                half_block,
-                half_block,
+            out_specs=[grad_block] * grad_count
+            + [
                 pl.BlockSpec(
                     (3, 1, rows, pair_width), lambda pair, side: (0, pair + start, 0, 0)
                 ),
                 whole((rows, LANES)),
             ],
         ),
-        out_shape=[
-            half_shape,
-            half_shape,
+        out_shape=[grad_shape] * grad_count
+        + [
             jax.ShapeDtypeStruct((3, experts // 2, rows, pair_width), jnp.bfloat16),
             jax.ShapeDtypeStruct((rows, LANES), jnp.float32),
         ],
-        input_output_aliases={9: 2} if extra else {},
+        input_output_aliases={9: grad_count} if extra else {},
         name="expert_chunk",
         compiler_params=params(1),
     )(
@@ -452,25 +479,27 @@
     )
 
 
-def expert_rows(kinds, weights, acts, d_gates, route_hot):
-    unused, pairs, rows, pair_width = acts.shape
-    experts, width, hidden = weights[0].shape
+def expert_rows(core, kinds, weights, acts, d_gates, route_hot):
+    _, pairs, rows, pair_width = acts.shape
+    _, width, hidden = weights[0].shape
     step_pairs = 4
     total = len(kinds)
     gate_lanes = 0 if d_gates is None else LANES
-    row_block = min(256, rows)
-
-    def kernel(*refs):
+    row_block = rows // 4
+
+    def kernel(core_ref, *refs):
         act_refs, weight_refs = refs[:total], refs[total : 2 * total]
-        keep = refs[-1]
-        out_ref = refs[-2]
+        stay, leave, keep = refs[-3:]
         step = pl.program_id(0)
         right_side = jnp.concatenate(
             [ref[j] for ref in weight_refs for j in range(2 * step_pairs)], 1
         )
-
-        def row_step(block, carry):
-            span = pl.ds(pl.multiple_of(block * row_block, row_block), row_block)
+        for slot in range(4):
+            target = leave if slot < 2 else stay
+            choice = core_ref[0] if slot >= 2 else 1 - core_ref[0]
+            span = pl.ds(
+                pl.multiple_of((2 * (slot % 2) + choice) * row_block, row_block), row_block
+            )
             left_side = jnp.concatenate(
                 [ref[0, j, span, :] for ref in act_refs for j in range(step_pairs)], 1
             )
@@ -486,39 +515,42 @@
 
             @pl.when(step == pl.num_programs(0) - 1)
             def _():
-                out_ref[span, :width] = (keep[span, :] + term).astype(jnp.bfloat16)
+                target[slot % 2, :, :width] = (keep[span, :] + term).astype(jnp.bfloat16)
                 if gate_lanes:
-                    out_ref[span, width:] = (
+                    target[slot % 2, :, width:] = (
                         refs[2 * total][span, :] * refs[2 * total + 1][span, :]
                     ).astype(jnp.bfloat16)
 
-            return carry
-
-        lax.fori_loop(0, rows // row_block, row_step, 0)
-
     def act_block(kind):
-        return pl.BlockSpec((1, step_pairs, rows, pair_width), lambda i: (kind, i, 0, 0))
+        return pl.BlockSpec((1, step_pairs, rows, pair_width), lambda i, core: (kind, i, 0, 0))
 
     extra = [] if d_gates is None else [d_gates, route_hot]
+    out_dims = (2, row_block, width + gate_lanes)
     return pl.pallas_call(
         kernel,
-        grid=(pairs // step_pairs,),
-        in_specs=[act_block(kind) for kind in kinds]
-        + [pl.BlockSpec((2 * step_pairs, width, hidden), lambda i: (i, 0, 0))] * total
-        + [whole((rows, LANES))] * len(extra),
-        out_specs=whole((rows, width + gate_lanes)),
-        out_shape=jax.ShapeDtypeStruct((rows, width + gate_lanes), jnp.bfloat16),
-        scratch_shapes=[pltpu.VMEM((rows, width), jnp.float32)],
+        grid_spec=pltpu.PrefetchScalarGridSpec(
+            num_scalar_prefetch=1,
+            grid=(pairs // step_pairs,),
+            in_specs=[act_block(kind) for kind in kinds]
+            + [pl.BlockSpec((2 * step_pairs, width, hidden), lambda i, core: (i, 0, 0))] * total
+            + [whole((rows, LANES))] * len(extra),
+            out_specs=[whole(out_dims)] * 2,
+            scratch_shapes=[pltpu.VMEM((rows, width), jnp.float32)],
+        ),
+        out_shape=[jax.ShapeDtypeStruct(out_dims, jnp.bfloat16)] * 2,
         name="expert_rows",
         compiler_params=params(1),
-    )(*([acts] * total), *weights, *extra)
-
-
-def middle_back(d_packed, probs, share_row, live_lanes, residual, cotangent_rows, gain_row, weight):
+    )(core, *([acts] * total), *weights, *extra)
+
+
+def middle_back(
+    d_kept, d_arrived, probs, share_row, live_lanes, residual, cotangent_rows, gain_row, weight
+):
     tokens, width = residual.shape
 
     def kernel(
-        packed,
+        kept_ref,
+        arrived_ref,
         prob_ref,
         share_ref,
         live_ref,
@@ -532,12 +564,13 @@
         d_gain,
         d_groups,
     ):
+        packed = kept_ref[...].astype(jnp.float32) + arrived_ref[...].astype(jnp.float32)
         prob = prob_ref[...]
         live = live_ref[...]
-        d_prob = packed[:, width:].astype(jnp.float32) + share_ref[...] * live
+        d_prob = packed[:, width:] + share_ref[...] * live
         logits = (prob * (d_prob - jnp.sum(prob * d_prob, -1, keepdims=True))).astype(jnp.bfloat16)
         d_logits[...] = logits
-        d_normed = packed[:, :width].astype(jnp.float32) + turned(logits, weight_ref[:, width:])
+        d_normed = packed[:, :width] + turned(logits, weight_ref[:, width:])
         total = residual_ref[...]
         scale = rms_scale(total)
         unit = total * scale
@@ -554,7 +587,7 @@
                 low, weight_ref[j * QUERY_GROUP : (j + 1) * QUERY_GROUP, :width]
             ).astype(jnp.bfloat16)
 
-    inputs = (d_packed, probs, share_row, live_lanes, residual, cotangent_rows, gain_row, weight)
+    inputs = (d_kept, d_arrived, probs, share_row, live_lanes, residual, cotangent_rows, gain_row, weight)
     out_shape = [
         jax.ShapeDtypeStruct((tokens, width), jnp.float32),
         jax.ShapeDtypeStruct((tokens, width), jnp.bfloat16),
@@ -603,16 +636,37 @@
 
 def project_back(d_fused, fused_weight, normed, rows_in, gain_row, d_residual):
     tokens, width = rows_in.shape
-    step_width = 2 * FUSED_GROUP
     steps = KEY_VALUE_HEADS // 2
-
-    def kernel(d_ref, weight, normed_ref, rows, gain, d_residual_ref, late, d_input, keep):
+    query_step, head_step = 2 * QUERY_GROUP, 2 * HEAD_DIM
+    key_start = KEY_VALUE_HEADS * QUERY_GROUP
+    value_start = key_start + KEY_VALUE_HEADS * HEAD_DIM
+
+    def kernel(
+        d_ref, query_w, key_w, value_w, normed_ref, rows, gain, d_residual_ref, late, d_input, keep
+    ):
         step = pl.program_id(0)
-        d_pair = jnp.concatenate([d_ref[0], d_ref[1]], 1)
-        late[:, pl.ds(pl.multiple_of(step * step_width, LANES), step_width)] = over_rows(
-            normed_ref[...], d_pair
-        ).astype(jnp.bfloat16)
-        term = turned(d_pair, weight[...])
+        first, second = d_ref[0], d_ref[1]
+        key_end = QUERY_GROUP + HEAD_DIM
+        d_pair = jnp.concatenate(
+            [
+                first[:, :QUERY_GROUP],
+                second[:, :QUERY_GROUP],
+                first[:, QUERY_GROUP:key_end],
+                second[:, QUERY_GROUP:key_end],
+                first[:, key_end:],
+                second[:, key_end:],
+            ],
+            1,
+        )
+        grad = over_rows(normed_ref[...], d_pair).astype(jnp.bfloat16)
+        late[:, pl.ds(pl.multiple_of(step * query_step, LANES), query_step)] = grad[:, :query_step]
+        late[:, pl.ds(pl.multiple_of(key_start + step * head_step, LANES), head_step)] = grad[
+            :, query_step : query_step + head_step
+        ]
+        late[:, pl.ds(pl.multiple_of(value_start + step * head_step, LANES), head_step)] = grad[
+            :, query_step + head_step :
+        ]
+        term = turned(d_pair, jnp.concatenate([query_w[...], key_w[...], value_w[...]], 1))
 
         @pl.when(step == 0)
         def _():
@@ -640,7 +694,9 @@
         grid=(steps,),
         in_specs=[
             pl.BlockSpec((2, tokens, FUSED_GROUP), lambda i: (i, 0, 0)),
-            pl.BlockSpec((width, step_width), lambda i: (0, i)),
+            pl.BlockSpec((width, query_step), lambda i: (0, i)),
+            pl.BlockSpec((width, head_step), lambda i: (0, key_start // head_step + i)),
+            pl.BlockSpec((width, head_step), lambda i: (0, value_start // head_step + i)),
             whole((tokens, width)),
             whole((tokens, width)),
             whole((1, width)),
@@ -654,10 +710,10 @@
         scratch_shapes=[pltpu.VMEM((tokens, width), jnp.float32)],
         name="project_back",
         compiler_params=params(1),
-    )(d_fused, fused_weight, normed, rows_in, gain_row, d_residual)
-
-
-def local(
+    )(d_fused, fused_weight, fused_weight, fused_weight, normed, rows_in, gain_row, d_residual)
+
+
+def body(
     layer_input,
     gain_attn,
     w_query,
@@ -692,21 +748,43 @@
     here_sequences = local_sequences // head_shares
     width_rows = gain_attn.shape[0]
 
-    def fused_columns(query_part, key_part, value_part):
-        rows = query_part.shape[0]
-        return jnp.concatenate(
-            [
-                query_part.reshape(rows, KEY_VALUE_HEADS, QUERY_GROUP),
-                key_part.reshape(rows, KEY_VALUE_HEADS, HEAD_DIM),
-                value_part.reshape(rows, KEY_VALUE_HEADS, HEAD_DIM),
-            ],
-            -1,
-        ).reshape(rows, FUSED_WIDTH)
+    core_pos = lax.axis_index("k")
+    chip_pos = lax.axis_index("x")
+    swap = [(0, 1), (1, 0)]
+
+    def added(first, second):
+        return (first.astype(jnp.float32) + second.astype(jnp.float32)).astype(jnp.bfloat16)
+
+    def picked(values, which):
+        return lax.dynamic_index_in_dim(values, which, 0, keepdims=False)
+
+    def chip_halves(stay, arrived):
+        leave_now = added(picked(stay, 1 - chip_pos), picked(arrived, 1 - chip_pos))
+        return (
+            added(picked(stay, chip_pos), picked(arrived, chip_pos)),
+            lax.ppermute(leave_now, "x", swap),
+        )
+
+    def halved_by(values, axis_name, which):
+        return added(
+            picked(values, which), lax.ppermute(picked(values, 1 - which), axis_name, swap)
+        )
+
+    def reduced_rows(terms):
+        columns = terms.shape[1]
+        parts = terms.reshape(ctx_parts, 2, 2, 2, -1, columns)
+        for axis_name, which, dim in (("k", core_pos, 3), ("x", chip_pos, 2), ("y", ctx_side, 1)):
+            parts = halved_by(jnp.moveaxis(parts, dim, 0), axis_name, which)
+        return lax.psum_scatter(
+            parts.reshape(-1, columns), "z", scatter_dimension=0, tiled=True
+        ).astype(jnp.float32)
 
     fused_weight = lax.all_gather(
         jnp.concatenate(
             [
-                fused_columns(w_query, key_projection_weight, value_projection_weight),
+                w_query,
+                key_projection_weight,
+                value_projection_weight,
                 jnp.pad(gain_attn[:, None], ((0, 0), (0, LANES - 1))),
             ],
             1,
@@ -753,13 +831,8 @@
     column_positions = jnp.broadcast_to(all_positions[None, :], (8, seq_len))
     every_cos, every_sin = rope_tables(all_positions)
     own_cos, own_sin = rope_tables(local_positions)
-    still = jnp.ones_like(own_cos)
-    step_cos = jnp.tile(
-        jnp.concatenate([own_cos] * (GROUP + 1) + [still], 1), (local_sequences, 2)
-    )
-    step_sin = jnp.tile(
-        jnp.concatenate([own_sin] * (GROUP + 1) + [0.0 * still], 1), (local_sequences, 2)
-    )
+    step_cos = jnp.tile(own_cos, (local_sequences, 2 * (GROUP + 1)))
+    step_sin = jnp.tile(own_sin, (local_sequences, 2 * (GROUP + 1)))
     pair_cos, pair_sin = jnp.tile(every_cos, (1, 2)), jnp.tile(every_sin, (1, 2))
 
     rows_in = layer_input.reshape(tokens, model_width)
@@ -792,12 +865,28 @@
     hot_table = jnp.pad(route_hot, lane_pad)
     gate_table = prob_table * hot_table
 
+    group_sums = jnp.concatenate(
+        [
+            jnp.sum(hot_table * live_group[:, None], 0, keepdims=True),
+            jnp.sum(prob_table * live_group[:, None], 0, keepdims=True),
+        ],
+        0,
+    )
+    for axis_name, count in (("y", 2), ("z", ctx_parts)):
+        step = 1
+        while step < count:
+            group_sums = group_sums + lax.ppermute(
+                group_sums, axis_name, [(i, i ^ step) for i in range(count)]
+            )
+            step *= 2
+    all_sums = group_sums[:, :experts]
+
     side = ctx_side.astype(jnp.int32).reshape(1)
-    swap = [(0, 1), (1, 0)]
+    core = core_pos.astype(jnp.int32).reshape(1)
     acts, d_gates, reduced = None, None, []
     first_expert = 0
-    for chunk in CHUNKS:
-        stay, leave, acts, gate_piece = expert_chunk(
+    for number, chunk in enumerate(CHUNKS):
+        *terms, acts, gate_piece = expert_chunk(
             first_expert,
             chunk,
             side,
@@ -811,25 +900,37 @@
             w_up,
             w_down,
             acts,
+            number > 0,
         )
         first_expert += chunk
         d_gates = gate_piece if d_gates is None else d_gates + gate_piece
-        arrived = lax.ppermute(leave, "y", swap)
-        halved = (stay.astype(jnp.float32) + arrived.astype(jnp.float32)).astype(jnp.bfloat16)
-        reduced.append(lax.psum_scatter(halved, "z", scatter_dimension=2, tiled=True))
-
-    d_packed = expert_rows((1, 2), (w_gate, w_up), acts, d_gates, hot_table)
-    d_packed_own = lax.psum_scatter(d_packed, SHARD, scatter_dimension=0, tiled=True)
-    moe_rows = expert_rows((0,), (w_down,), acts, None, None)
-    moe_own = lax.psum_scatter(moe_rows, SHARD, scatter_dimension=0, tiled=True)
+        if number:
+            arrived = lax.ppermute(terms[1], "y", swap)
+            halved = added(terms[0], arrived)
+            if number == 1:
+                first_halved = halved
+            if number == 2:
+                second_halved = halved
+            reduced.append(lax.psum_scatter(halved, "z", scatter_dimension=2, tiled=True))
+        else:
+            ringed = lax.psum_scatter(terms[0], "z", scatter_dimension=2, tiled=True)
+
+    acts, first_halved = lax.optimization_barrier((acts, first_halved))
+    d_stay, d_leave = expert_rows(core, (1, 2), (w_gate, w_up), acts, d_gates, hot_table)
+    d_came = lax.ppermute(d_leave, "k", swap)
+    d_kept, d_arrived = chip_halves(d_stay, d_came)
+    moe_stay, moe_leave = expert_rows(core, (0,), (w_down,), acts, None, None)
+    moe_kept, moe_arrived = chip_halves(moe_stay, lax.ppermute(moe_leave, "k", swap))
     layer_output = (
-        (residual + moe_own.astype(jnp.float32)).astype(jnp.bfloat16).reshape(layer_input.shape)
-    )
-
-    group_sums = jnp.stack(
-        [jnp.sum(route_hot * live_group[:, None], 0), jnp.sum(router_probs * live_group[:, None], 0)]
-    )
-    all_sums = lax.psum(group_sums, CTX)
+        (residual + moe_kept.astype(jnp.float32) + moe_arrived.astype(jnp.float32))
+        .astype(jnp.bfloat16)
+        .reshape(layer_input.shape)
+    )
+    ringed = jnp.moveaxis(
+        ringed.reshape(3, CHUNKS[0], 2, model_width // n_ctx, -1), 2, 0
+    )
+    reduced.insert(0, halved_by(ringed, "y", ctx_side))
+
     live_all = jnp.sum(lengths).astype(jnp.float32)
     route_share = all_sums[0] / (top_k * live_all)
     aux_loss = experts * jnp.sum(route_share * all_sums[1] / live_all)
@@ -837,7 +938,8 @@
 
     own_probs = lax.dynamic_slice_in_dim(prob_table, shard_pos * tokens, tokens, 0)
     d_residual, d_branch, d_logits, d_gain_two, d_groups = middle_back(
-        d_packed_own,
+        d_kept,
+        d_arrived,
         own_probs,
         share_row,
         live_lanes,
@@ -847,6 +949,9 @@
         out_weight,
     )
     d_attended = exchange(d_groups.reshape(n_ctx, here_sequences, sequence_rows, QUERY_GROUP))
+    d_branch, d_attended, second_halved = lax.optimization_barrier(
+        (d_branch, d_attended, second_halved)
+    )
     early_terms = early_grads(attended_low, d_branch, second_normed, d_logits, d_gain_two, experts)
     d_fused_rows = attend_back(
         fused_rows,
@@ -861,11 +966,9 @@
     late_terms, grad_input = project_back(
         d_fused, fused_weight, first_normed, rows_in, gain_one, d_residual
     )
-    early_rows = lax.psum_scatter(early_terms, EVERY, scatter_dimension=0, tiled=True)
-    late_rows = lax.psum_scatter(late_terms, EVERY, scatter_dimension=0, tiled=True)
-    early_rows, late_rows = early_rows.astype(jnp.float32), late_rows.astype(jnp.float32)
-    late_groups = late_rows[:, :FUSED_WIDTH].reshape(-1, KEY_VALUE_HEADS, FUSED_GROUP)
-    own_rows = late_rows.shape[0]
+    early_rows, late_rows = reduced_rows(early_terms), reduced_rows(late_terms)
+    query_end = KEY_VALUE_HEADS * QUERY_GROUP
+    key_end = query_end + KEY_VALUE_HEADS * HEAD_DIM
     grads = [
         jnp.concatenate([piece[kind] for piece in reduced], 0).astype(jnp.float32)
         for kind in range(3)
@@ -874,9 +977,9 @@
         layer_output,
         grad_input.reshape(layer_input.shape),
         late_rows[:, FUSED_WIDTH],
-        late_groups[:, :, :QUERY_GROUP].reshape(own_rows, -1),
-        late_groups[:, :, QUERY_GROUP : QUERY_GROUP + HEAD_DIM].reshape(own_rows, -1),
-        late_groups[:, :, QUERY_GROUP + HEAD_DIM :].reshape(own_rows, -1),
+        late_rows[:, :query_end],
+        late_rows[:, query_end:key_end],
+        late_rows[:, key_end:FUSED_WIDTH],
         early_rows[:, :model_width],
         early_rows[:, model_width + experts],
         early_rows[:, model_width : model_width + experts],
@@ -907,7 +1010,7 @@
         P(SHARD, CTX, None, None, None),
     )
     return jax.shard_map(
-        local,
+        body,
         mesh=fine,
         in_specs=placed,
         out_specs=(

time: 1330 us -> 1050 us (0.79)
  waiting for transfers between devices: 742 us -> 416 us
  other arithmetic: 57.5 us -> 78.7 us
    ppermute x5 -> x18, waiting for transfers between devices: 493 us -> 251 us  [the longest x4 107 us: body(): arrived = lax.ppermute(terms[1], 'y', swap)]
    reduce_scatter x9 -> x7, waiting for transfers between devices: 108 us -> 50.6 us  [the longest x4 29.9 us: body(): lax.psum_scatter(halved, 'z', scatter_dimension=2, tiled=True)]
    all_to_all x2, blocking collectives: 106 us -> 139 us  [exchange(): return lax.all_to_all(groups, CTX, 0, 0, tiled=True)]
    all_to_all x2, waiting for transfers between devices: 67.3 us -> 39.1 us  [exchange(): return lax.all_to_all(groups, CTX, 0, 0, tiled=True)]
    convert_element_type x15 -> x23, other arithmetic: 42.9 us -> 64.5 us  [the longest x13 49.4 us: added(): (first.astype(jnp.float32) + second.astype(jnp.float32)).astype(jnp.bfloa...]
    psum x1 -> x0, blocking collectives: 21.4 us -> none  [local(): all_sums = lax.psum(group_sums, CTX)]
  transfers between devices with their start and end apart: 20 -> 31, of which waited for: 10 -> 18; matrix products, arithmetic and copies ran while one was open for 6% -> 11% of each run, Pallas kernels for 8% -> 26%
where the time goes in v3:
time: 1050 us; the launch traced here: 1040 us
  waiting for transfers between devices  416 us (40%)
  Pallas kernels  303 us (29%)
  blocking collectives  139 us (13%)
  other arithmetic  78.7 us (7%)
  local copies, waits for them, and re-layouts  59.9 us (6%)
  starting transfers between devices  25.7 us (2%)
  between operations  17.3 us (2%)
    pallas_call x5, Pallas kernels, expert_chunk(): pl.pallas_call(kernel, grid_spec=pltpu.PrefetchScalarGridSpec(num_scalar_...  157 us
    all_to_all x2, blocking collectives, exchange(): return lax.all_to_all(groups, CTX, 0, 0, tiled=True)  139 us
    ppermute x4, waiting for transfers between devices, body(): arrived = lax.ppermute(terms[1], 'y', swap)  107 us
    ppermute x7, waiting for transfers between devices, halved_by(): lax.ppermute(picked(values, 1 - which), axis_name, swap)  99.9 us
    pallas_call x2, Pallas kernels, expert_rows(): pl.pallas_call(kernel, grid_spec=pltpu.PrefetchScalarGridSpec(num_scalar_...  72.9 us
    all_gather x1, waiting for transfers between devices, body(): lax.all_gather(jnp.concatenate([w_query, key_projection_weight, value_pro...  52.2 us
    convert_element_type x13, other arithmetic, added(): (first.astype(jnp.float32) + second.astype(jnp.float32)).astype(jnp.bfloa...  49.4 us
    ppermute x3, waiting for transfers between devices, body(): lax.ppermute(group_sums, axis_name, [(i, i ^ step) for i in range(count)])  42.2 us
  transfers between devices with their start and end apart: 31, of which 18 were waited for; matrix products, arithmetic and copies ran while one was open for 11% of the time, Pallas kernels for 26%

profile of v3, /device:TPU:0, one launch (start us, length us, event | category | flops | bytes accessed | tf_op | source)
XLA Modules:
  0.0 1042.4 jit_solution(5812499595935579592)
XLA Ops:
  19.2 52.2 %all-gather.5.cloned.1.call-done.query_w.key_w.value_w = bf16[1536,2688]{1,0:T(8,128)(2,1)} async-done(((bf16[384,2688]{1,0:T(8,128)(2,1)}), bf16[1536,2688]{1,0:T(8,128)(2,1)}) %all-gather.5.cloned.1.call-update) | async-done | bytes 8257552 | tf_op jit(solution)/shard_map/all_gather | solution.py:782
  81.2 43.0 %all_to_all.20.query_ref.key_ref = bf16[8,4,64,320]{3,2,1,0:T(8,128)(2,1)} all-to-all(bf16[8,4,64,320]{3,2,1,0:T(8,128)(2,1)} %bitcast.164), channel_id=1, replica_groups=mesh['z'=4,'y'=2,'x'=2,'k'=2] {'z','y'}, dimensions={0} | all-to-all | bytes 2621440 | tf_op jit(solution)/shard_map/all_to_all | solution.py:845
  142.9 23.8 %all-to-all-done.1 = bf16[8,4,64,192]{3,2,1,0:T(8,128)(2,1)S(1)} async-done(((bf16[8,4,64,192]{3,2,1,0:T(8,128)(2,1)}), bf16[8,4,64,192]{3,2,1,0:T(8,128)(2,1)S(1)}, u32[]{:S(2)}, u32[]{:S(2)}) %all-to-all-start.1) | async-done | bytes 786464 | tf_op jit(solution)/shard_map/all_to_all | solution.py:845
  181.8 21.5 %all-gather.9.cloned.1.call-done = bf16[1024,1536]{0,1:T(8,128)(2,1)} async-done(((bf16[256,1536]{0,1:T(8,128)(2,1)}), bf16[1024,1536]{0,1:T(8,128)(2,1)}) %all-gather.9.cloned.1.call-update) | async-done | bytes 3145744 | tf_op jit(solution)/shard_map/all_gather | solution.py:857
  215.2 31.1 %expert_chunk.5 = (bf16[3,8,1536,128]{3,2,1,0:T(8,128)(2,1)}, bf16[3,20,1024,256]{3,2,1,0:T(8,128)(2,1)}, f32[1024,128]{1,0:T(8,128)}) custom-call(s32[1]{0:T(128)} %bitcast.4.side_ref, bf16[1024,1536]{1,0:T(8,128)(2,1)} %copy.139.normed, bf16[1536,1024]{1,0:T(8,128)(2,1)} %bitcast.144, bf16[1024,1536]{1,0:T(8,128)(2,1)} %all-gather.11.cloned.1.call-done.cotan, ...), custom_call_target="tpu_custom_call" | custom-call | tf_op jit(solution)/shard_map/expert_chunk/pallas_call | solution.py:436
  246.3 31.2 %expert_chunk.6 = (bf16[3,8,768,128]{3,2,1,0:T(8,128)(2,1)}, bf16[3,8,768,128]{3,2,1,0:T(8,128)(2,1)}, bf16[3,20,1024,256]{3,2,1,0:T(8,128)(2,1)}, f32[1024,128]{1,0:T(8,128)}) custom-call(s32[1]{0:T(128)} %bitcast.4.side_ref, bf16[1024,1536]{1,0:T(8,128)(2,1)} %copy.139.normed, bf16[1536,1024]{1,0:T(8,128)(2,1)} %bitcast.145, ...), custom_call_target="tpu_custom_call", output_to_operand_aliasing={{2}: (9, {})} | custom-call | tf_op jit(solution)/shard_map/expert_chunk/pallas_call | solution.py:436
  279.1 31.5 %expert_chunk.7 = (bf16[3,8,768,128]{3,2,1,0:T(8,128)(2,1)}, bf16[3,8,768,128]{3,2,1,0:T(8,128)(2,1)}, bf16[3,20,1024,256]{3,2,1,0:T(8,128)(2,1)}, f32[1024,128]{1,0:T(8,128)}) custom-call(s32[1]{0:T(128)} %bitcast.4.side_ref, bf16[1024,1536]{1,0:T(8,128)(2,1)} %copy.139.normed, bf16[1536,1024]{1,0:T(8,128)(2,1)} %bitcast.146, ...), custom_call_target="tpu_custom_call", output_to_operand_aliasing={{2}: (9, {})} | custom-call | tf_op jit(solution)/shard_map/expert_chunk/pallas_call | solution.py:436
  312.0 31.4 %expert_chunk.8 = (bf16[3,8,768,128]{3,2,1,0:T(8,128)(2,1)}, bf16[3,8,768,128]{3,2,1,0:T(8,128)(2,1)}, bf16[3,20,1024,256]{3,2,1,0:T(8,128)(2,1)}, f32[1024,128]{1,0:T(8,128)}) custom-call(s32[1]{0:T(128)} %bitcast.4.side_ref, bf16[1024,1536]{1,0:T(8,128)(2,1)} %copy.139.normed, bf16[1536,1024]{1,0:T(8,128)(2,1)} %bitcast.147, ...), custom_call_target="tpu_custom_call", output_to_operand_aliasing={{2}: (9, {})} | custom-call | tf_op jit(solution)/shard_map/expert_chunk/pallas_call | solution.py:436
  343.5 31.6 %expert_chunk.9 = (bf16[3,8,768,128]{3,2,1,0:T(8,128)(2,1)}, bf16[3,8,768,128]{3,2,1,0:T(8,128)(2,1)}, bf16[3,20,1024,256]{3,2,1,0:T(8,128)(2,1)}, f32[1024,128]{1,0:T(8,128)}) custom-call(s32[1]{0:T(128)} %bitcast.4.side_ref, bf16[1024,1536]{1,0:T(8,128)(2,1)} %copy.139.normed, bf16[1536,1024]{1,0:T(8,128)(2,1)} %bitcast.148, ...), custom_call_target="tpu_custom_call", output_to_operand_aliasing={{2}: (9, {})} | custom-call | tf_op jit(solution)/shard_map/expert_chunk/pallas_call | solution.py:436
  390.2 45.8 %expert_rows.3 = (bf16[2,256,1664]{2,1,0:T(8,128)(2,1)}, bf16[2,256,1664]{2,1,0:T(8,128)(2,1)}) custom-call(s32[1]{0:T(128)} %bitcast.3.core_ref, bf16[3,20,1024,256]{3,2,1,0:T(8,128)(2,1)} %get-tuple-element.61.refs_0_.refs_1_, bf16[3,20,1024,256]{3,2,1,0:T(8,128)(2,1)} %get-tuple-element.61.refs_0_.refs_1_, bf16[40,1536,128]{2,1,0:T(8,128)(2,1)} %refs_2_.1, ...), custom_call_target="tpu_custom_call" | custom-call | tf_op jit(solution)/shard_map/expert_rows/pallas_call | solution.py:529
  442.9 40.1 %collective-permute-done.5 = f32[2,128]{1,0:T(2,128)S(1)} collective-permute-done((f32[2,128]{1,0:T(2,128)S(1)}, f32[2,128]{1,0:T(2,128)S(1)}, u32[]{:S(2)}, u32[]{:S(2)}) %collective-permute-start.5) | collective-permute-done | bytes 1056 | tf_op jit(solution)/shard_map/ppermute | solution.py:878
  514.3 15.3 %all-to-all-done.2.d_ref = bf16[8,4,64,192]{3,2,1,0:T(8,128)(2,1)S(1)} async-done(((bf16[8,4,64,192]{3,2,1,0:T(8,128)(2,1)}), bf16[8,4,64,192]{3,2,1,0:T(8,128)(2,1)S(1)}, u32[]{:S(2)}, u32[]{:S(2)}) %all-to-all-start.2) | async-done | bytes 786464 | tf_op jit(solution)/shard_map/all_to_all | solution.py:845
  545.8 29.9 %collective-permute-done.13 = bf16[4,2,48,1664]{3,2,0,1:T(8,128)(2,1)} collective-permute-done((bf16[4,2,48,1664]{3,2,0,1:T(8,128)(2,1)}, bf16[4,2,48,1664]{3,2,0,1:T(8,128)(2,1)}, u32[]{:S(2)}, u32[]{:S(2)}) %collective-permute-start.13) | collective-permute-done | bytes 1277984 | tf_op jit(solution)/shard_map/ppermute | solution.py:770
  579.7 14.4 %collective-permute-done.14 = bf16[4,48,1664]{2,1,0:T(8,128)(2,1)S(1)} collective-permute-done((bf16[4,48,1664]{2,1,0:T(8,128)(2,1)S(1)}, bf16[4,48,1664]{2,1,0:T(8,128)(2,1)S(1)}, u32[]{:S(2)}, u32[]{:S(2)}) %collective-permute-start.14) | collective-permute-done | bytes 639008 | tf_op jit(solution)/shard_map/ppermute | solution.py:770
  599.0 101.1 %collective-permute-done.16 = bf16[3,8,768,128]{3,2,1,0:T(8,128)(2,1)S(1)} collective-permute-done((bf16[3,8,768,128]{3,2,1,0:T(8,128)(2,1)}, bf16[3,8,768,128]{3,2,1,0:T(8,128)(2,1)S(1)}, u32[]{:S(2)}, u32[]{:S(2)}) %collective-permute-start.16) | collective-permute-done | bytes 4718624 | tf_op jit(solution)/shard_map/ppermute | solution.py:908
  709.6 18.8 %attend_back.1 = bf16[8,4,64,320]{3,2,1,0:T(8,128)(2,1)} custom-call(s32[4]{0:T(128)} %copy-done.25, bf16[8,4,64,320]{3,2,1,0:T(8,128)(2,1)} %all_to_all.20.query_ref.key_ref, bf16[8,4,64,320]{3,2,1,0:T(8,128)(2,1)} %all_to_all.20.query_ref.key_ref, bf16[8,4,64,192]{3,2,1,0:T(8,128)(2,1)} %copy-done.6, s32[512,128]{1,0:T(8,128)} %broadcast_in_dim.33.row_ref, ...), custom_call_target="tpu_custom_call" | custom-call | tf_op jit(solution)/shard_map/attend_back/pallas_call | solution.py:247
  728.4 96.5 %all_to_all.21 = bf16[8,4,64,320]{3,2,1,0:T(8,128)(2,1)} all-to-all(bf16[8,4,64,320]{3,2,1,0:T(8,128)(2,1)} %attend_back.1), channel_id=1, replica_groups=mesh['z'=4,'y'=2,'x'=2,'k'=2] {'z','y'}, dimensions={0} | all-to-all | bytes 2621440 | tf_op jit(solution)/shard_map/all_to_all | solution.py:845
  824.9 15.2 %project_back.1 = (bf16[1536,2688]{1,0:T(8,128)(2,1)}, f32[256,1536]{1,0:T(8,128)}) custom-call(bf16[8,256,320]{2,1,0:T(8,128)(2,1)} %bitcast.156, bf16[1536,2688]{1,0:T(8,128)(2,1)} %all-gather.5.cloned.1.call-done.query_w.key_w.value_w, bf16[1536,2688]{1,0:T(8,128)(2,1)} %all-gather.5.cloned.1.call-done.query_w.key_w.value_w, ...), custom_call_target="tpu_custom_call" | custom-call | tf_op jit(solution)/shard_map/project_back/pallas_call | solution.py:692
  858.2 27.1 %expert_rows.2 = (bf16[2,256,1536]{2,1,0:T(8,128)(2,1)}, bf16[2,256,1536]{2,1,0:T(8,128)(2,1)}) custom-call(s32[1]{0:T(128)} %bitcast.3.core_ref, bf16[3,20,1024,256]{3,2,1,0:T(8,128)(2,1)} %get-tuple-element.61.refs_0_.refs_1_, bf16[40,1536,128]{2,1,0:T(8,128)(2,1)} %refs_1_.1), custom_call_target="tpu_custom_call" | custom-call | tf_op jit(solution)/shard_map/expert_rows/pallas_call | solution.py:529
  885.9 20.1 %collective-permute-done.10 = bf16[4,2,48,2688]{3,2,1,0:T(8,128)(2,1)} collective-permute-done((bf16[4,2,48,2688]{3,2,1,0:T(8,128)(2,1)}, bf16[4,2,48,2688]{3,2,1,0:T(8,128)(2,1)}, u32[]{:S(2)}, u32[]{:S(2)}) %collective-permute-start.10) | collective-permute-done | bytes 2064416 | tf_op jit(solution)/shard_map/ppermute | solution.py:770
  917.6 18.7 %collective-permute-done.11 = bf16[4,48,2688]{2,1,0:T(8,128)(2,1)} collective-permute-done((bf16[4,48,2688]{2,1,0:T(8,128)(2,1)}, bf16[4,48,2688]{2,1,0:T(8,128)(2,1)}, u32[]{:S(2)}, u32[]{:S(2)}) %collective-permute-start.11) | collective-permute-done | bytes 1032224 | tf_op jit(solution)/shard_map/ppermute | solution.py:770
  948.4 12.1 %collective-permute-done.15 = bf16[3,8,192,128]{3,2,1,0:T(8,128)(2,1)} collective-permute-done((bf16[3,8,192,128]{3,2,1,0:T(8,128)(2,1)S(1)}, bf16[3,8,192,128]{3,2,1,0:T(8,128)(2,1)}, u32[]{:S(2)}, u32[]{:S(2)}) %collective-permute-start.15) | collective-permute-done | bytes 1179680 | tf_op jit(solution)/shard_map/ppermute | solution.py:770
  969.7 29.9 %reduce-scatter.20.cloned.1.call-done = bf16[3,8,192,128]{3,2,1,0:T(8,128)(2,1)} async-done(((bf16[3,8,768,128]{3,2,1,0:T(8,128)(2,1)}), bf16[3,8,192,128]{3,2,1,0:T(8,128)(2,1)}) %reduce-scatter.20.cloned.1.call-update) | async-done | bytes 1179664 | tf_op jit(solution)/shard_map/reduce_scatter | solution.py:914
  1008.9 20.7 %reduce-scatter.8.cloned.1.call-done = bf16[48,2688]{1,0:T(8,128)(2,1)} async-done(((bf16[192,2688]{1,0:T(8,128)(2,1)}), bf16[48,2688]{1,0:T(8,128)(2,1)}) %reduce-scatter.8.cloned.1.call-update) | async-done | bytes 258064 | tf_op jit(solution)/shard_map/reduce_scatter | solution.py:778
  (226 shorter events, 222.1 us)
Async XLA Ops:
  7.2 64.3 %all-gather.5.cloned.1.call-start = ((), (), s32[]{:S(2)}) async-start(), calls=%async_computation.11 | async-start | bytes 10321920 | tf_op jit(solution)/shard_map/all_gather | solution.py:782
  11.0 130.0 %all-gather.7.cloned.1.call-start = ((), (), s32[]{:S(2)}) async-start(), calls=%async_computation.12 | async-start | bytes 6389760 | tf_op jit(solution)/shard_map/all_gather | solution.py:796
  14.1 163.0 %all-gather.11.cloned.1.call-start = ((), (), s32[]{:S(2)}) async-start(), calls=%async_computation.14 | async-start | bytes 3932160 | tf_op jit(solution)/shard_map/all_gather | solution.py:841
  137.3 29.4 %all-to-all-start.1 = ((bf16[8,4,64,192]{3,2,1,0:T(8,128)(2,1)}), bf16[8,4,64,192]{3,2,1,0:T(8,128)(2,1)S(1)}, u32[]{:S(2)}, u32[]{:S(2)}) async-start(bf16[8,4,64,192]{3,2,1,0:T(8,128)(2,1)} %attend.1), calls=%async_computation.1 | async-start | bytes 2097152 | tf_op jit(solution)/shard_map/all_to_all | solution.py:845
  140.9 62.5 %all-gather.9.cloned.1.call-start = ((), (), s32[]{:S(2)}) async-start(), calls=%async_computation.13 | async-start | bytes 3932160 | tf_op jit(solution)/shard_map/all_gather | solution.py:857
  176.0 738.9 %reduce-scatter.12.cloned.1.call-start = ((), (), s32[]{:S(2)}) async-start(), calls=%async_computation.17 | async-start | bytes 11796480 | tf_op jit(solution)/shard_map/reduce_scatter | solution.py:916
  277.5 105.1 %collective-permute-start = (bf16[3,8,768,128]{3,2,1,0:T(8,128)(2,1)}, bf16[3,8,768,128]{3,2,1,0:T(8,128)(2,1)}, u32[]{:S(2)}, u32[]{:S(2)}) collective-permute-start(bf16[3,8,768,128]{3,2,1,0:T(8,128)(2,1)} %get-tuple-element.60), channel_id=1, source_target_pairs={{0,4},{4,0},{1,5},{5,1},{2,6},{6,2},{3,7},{7,3},{8,12},{12,8},{9,1... | collective-permute-start | bytes 14155784 | tf_op jit(solution)/shard_map/ppermute | solution.py:908
  310.6 196.0 %collective-permute-start.8 = (bf16[3,8,768,128]{3,2,1,0:T(8,128)(2,1)}, bf16[3,8,768,128]{3,2,1,0:T(8,128)(2,1)}, u32[]{:S(2)}, u32[]{:S(2)}) collective-permute-start(bf16[3,8,768,128]{3,2,1,0:T(8,128)(2,1)} %get-tuple-element.74), channel_id=1, source_target_pairs={{0,4},{4,0},{1,5},{5,1},{2,6},{6,2},{3,7},{7,3},{8,12},{12,8},{9,1... | collective-permute-start | bytes 14155784 | tf_op jit(solution)/shard_map/ppermute | solution.py:908
  436.0 47.0 %collective-permute-start.5 = (f32[2,128]{1,0:T(2,128)S(1)}, f32[2,128]{1,0:T(2,128)S(1)}, u32[]{:S(2)}, u32[]{:S(2)}) collective-permute-start(f32[2,128]{1,0:T(2,128)S(1)} %pad_maximum_fusion.4), channel_id=1, source_target_pairs={{0,4},{4,0},{1,5},{5,1},{2,6},{6,2},{3,7},{7,3},{8,12},{12,8},{9,1... | collective-permute-start | bytes 3080 | tf_op jit(solution)/shard_map/ppermute | solution.py:878
  442.6 49.9 %collective-permute-start.4 = (bf16[256,1664]{1,0:T(8,128)(2,1)S(1)}, bf16[256,1664]{1,0:T(8,128)(2,1)S(1)}, u32[]{:S(2)}, u32[]{:S(2)}) collective-permute-start(bf16[256,1664]{1,0:T(8,128)(2,1)S(1)} %get-tuple-element.162), channel_id=1, source_target_pairs={{0,2},{2,0},{1,3},{3,1},{4,6},{6,4},{5,7},{7,5},{8,10},{10,8},{9,1... | collective-permute-start | bytes 2555912 | tf_op jit(solution)/shard_map/ppermute | solution.py:765
  500.8 28.8 %all-to-all-start.2 = ((bf16[8,4,64,192]{3,2,1,0:T(8,128)(2,1)}), bf16[8,4,64,192]{3,2,1,0:T(8,128)(2,1)S(1)}, u32[]{:S(2)}, u32[]{:S(2)}) async-start(bf16[8,4,64,192]{3,2,1,0:T(8,128)(2,1)} %bitcast.165), calls=%async_computation.2 | async-start | bytes 2097152 | tf_op jit(solution)/shard_map/all_to_all | solution.py:845
  506.4 436.0 %reduce-scatter.10.cloned.1.call-start = ((), (), s32[]{:S(2)}) async-start(), calls=%async_computation.16 | async-start | bytes 798720 | tf_op jit(solution)/shard_map/reduce_scatter | solution.py:778
  545.3 30.4 %collective-permute-start.13 = (bf16[4,2,48,1664]{3,2,0,1:T(8,128)(2,1)}, bf16[4,2,48,1664]{3,2,0,1:T(8,128)(2,1)}, u32[]{:S(2)}, u32[]{:S(2)}) collective-permute-start(bf16[4,2,48,1664]{3,2,0,1:T(8,128)(2,1)} %dynamic-slice_bitcast_fusion.2), channel_id=1, source_target_pairs={{0,2},{2,0},{1,3},{3,1},{4,6},{6,4},{5,7},{7,5},{8,10},{10,8},{9,1... | collective-permute-start | bytes 3833864 | tf_op jit(solution)/shard_map/ppermute | solution.py:770
  596.2 366.9 %reduce-scatter.14.cloned.1.call-start = ((), (), s32[]{:S(2)}) async-start(), calls=%async_computation.18 | async-start | bytes 5898240 | tf_op jit(solution)/shard_map/reduce_scatter | solution.py:914
  596.9 368.3 %reduce-scatter.16.cloned.1.call-start = ((), (), s32[]{:S(2)}) async-start(), calls=%async_computation.19 | async-start | bytes 5898240 | tf_op jit(solution)/shard_map/reduce_scatter | solution.py:914
  597.7 369.8 %reduce-scatter.18.cloned.1.call-start = ((), (), s32[]{:S(2)}) async-start(), calls=%async_computation.20 | async-start | bytes 5898240 | tf_op jit(solution)/shard_map/reduce_scatter | solution.py:914
  597.7 102.4 %collective-permute-start.16 = (bf16[3,8,768,128]{3,2,1,0:T(8,128)(2,1)}, bf16[3,8,768,128]{3,2,1,0:T(8,128)(2,1)S(1)}, u32[]{:S(2)}, u32[]{:S(2)}) collective-permute-start(bf16[3,8,768,128]{3,2,1,0:T(8,128)(2,1)} %get-tuple-element.86), channel_id=1, source_target_pairs={{0,4},{4,0},{1,5},{5,1},{2,6},{6,2},{3,7},{7,3},{8,12},{12,8},{9,1... | collective-permute-start | bytes 14155784 | tf_op jit(solution)/shard_map/ppermute | solution.py:908
  706.2 293.3 %reduce-scatter.20.cloned.1.call-start = ((), (), s32[]{:S(2)}) async-start(), calls=%async_computation.21 | async-start | bytes 5898240 | tf_op jit(solution)/shard_map/reduce_scatter | solution.py:914
  706.3 138.3 %collective-permute-start.17 = (bf16[3,8,768,128]{3,2,1,0:T(8,128)(2,1)}, bf16[3,8,768,128]{3,2,1,0:T(8,128)(2,1)}, u32[]{:S(2)}, u32[]{:S(2)}) collective-permute-start(bf16[3,8,768,128]{3,2,1,0:T(8,128)(2,1)} %get-tuple-element.88), channel_id=1, source_target_pairs={{0,4},{4,0},{1,5},{5,1},{2,6},{6,2},{3,7},{7,3},{8,12},{12,8},{9,1... | collective-permute-start | bytes 14155784 | tf_op jit(solution)/shard_map/ppermute | solution.py:908
  852.2 177.4 %reduce-scatter.8.cloned.1.call-start = ((), (), s32[]{:S(2)}) async-start(), calls=%async_computation.15 | async-start | bytes 1290240 | tf_op jit(solution)/shard_map/reduce_scatter | solution.py:778
  858.2 47.8 %collective-permute-start.10 = (bf16[4,2,48,2688]{3,2,1,0:T(8,128)(2,1)}, bf16[4,2,48,2688]{3,2,1,0:T(8,128)(2,1)}, u32[]{:S(2)}, u32[]{:S(2)}) collective-permute-start(bf16[4,2,48,2688]{3,2,1,0:T(8,128)(2,1)} %dynamic-slice_bitcast_fusion.1), channel_id=1, source_target_pairs={{0,2},{2,0},{1,3},{3,1},{4,6},{6,4},{5,7},{7,5},{8,10},{10,8},{9,1... | collective-permute-start | bytes 6193160 | tf_op jit(solution)/shard_map/ppermute | solution.py:770
  885.3 26.4 %collective-permute-start.1 = (bf16[2,256,1536]{2,1,0:T(8,128)(2,1)}, bf16[2,256,1536]{2,1,0:T(8,128)(2,1)}, u32[]{:S(2)}, u32[]{:S(2)}) collective-permute-start(bf16[2,256,1536]{2,1,0:T(8,128)(2,1)} %get-tuple-element.63), channel_id=1, source_target_pairs={{0,1},{1,0},{2,3},{3,2},{4,5},{5,4},{6,7},{7,6},{8,9},{9,8},{10,11... | collective-permute-start | bytes 4718600 | tf_op jit(solution)/shard_map/ppermute | solution.py:923
  910.4 26.0 %collective-permute-start.11 = (bf16[4,48,2688]{2,1,0:T(8,128)(2,1)}, bf16[4,48,2688]{2,1,0:T(8,128)(2,1)}, u32[]{:S(2)}, u32[]{:S(2)}) collective-permute-start(bf16[4,48,2688]{2,1,0:T(8,128)(2,1)} %dynamic-slice_bitcast_fusion.4), channel_id=1, source_target_pairs={{0,4},{4,0},{1,5},{5,1},{2,6},{6,2},{3,7},{7,3},{8,12},{12,8},{9,1... | collective-permute-start | bytes 3096584 | tf_op jit(solution)/shard_map/ppermute | solution.py:770
  916.3 44.2 %collective-permute-start.15 = (bf16[3,8,192,128]{3,2,1,0:T(8,128)(2,1)S(1)}, bf16[3,8,192,128]{3,2,1,0:T(8,128)(2,1)}, u32[]{:S(2)}, u32[]{:S(2)}) collective-permute-start(bf16[3,8,192,128]{3,2,1,0:T(8,128)(2,1)S(1)} %dynamic-slice_bitcast_fusion.3), channel_id=1, source_target_pairs={{0,4},{4,0},{1,5},{5,1},{2,6},{6,2},{3,7},{7,3},{8,12},{12,8},{9,1... | collective-permute-start | bytes 3538952 | tf_op jit(solution)/shard_map/ppermute | solution.py:770
  (38 other events, 509.1 us)
Sparse Core Ops, SparseCore 0:
  11.1 60.2 all-gather.4
  73.6 39.6 all-gather.6
  114.8 28.4 all-gather.10
  176.1 27.2 all-gather.8
  246.4 161.1 reduce-scatter.11
  596.3 20.5 reduce-scatter.9
  619.2 83.8 reduce-scatter.13
  705.3 111.2 reduce-scatter.15
  818.9 92.6 reduce-scatter.17
  913.7 85.7 reduce-scatter.19
  1001.8 27.7 reduce-scatter.7

commit v4 on v3

--- a/solution.py
+++ b/solution.py
@@ -16,7 +16,7 @@
 FUSED_WIDTH = KEY_VALUE_HEADS * FUSED_GROUP
 LANES = 128
 ROW_BLOCK = 512
-CHUNKS = (8, 8, 8, 8, 8)
+CHUNKS = (8, 8, 8, 4, 8, 4)
 CTX = ("z", "y")
 SHARD = ("x", "k")
 EVERY = ("z", "y", "x", "k")
@@ -770,14 +770,18 @@
             picked(values, which), lax.ppermute(picked(values, 1 - which), axis_name, swap)
         )
 
-    def reduced_rows(terms):
-        columns = terms.shape[1]
-        parts = terms.reshape(ctx_parts, 2, 2, 2, -1, columns)
-        for axis_name, which, dim in (("k", core_pos, 3), ("x", chip_pos, 2), ("y", ctx_side, 1)):
+    def chip_reduced(terms):
+        parts = terms.reshape(ctx_parts, 2, 2, 2, -1, terms.shape[1])
+        for axis_name, which, dim in (("k", core_pos, 3), ("x", chip_pos, 2)):
             parts = halved_by(jnp.moveaxis(parts, dim, 0), axis_name, which)
-        return lax.psum_scatter(
-            parts.reshape(-1, columns), "z", scatter_dimension=0, tiled=True
-        ).astype(jnp.float32)
+        return parts
+
+    def side_reduced(parts):
+        parts = halved_by(jnp.moveaxis(parts, 1, 0), "y", ctx_side)
+        own = lax.psum_scatter(
+            parts.reshape(-1, parts.shape[-1]), "z", scatter_dimension=0, tiled=True
+        )
+        return own.astype(jnp.float32)
 
     fused_weight = lax.all_gather(
         jnp.concatenate(
@@ -872,20 +876,23 @@
         ],
         0,
     )
-    for axis_name, count in (("y", 2), ("z", ctx_parts)):
-        step = 1
-        while step < count:
-            group_sums = group_sums + lax.ppermute(
-                group_sums, axis_name, [(i, i ^ step) for i in range(count)]
-            )
-            step *= 2
-    all_sums = group_sums[:, :experts]
+    sum_steps = [("y", 1)]
+    while 2 ** (len(sum_steps) - 1) < ctx_parts:
+        sum_steps.append(("z", 2 ** (len(sum_steps) - 1)))
+
+    def summed_once(values, axis_name, step):
+        count = lax.axis_size(axis_name)
+        return values + lax.ppermute(values, axis_name, [(i, i ^ step) for i in range(count)])
+
 
     side = ctx_side.astype(jnp.int32).reshape(1)
     core = core_pos.astype(jnp.int32).reshape(1)
     acts, d_gates, reduced = None, None, []
     first_expert = 0
     for number, chunk in enumerate(CHUNKS):
+        if 0 < number <= len(sum_steps):
+            group_sums = summed_once(group_sums, *sum_steps[number - 1])
+            acts, group_sums = lax.optimization_barrier((acts, group_sums))
         *terms, acts, gate_piece = expert_chunk(
             first_expert,
             chunk,
@@ -915,6 +922,10 @@
         else:
             ringed = lax.psum_scatter(terms[0], "z", scatter_dimension=2, tiled=True)
 
+    for sum_step in sum_steps[len(CHUNKS) - 1 :]:
+        group_sums = summed_once(group_sums, *sum_step)
+    all_sums = group_sums[:, :experts]
+
     acts, first_halved = lax.optimization_barrier((acts, first_halved))
     d_stay, d_leave = expert_rows(core, (1, 2), (w_gate, w_up), acts, d_gates, hot_table)
     d_came = lax.ppermute(d_leave, "k", swap)
@@ -953,6 +964,7 @@
         (d_branch, d_attended, second_halved)
     )
     early_terms = early_grads(attended_low, d_branch, second_normed, d_logits, d_gain_two, experts)
+    early_parts = chip_reduced(early_terms)
     d_fused_rows = attend_back(
         fused_rows,
         d_attended,
@@ -962,11 +974,14 @@
         pair_sin,
         lengths_here,
     )
-    d_fused = exchange(d_fused_rows).reshape(KEY_VALUE_HEADS, tokens, FUSED_GROUP)
+    d_fused = exchange(d_fused_rows)
+    d_fused = d_fused.reshape(KEY_VALUE_HEADS, tokens, FUSED_GROUP)
     late_terms, grad_input = project_back(
         d_fused, fused_weight, first_normed, rows_in, gain_one, d_residual
     )
-    early_rows, late_rows = reduced_rows(early_terms), reduced_rows(late_terms)
+    early_parts, late_terms = lax.optimization_barrier((early_parts, late_terms))
+    early_rows = side_reduced(early_parts)
+    late_rows = side_reduced(chip_reduced(late_terms))
     query_end = KEY_VALUE_HEADS * QUERY_GROUP
     key_end = query_end + KEY_VALUE_HEADS * HEAD_DIM
     grads = [

time: 1050 us -> 1060 us (level)
  blocking collectives: 139 us -> 43 us
  waiting for transfers between devices: 416 us -> 504 us
    all_to_all x2 -> x1, blocking collectives: 139 us -> 43 us  [exchange(): return lax.all_to_all(groups, CTX, 0, 0, tiled=True)]
    ppermute x4 -> x5, waiting for transfers between devices: 107 us -> 188 us  [body(): arrived = lax.ppermute(terms[1], 'y', swap)]
    ppermute x7, waiting for transfers between devices: 99.9 us -> 50.2 us  [halved_by(): lax.ppermute(picked(values, 1 - which), axis_name, swap)]
    reduce_scatter x4 -> x5, waiting for transfers between devices: 29.9 us -> 70.2 us  [body(): lax.psum_scatter(halved, 'z', scatter_dimension=2, tiled=True)]
    ppermute x3, waiting for transfers between devices: 42.2 us -> 5.64 us  [summed_once(): lax.ppermute(values, axis_name, [(i, i ^ step) for i in range(count)])]
    all_to_all x2 -> x3, waiting for transfers between devices: 39.1 us -> 74.5 us  [exchange(): return lax.all_to_all(groups, CTX, 0, 0, tiled=True)]
    ppermute x2, waiting for transfers between devices: 0.01 us -> 17 us  [chip_halves(): lax.ppermute(leave_now, 'x', swap)]
    pallas_call x5 -> x6, Pallas kernels: 157 us -> 165 us  [expert_chunk(): pl.pallas_call(kernel, grid_spec=pltpu.PrefetchScalarGridSpec(num_scalar_...]
  transfers between devices with their start and end apart: 31 -> 34, of which waited for: 18 -> 20; matrix products, arithmetic and copies ran while one was open for 11% -> 11% of each run, Pallas kernels for 26% -> 27%
where the time goes in v4:
time: 1060 us; the launch traced here: 1050 us
  waiting for transfers between devices  504 us (48%)
  Pallas kernels  312 us (29%)
  other arithmetic  75.5 us (7%)
  local copies, waits for them, and re-layouts  62.2 us (6%)
  blocking collectives  43 us (4%)
  starting transfers between devices  34.1 us (3%)
  between operations  17.5 us (2%)
    ppermute x5, waiting for transfers between devices, body(): arrived = lax.ppermute(terms[1], 'y', swap)  188 us
    pallas_call x6, Pallas kernels, expert_chunk(): pl.pallas_call(kernel, grid_spec=pltpu.PrefetchScalarGridSpec(num_scalar_...  165 us
    all_to_all x3, waiting for transfers between devices, exchange(): return lax.all_to_all(groups, CTX, 0, 0, tiled=True)  74.5 us
    pallas_call x2, Pallas kernels, expert_rows(): pl.pallas_call(kernel, grid_spec=pltpu.PrefetchScalarGridSpec(num_scalar_...  73.7 us
    reduce_scatter x5, waiting for transfers between devices, body(): lax.psum_scatter(halved, 'z', scatter_dimension=2, tiled=True)  70.2 us
    all_gather x1, waiting for transfers between devices, body(): lax.all_gather(jnp.concatenate([w_query, key_projection_weight, value_pro...  52.3 us
    ppermute x7, waiting for transfers between devices, halved_by(): lax.ppermute(picked(values, 1 - which), axis_name, swap)  50.2 us
    convert_element_type x14, other arithmetic, added(): (first.astype(jnp.float32) + second.astype(jnp.float32)).astype(jnp.bfloa...  46.8 us
  transfers between devices with their start and end apart: 34, of which 20 were waited for; matrix products, arithmetic and copies ran while one was open for 11% of the time, Pallas kernels for 27%

profile of v4, /device:TPU:0, one launch (start us, length us, event | category | flops | bytes accessed | tf_op | source)
XLA Modules:
  0.0 1051.2 jit_solution(11113349816262400006)
XLA Ops:
  19.2 52.3 %all-gather.5.cloned.1.call-done.query_w.key_w.value_w = bf16[1536,2688]{1,0:T(8,128)(2,1)} async-done(((bf16[384,2688]{1,0:T(8,128)(2,1)}), bf16[1536,2688]{1,0:T(8,128)(2,1)}) %all-gather.5.cloned.1.call-update) | async-done | bytes 8257552 | tf_op jit(solution)/shard_map/all_gather | solution.py:786
  81.1 43.0 %all_to_all.20.query_ref.key_ref = bf16[8,4,64,320]{3,2,1,0:T(8,128)(2,1)} all-to-all(bf16[8,4,64,320]{3,2,1,0:T(8,128)(2,1)} %bitcast.175), channel_id=1, replica_groups=mesh['z'=4,'y'=2,'x'=2,'k'=2] {'z','y'}, dimensions={0} | all-to-all | bytes 2621440 | tf_op jit(solution)/shard_map/all_to_all | solution.py:849
  143.0 23.8 %all-to-all-done.1 = bf16[8,4,64,192]{3,2,1,0:T(8,128)(2,1)S(1)} async-done(((bf16[8,4,64,192]{3,2,1,0:T(8,128)(2,1)}), bf16[8,4,64,192]{3,2,1,0:T(8,128)(2,1)S(1)}, u32[]{:S(2)}, u32[]{:S(2)}) %all-to-all-start.1) | async-done | bytes 786464 | tf_op jit(solution)/shard_map/all_to_all | solution.py:849
  182.2 21.1 %all-gather.9.cloned.1.call-done = bf16[1024,1536]{0,1:T(8,128)(2,1)} async-done(((bf16[256,1536]{0,1:T(8,128)(2,1)}), bf16[1024,1536]{0,1:T(8,128)(2,1)}) %all-gather.9.cloned.1.call-update) | async-done | bytes 3145744 | tf_op jit(solution)/shard_map/all_gather | solution.py:861
  214.5 31.1 %expert_chunk.6 = (bf16[3,8,1536,128]{3,2,1,0:T(8,128)(2,1)}, bf16[3,20,1024,256]{3,2,1,0:T(8,128)(2,1)}, f32[1024,128]{1,0:T(8,128)}) custom-call(s32[1]{0:T(128)} %bitcast.4.side_ref, bf16[1024,1536]{1,0:T(8,128)(2,1)} %copy.150.normed, bf16[1536,1024]{1,0:T(8,128)(2,1)} %bitcast.156, bf16[1024,1536]{1,0:T(8,128)(2,1)} %all-gather.11.cloned.1.call-done.cotan, ...), custom_call_target="tpu_custom_call" | custom-call | tf_op jit(solution)/shard_map/expert_chunk/pallas_call | solution.py:436
  249.2 32.0 %expert_chunk.7 = (bf16[3,8,768,128]{3,2,1,0:T(8,128)(2,1)}, bf16[3,8,768,128]{3,2,1,0:T(8,128)(2,1)}, bf16[3,20,1024,256]{3,2,1,0:T(8,128)(2,1)}, f32[1024,128]{1,0:T(8,128)}) custom-call(s32[1]{0:T(128)} %bitcast.4.side_ref, bf16[1024,1536]{1,0:T(8,128)(2,1)} %copy.150.normed, bf16[1536,1024]{1,0:T(8,128)(2,1)} %bitcast.157, ...), custom_call_target="tpu_custom_call", output_to_operand_aliasing={{2}: (9, {})} | custom-call | tf_op jit(solution)/shard_map/expert_chunk/pallas_call | solution.py:436
  286.5 31.4 %expert_chunk.8 = (bf16[3,8,768,128]{3,2,1,0:T(8,128)(2,1)}, bf16[3,8,768,128]{3,2,1,0:T(8,128)(2,1)}, bf16[3,20,1024,256]{3,2,1,0:T(8,128)(2,1)}, f32[1024,128]{1,0:T(8,128)}) custom-call(s32[1]{0:T(128)} %bitcast.4.side_ref, bf16[1024,1536]{1,0:T(8,128)(2,1)} %copy.150.normed, bf16[1536,1024]{1,0:T(8,128)(2,1)} %bitcast.158, ...), custom_call_target="tpu_custom_call", output_to_operand_aliasing={{2}: (9, {})} | custom-call | tf_op jit(solution)/shard_map/expert_chunk/pallas_call | solution.py:436
  323.1 19.7 %expert_chunk.9 = (bf16[3,4,768,128]{3,2,1,0:T(8,128)(2,1)}, bf16[3,4,768,128]{3,2,1,0:T(8,128)(2,1)}, bf16[3,20,1024,256]{3,2,1,0:T(8,128)(2,1)}, f32[1024,128]{1,0:T(8,128)}) custom-call(s32[1]{0:T(128)} %bitcast.4.side_ref, bf16[1024,1536]{1,0:T(8,128)(2,1)} %copy.150.normed, bf16[1536,1024]{1,0:T(8,128)(2,1)} %bitcast.159, ...), custom_call_target="tpu_custom_call", output_to_operand_aliasing={{2}: (9, {})} | custom-call | tf_op jit(solution)/shard_map/expert_chunk/pallas_call | solution.py:436
  342.9 31.3 %expert_chunk.10 = (bf16[3,8,768,128]{3,2,1,0:T(8,128)(2,1)}, bf16[3,8,768,128]{3,2,1,0:T(8,128)(2,1)}, bf16[3,20,1024,256]{3,2,1,0:T(8,128)(2,1)}, f32[1024,128]{1,0:T(8,128)}) custom-call(s32[1]{0:T(128)} %bitcast.4.side_ref, bf16[1024,1536]{1,0:T(8,128)(2,1)} %copy.150.normed, bf16[1536,1024]{1,0:T(8,128)(2,1)} %bitcast.160, ...), custom_call_target="tpu_custom_call", output_to_operand_aliasing={{2}: (9, {})} | custom-call | tf_op jit(solution)/shard_map/expert_chunk/pallas_call | solution.py:436
  374.2 19.8 %expert_chunk.11 = (bf16[3,4,768,128]{3,2,1,0:T(8,128)(2,1)}, bf16[3,4,768,128]{3,2,1,0:T(8,128)(2,1)}, bf16[3,20,1024,256]{3,2,1,0:T(8,128)(2,1)}, f32[1024,128]{1,0:T(8,128)}) custom-call(s32[1]{0:T(128)} %bitcast.4.side_ref, bf16[1024,1536]{1,0:T(8,128)(2,1)} %copy.150.normed, bf16[1536,1024]{1,0:T(8,128)(2,1)} %bitcast.161, ...), custom_call_target="tpu_custom_call", output_to_operand_aliasing={{2}: (9, {})} | custom-call | tf_op jit(solution)/shard_map/expert_chunk/pallas_call | solution.py:436
  403.7 46.2 %expert_rows.3 = (bf16[2,256,1664]{2,1,0:T(8,128)(2,1)}, bf16[2,256,1664]{2,1,0:T(8,128)(2,1)}) custom-call(s32[1]{0:T(128)} %bitcast.3.core_ref, bf16[3,20,1024,256]{3,2,1,0:T(8,128)(2,1)} %get-tuple-element.79.refs_0_.refs_1_, bf16[3,20,1024,256]{3,2,1,0:T(8,128)(2,1)} %get-tuple-element.79.refs_0_.refs_1_, bf16[40,1536,128]{2,1,0:T(8,128)(2,1)} %refs_2_.1, ...), custom_call_target="tpu_custom_call" | custom-call | tf_op jit(solution)/shard_map/expert_rows/pallas_call | solution.py:529
  460.5 17.0 %collective-permute-done.7.arrived_ref = bf16[256,1664]{1,0:T(8,128)(2,1)S(1)} collective-permute-done((bf16[256,1664]{1,0:T(8,128)(2,1)S(1)}, bf16[256,1664]{1,0:T(8,128)(2,1)S(1)}, u32[]{:S(2)}, u32[]{:S(2)}) %collective-permute-start.7) | collective-permute-done | bytes 852000 | tf_op jit(solution)/shard_map/ppermute | solution.py:765
  499.0 17.9 %all-to-all-done.2.d_ref = bf16[8,4,64,192]{3,2,1,0:T(8,128)(2,1)S(1)} async-done(((bf16[8,4,64,192]{3,2,1,0:T(8,128)(2,1)}), bf16[8,4,64,192]{3,2,1,0:T(8,128)(2,1)S(1)}, u32[]{:S(2)}, u32[]{:S(2)}) %all-to-all-start.2) | async-done | bytes 786464 | tf_op jit(solution)/shard_map/all_to_all | solution.py:849
  529.4 18.7 %attend_back.1 = bf16[8,4,64,320]{3,2,1,0:T(8,128)(2,1)} custom-call(s32[4]{0:T(128)} %copy-done.29, bf16[8,4,64,320]{3,2,1,0:T(8,128)(2,1)} %all_to_all.20.query_ref.key_ref, bf16[8,4,64,320]{3,2,1,0:T(8,128)(2,1)} %all_to_all.20.query_ref.key_ref, bf16[8,4,64,192]{3,2,1,0:T(8,128)(2,1)} %copy-done.9, s32[512,128]{1,0:T(8,128)} %broadcast_in_dim.33.row_ref, ...), custom_call_target="tpu_custom_call" | custom-call | tf_op jit(solution)/shard_map/attend_back/pallas_call | solution.py:247
  557.6 32.8 %all-to-all-done.3 = bf16[8,4,64,320]{3,2,1,0:T(8,128)(2,1)} async-done(((bf16[8,4,64,320]{3,2,1,0:T(8,128)(2,1)}), bf16[8,4,64,320]{3,2,1,0:T(8,128)(2,1)}, u32[]{:S(2)}, u32[]{:S(2)}) %all-to-all-start.3) | async-done | bytes 1310752 | tf_op jit(solution)/shard_map/all_to_all | solution.py:849
  590.4 15.0 %project_back.1 = (bf16[1536,2688]{1,0:T(8,128)(2,1)}, f32[256,1536]{1,0:T(8,128)}) custom-call(bf16[8,256,320]{2,1,0:T(8,128)(2,1)} %bitcast.19.d_ref, bf16[1536,2688]{1,0:T(8,128)(2,1)} %all-gather.5.cloned.1.call-done.query_w.key_w.value_w, bf16[1536,2688]{1,0:T(8,128)(2,1)} %all-gather.5.cloned.1.call-done.query_w.key_w.value_w, ...), custom_call_target="tpu_custom_call" | custom-call | tf_op jit(solution)/shard_map/project_back/pallas_call | solution.py:692
  627.8 52.3 %collective-permute-done.16 = bf16[3,4,768,128]{3,2,1,0:T(8,128)(2,1)S(1)} collective-permute-done((bf16[3,4,768,128]{3,2,1,0:T(8,128)(2,1)}, bf16[3,4,768,128]{3,2,1,0:T(8,128)(2,1)S(1)}, u32[]{:S(2)}, u32[]{:S(2)}) %collective-permute-start.16) | collective-permute-done | bytes 2359328 | tf_op jit(solution)/shard_map/ppermute | solution.py:915
  682.3 96.9 %collective-permute-done.17 = bf16[3,8,768,128]{3,2,1,0:T(8,128)(2,1)} collective-permute-done((bf16[3,8,768,128]{3,2,1,0:T(8,128)(2,1)}, bf16[3,8,768,128]{3,2,1,0:T(8,128)(2,1)}, u32[]{:S(2)}, u32[]{:S(2)}) %collective-permute-start.17) | collective-permute-done | bytes 4718624 | tf_op jit(solution)/shard_map/ppermute | solution.py:915
  804.0 39.3 %collective-permute-done.18 = bf16[3,4,768,128]{3,2,1,0:T(8,128)(2,1)S(1)} collective-permute-done((bf16[3,4,768,128]{3,2,1,0:T(8,128)(2,1)S(1)}, bf16[3,4,768,128]{3,2,1,0:T(8,128)(2,1)S(1)}, u32[]{:S(2)}, u32[]{:S(2)}) %collective-permute-start.18) | collective-permute-done | bytes 2359328 | tf_op jit(solution)/shard_map/ppermute | solution.py:915
  845.4 27.5 %expert_rows.2 = (bf16[2,256,1536]{2,1,0:T(8,128)(2,1)}, bf16[2,256,1536]{2,1,0:T(8,128)(2,1)}) custom-call(s32[1]{0:T(128)} %bitcast.3.core_ref, bf16[3,20,1024,256]{3,2,1,0:T(8,128)(2,1)} %get-tuple-element.79.refs_0_.refs_1_, bf16[40,1536,128]{2,1,0:T(8,128)(2,1)} %refs_1_.1), custom_call_target="tpu_custom_call" | custom-call | tf_op jit(solution)/shard_map/expert_rows/pallas_call | solution.py:529
  885.8 17.6 %collective-permute-done.13 = bf16[4,48,2688]{2,1,0:T(8,128)(2,1)} collective-permute-done((bf16[4,48,2688]{2,1,0:T(8,128)(2,1)}, bf16[4,48,2688]{2,1,0:T(8,128)(2,1)}, u32[]{:S(2)}, u32[]{:S(2)}) %collective-permute-start.13) | collective-permute-done | bytes 1032224 | tf_op jit(solution)/shard_map/ppermute | solution.py:770
  937.1 21.2 %reduce-scatter.21.cloned.1.call-done = bf16[3,8,192,128]{3,2,1,0:T(8,128)(2,1)} async-done(((bf16[3,8,768,128]{3,2,1,0:T(8,128)(2,1)}), bf16[3,8,192,128]{3,2,1,0:T(8,128)(2,1)}) %reduce-scatter.21.cloned.1.call-update) | async-done | bytes 1179664 | tf_op jit(solution)/shard_map/reduce_scatter | solution.py:921
  960.5 48.9 %reduce-scatter.23.cloned.1.call-done = bf16[3,4,192,128]{3,2,1,0:T(8,128)(2,1)} async-done(((bf16[3,4,768,128]{3,2,1,0:T(8,128)(2,1)}), bf16[3,4,192,128]{3,2,1,0:T(8,128)(2,1)}) %reduce-scatter.23.cloned.1.call-update) | async-done | bytes 589840 | tf_op jit(solution)/shard_map/reduce_scatter | solution.py:921
  1018.5 19.7 %reduce-scatter.9.cloned.1.call-done = bf16[48,2688]{1,0:T(8,128)(2,1)} async-done(((bf16[192,2688]{1,0:T(8,128)(2,1)}), bf16[48,2688]{1,0:T(8,128)(2,1)}) %reduce-scatter.9.cloned.1.call-update) | async-done | bytes 258064 | tf_op jit(solution)/shard_map/reduce_scatter | solution.py:781
  (245 shorter events, 257.0 us)
Async XLA Ops:
  7.2 64.3 %all-gather.5.cloned.1.call-start = ((), (), s32[]{:S(2)}) async-start(), calls=%async_computation.12 | async-start | bytes 10321920 | tf_op jit(solution)/shard_map/all_gather | solution.py:786
  11.0 130.0 %all-gather.7.cloned.1.call-start = ((), (), s32[]{:S(2)}) async-start(), calls=%async_computation.13 | async-start | bytes 6389760 | tf_op jit(solution)/shard_map/all_gather | solution.py:800
  14.1 163.3 %all-gather.11.cloned.1.call-start = ((), (), s32[]{:S(2)}) async-start(), calls=%async_computation.15 | async-start | bytes 3932160 | tf_op jit(solution)/shard_map/all_gather | solution.py:845
  137.3 29.5 %all-to-all-start.1 = ((bf16[8,4,64,192]{3,2,1,0:T(8,128)(2,1)}), bf16[8,4,64,192]{3,2,1,0:T(8,128)(2,1)S(1)}, u32[]{:S(2)}, u32[]{:S(2)}) async-start(bf16[8,4,64,192]{3,2,1,0:T(8,128)(2,1)} %attend.1), calls=%async_computation.1 | async-start | bytes 2097152 | tf_op jit(solution)/shard_map/all_to_all | solution.py:849
  140.9 62.3 %all-gather.9.cloned.1.call-start = ((), (), s32[]{:S(2)}) async-start(), calls=%async_computation.14 | async-start | bytes 3932160 | tf_op jit(solution)/shard_map/all_gather | solution.py:861
  176.1 707.6 %reduce-scatter.13.cloned.1.call-start = ((), (), s32[]{:S(2)}) async-start(), calls=%async_computation.18 | async-start | bytes 11796480 | tf_op jit(solution)/shard_map/reduce_scatter | solution.py:923
  281.3 114.8 %collective-permute-start.3 = (bf16[3,8,768,128]{3,2,1,0:T(8,128)(2,1)}, bf16[3,8,768,128]{3,2,1,0:T(8,128)(2,1)}, u32[]{:S(2)}, u32[]{:S(2)}) collective-permute-start(bf16[3,8,768,128]{3,2,1,0:T(8,128)(2,1)} %get-tuple-element.78), channel_id=1, source_target_pairs={{0,4},{4,0},{1,5},{5,1},{2,6},{6,2},{3,7},{7,3},{8,12},{12,8},{9,1... | collective-permute-start | bytes 14155784 | tf_op jit(solution)/shard_map/ppermute | solution.py:915
  318.0 173.4 %collective-permute-start.8 = (bf16[3,8,768,128]{3,2,1,0:T(8,128)(2,1)}, bf16[3,8,768,128]{3,2,1,0:T(8,128)(2,1)}, u32[]{:S(2)}, u32[]{:S(2)}) collective-permute-start(bf16[3,8,768,128]{3,2,1,0:T(8,128)(2,1)} %get-tuple-element.94), channel_id=1, source_target_pairs={{0,4},{4,0},{1,5},{5,1},{2,6},{6,2},{3,7},{7,3},{8,12},{12,8},{9,1... | collective-permute-start | bytes 14155784 | tf_op jit(solution)/shard_map/ppermute | solution.py:915
  485.9 31.0 %all-to-all-start.2 = ((bf16[8,4,64,192]{3,2,1,0:T(8,128)(2,1)}), bf16[8,4,64,192]{3,2,1,0:T(8,128)(2,1)S(1)}, u32[]{:S(2)}, u32[]{:S(2)}) async-start(bf16[8,4,64,192]{3,2,1,0:T(8,128)(2,1)} %bitcast.176), calls=%async_computation.2 | async-start | bytes 2097152 | tf_op jit(solution)/shard_map/all_to_all | solution.py:849
  548.2 42.2 %all-to-all-start.3 = ((bf16[8,4,64,320]{3,2,1,0:T(8,128)(2,1)}), bf16[8,4,64,320]{3,2,1,0:T(8,128)(2,1)}, u32[]{:S(2)}, u32[]{:S(2)}) async-start(bf16[8,4,64,320]{3,2,1,0:T(8,128)(2,1)} %attend_back.1), calls=%async_computation.3 | async-start | bytes 3145728 | tf_op jit(solution)/shard_map/all_to_all | solution.py:849
  552.5 356.9 %reduce-scatter.11.cloned.1.call-start = ((), (), s32[]{:S(2)}) async-start(), calls=%async_computation.17 | async-start | bytes 798720 | tf_op jit(solution)/shard_map/reduce_scatter | solution.py:781
  556.4 49.0 %collective-permute-start.10 = (bf16[4,2,48,1664]{3,2,0,1:T(8,128)(2,1)S(1)}, bf16[4,2,48,1664]{3,2,0,1:T(8,128)(2,1)}, u32[]{:S(2)}, u32[]{:S(2)}) collective-permute-start(bf16[4,2,48,1664]{3,2,0,1:T(8,128)(2,1)S(1)} %dynamic-slice_bitcast_fusion.2), channel_id=1, source_target_pairs={{0,2},{2,0},{1,3},{3,1},{4,6},{6,4},{5,7},{7,5},{8,10},{10,8},{9,1... | collective-permute-start | bytes 3833864 | tf_op jit(solution)/shard_map/ppermute | solution.py:770
  624.2 306.6 %reduce-scatter.15.cloned.1.call-start = ((), (), s32[]{:S(2)}) async-start(), calls=%async_computation.19 | async-start | bytes 5898240 | tf_op jit(solution)/shard_map/reduce_scatter | solution.py:921
  624.9 308.0 %reduce-scatter.17.cloned.1.call-start = ((), (), s32[]{:S(2)}) async-start(), calls=%async_computation.20 | async-start | bytes 5898240 | tf_op jit(solution)/shard_map/reduce_scatter | solution.py:921
  625.7 309.5 %reduce-scatter.19.cloned.1.call-start = ((), (), s32[]{:S(2)}) async-start(), calls=%async_computation.21 | async-start | bytes 2949120 | tf_op jit(solution)/shard_map/reduce_scatter | solution.py:921
  625.7 54.4 %collective-permute-start.16 = (bf16[3,4,768,128]{3,2,1,0:T(8,128)(2,1)}, bf16[3,4,768,128]{3,2,1,0:T(8,128)(2,1)S(1)}, u32[]{:S(2)}, u32[]{:S(2)}) collective-permute-start(bf16[3,4,768,128]{3,2,1,0:T(8,128)(2,1)} %get-tuple-element.108), channel_id=1, source_target_pairs={{0,4},{4,0},{1,5},{5,1},{2,6},{6,2},{3,7},{7,3},{8,12},{12,8},{9,1... | collective-permute-start | bytes 7077896 | tf_op jit(solution)/shard_map/ppermute | solution.py:915
  627.3 151.9 %collective-permute-start.17 = (bf16[3,8,768,128]{3,2,1,0:T(8,128)(2,1)}, bf16[3,8,768,128]{3,2,1,0:T(8,128)(2,1)}, u32[]{:S(2)}, u32[]{:S(2)}) collective-permute-start(bf16[3,8,768,128]{3,2,1,0:T(8,128)(2,1)} %get-tuple-element.110), channel_id=1, source_target_pairs={{0,4},{4,0},{1,5},{5,1},{2,6},{6,2},{3,7},{7,3},{8,12},{12,8},{9,1... | collective-permute-start | bytes 14155784 | tf_op jit(solution)/shard_map/ppermute | solution.py:915
  682.2 276.1 %reduce-scatter.21.cloned.1.call-start = ((), (), s32[]{:S(2)}) async-start(), calls=%async_computation.22 | async-start | bytes 5898240 | tf_op jit(solution)/shard_map/reduce_scatter | solution.py:921
  786.9 222.5 %reduce-scatter.23.cloned.1.call-start = ((), (), s32[]{:S(2)}) async-start(), calls=%async_computation.23 | async-start | bytes 2949120 | tf_op jit(solution)/shard_map/reduce_scatter | solution.py:921
  789.8 53.5 %collective-permute-start.18 = (bf16[3,4,768,128]{3,2,1,0:T(8,128)(2,1)S(1)}, bf16[3,4,768,128]{3,2,1,0:T(8,128)(2,1)S(1)}, u32[]{:S(2)}, u32[]{:S(2)}) collective-permute-start(bf16[3,4,768,128]{3,2,1,0:T(8,128)(2,1)S(1)} %copy-done.35), channel_id=1, source_target_pairs={{0,4},{4,0},{1,5},{5,1},{2,6},{6,2},{3,7},{7,3},{8,12},{12,8},{9,1... | collective-permute-start | bytes 7077896 | tf_op jit(solution)/shard_map/ppermute | solution.py:915
  802.9 70.0 %collective-permute-start.12 = (bf16[4,2,48,2688]{3,2,1,0:T(8,128)(2,1)}, bf16[4,2,48,2688]{3,2,1,0:T(8,128)(2,1)}, u32[]{:S(2)}, u32[]{:S(2)}) collective-permute-start(bf16[4,2,48,2688]{3,2,1,0:T(8,128)(2,1)} %dynamic-slice_bitcast_fusion.1), channel_id=1, source_target_pairs={{0,2},{2,0},{1,3},{3,1},{4,6},{6,4},{5,7},{7,5},{8,10},{10,8},{9,1... | collective-permute-start | bytes 6193160 | tf_op jit(solution)/shard_map/ppermute | solution.py:770
  845.4 192.8 %reduce-scatter.9.cloned.1.call-start = ((), (), s32[]{:S(2)}) async-start(), calls=%async_computation.16 | async-start | bytes 1290240 | tf_op jit(solution)/shard_map/reduce_scatter | solution.py:781
  877.4 26.0 %collective-permute-start.13 = (bf16[4,48,2688]{2,1,0:T(8,128)(2,1)}, bf16[4,48,2688]{2,1,0:T(8,128)(2,1)}, u32[]{:S(2)}, u32[]{:S(2)}) collective-permute-start(bf16[4,48,2688]{2,1,0:T(8,128)(2,1)} %dynamic-slice_bitcast_fusion.4), channel_id=1, source_target_pairs={{0,4},{4,0},{1,5},{5,1},{2,6},{6,2},{3,7},{7,3},{8,12},{12,8},{9,1... | collective-permute-start | bytes 3096584 | tf_op jit(solution)/shard_map/ppermute | solution.py:770
  885.0 43.2 %collective-permute-start.15 = (bf16[3,8,192,128]{3,2,1,0:T(8,128)(2,1)S(1)}, bf16[3,8,192,128]{3,2,1,0:T(8,128)(2,1)}, u32[]{:S(2)}, u32[]{:S(2)}) collective-permute-start(bf16[3,8,192,128]{3,2,1,0:T(8,128)(2,1)S(1)} %dynamic-slice_bitcast_fusion.3), channel_id=1, source_target_pairs={{0,4},{4,0},{1,5},{5,1},{2,6},{6,2},{3,7},{7,3},{8,12},{12,8},{9,1... | collective-permute-start | bytes 3538952 | tf_op jit(solution)/shard_map/ppermute | solution.py:770
  (46 other events, 461.8 us)
Sparse Core Ops, SparseCore 0:
  11.1 60.2 all-gather.4
  73.6 39.6 all-gather.6
  115.4 28.4 all-gather.10
  176.2 27.0 all-gather.8
  245.7 161.2 reduce-scatter.12
  624.3 21.5 reduce-scatter.10
  648.2 83.9 reduce-scatter.14
  734.5 85.7 reduce-scatter.16
  823.2 48.1 reduce-scatter.18
  873.6 84.6 reduce-scatter.20
  961.2 48.1 reduce-scatter.22
  1011.6 26.5 reduce-scatter.8
